TPU v7x, 512 devices: a whole 4x4x16 slice. The times are simulated.
512 devices in a mesh: store: 32 (over z, core), tensor: 16 (over y, x).
Axes of the slice: x: 4, y: 4, z: 16, core: 2. Of those that a mesh axis runs over, the one named last changes fastest.
Arguments:
- tokens: bfloat16 [98304, 8192], P('store', 'tensor'), may hold values from -6 to 6
- base_weight: bfloat16 [8192, 512], P('tensor'), may hold values from -0.0625 to 0.0625
- adapter_down: bfloat16 [512, 64, 8192], P('store', None, 'tensor'), may hold values from -0.0625 to 0.0625
- adapter_up: bfloat16 [512, 64, 512], P('store', 'tensor'), may hold values from -0.75 to 0.75
- segment_blocks: int32 [32, 22], P('store'), may hold values from 1 to 2, 24 in all within a row
- segment_owner: int32 [704, 1], P('store'), may hold values from 0 to 31; in each aligned block of 22 rows (0 to 21, 22 to 43, ...) at most 2 rows name the same one
- segment_slot: int32 [704], P('store'), may hold values from 0 to 15
Outputs:
- projected: bfloat16 [98304, 512], P(('store', 'tensor'))
Inputs may be any that keep to these rules, and one draw needn't show every extreme that they name: `segment_blocks`: each row sums to 24, and some entry of every row equals 2. `segment_owner`: among the 22 segments of one store index no owner is named more than 2 times; in every draw some owner is named exactly 2 times by some store index's segments.
All inputs are finite; a program needn't handle non-finite values.
Results may differ from a plain program's by a relative error of at most 0.015.
Values may be sent and summed in bfloat16 or wider, within the bound.
No kernel may reach another device: no remote copies, remote signals or barrier semaphores. Data moves between devices by JAX's collectives and lax.ppermute only.
A program may use at most 64 MiB of HBM per device.

v0:
```python
import jax
import jax.numpy as jnp
from jax import lax
from jax.sharding import Mesh
from jax.sharding import PartitionSpec as P

BLOCK = 128
TENSOR = ("tensor_0", "tensor_1")
STORE_TENSOR = ("store", "tensor_0", "tensor_1")


def rows_first(arrays, axis, dims):
    turned = [jnp.moveaxis(a, dim, 0) for a, dim in zip(arrays, dims)]
    widths = [t[0].size for t in turned]
    both = jnp.concatenate([t.reshape(-1, w) for t, w in zip(turned, widths)], axis=1)
    filled = lax.all_gather(both, axis, axis=0, tiled=True)
    blocks = jnp.split(filled, [sum(widths[:k]) for k in range(1, len(widths))], axis=1)
    return tuple(
        (
            jnp.moveaxis(b.reshape(-1, *t.shape[1:]), 0, dim)
            for b, t, dim in zip(blocks, turned, dims)
        )
    )


def in_one_piece(arrays, axis, split_dim, concat_dim, along):
    both = jnp.concatenate(arrays, axis=along)
    filled, at, done = (
        lax.all_to_all(both, axis, split_axis=split_dim, concat_axis=concat_dim, tiled=True),
        0,
        [],
    )
    for a in arrays:
        done.append(lax.slice_in_dim(filled, at, at + a.shape[along], axis=along))
        at += a.shape[along]
    return tuple(done)


def cut_along(x, dim, count):
    before, after = (x.shape[:dim], x.shape[dim + 1 :])
    return jnp.moveaxis(x.reshape(*before, count, -1, *after), dim, 0)


def summed_on_arrival(x, axis, dim):
    blocks = cut_along(x, dim, lax.axis_size(axis))
    arrived = lax.all_to_all(blocks, axis, split_axis=0, concat_axis=0, tiled=True)
    return arrived.astype(jnp.float32).sum(axis=0)


def sent_to_all(x, axis):
    copies = jnp.broadcast_to(x, (lax.axis_size(axis), *x.shape))
    return lax.all_to_all(copies, axis, split_axis=0, concat_axis=0, tiled=True)


def laid_out(blocks, dim):
    shape = list(blocks.shape[1:])
    shape[dim] *= blocks.shape[0]
    return jnp.moveaxis(blocks, 0, dim).reshape(shape)


def collect(x, axis, dim):
    blocks = sent_to_all(x, axis)
    return laid_out(blocks, dim)


def summed_rows(terms, axes):
    running = terms.astype(jnp.bfloat16)
    for axis in axes:
        running = lax.psum_scatter(running, axis, scatter_dimension=0, tiled=True)
    return running.astype(jnp.float32)


def block_segments(lengths, block_count):
    seg_ends = jnp.cumsum(lengths, axis=-1)
    blocks = jnp.arange(block_count, dtype=jnp.int32)
    return jnp.sum(
        (seg_ends[..., None, :] <= blocks[:, None]).astype(jnp.int32), axis=-1, dtype=jnp.int32
    )


def pick_slots(unit_owner, unit_slot, my_store, capacity):
    held_here = (unit_owner == my_store).astype(jnp.int32)
    before = jnp.cumsum(held_here, axis=1) - held_here
    places = jnp.arange(capacity, dtype=jnp.int32)
    matches = held_here[:, None, :] * (before[:, None, :] == places[None, :, None]).astype(
        jnp.int32
    )
    return jnp.sum(matches * unit_slot[:, None, :], axis=2, dtype=jnp.int32).reshape(-1)


def place_units(unit_owner, capacity):
    unit_count = unit_owner.shape[0]
    same_owner = (unit_owner[:, None] == unit_owner[None, :]).astype(jnp.int32)
    unit_ids = jnp.arange(unit_count, dtype=jnp.int32)
    earlier = (unit_ids[None, :] < unit_ids[:, None]).astype(jnp.int32)
    return unit_owner * capacity + jnp.sum(same_owner * earlier, axis=1, dtype=jnp.int32)


def local(
    tokens, base_weight, adapter_down, adapter_up, segment_blocks, segment_owner, segment_slot
):
    tok_rows, local_feats = tokens.shape
    kv_width = base_weight.shape[1]
    rank_size = adapter_down.shape[1]
    rank_local = adapter_up.shape[1]
    stores = lax.axis_size("store")
    tensors = lax.axis_size(TENSOR)
    seg_count = segment_slot.shape[0]
    block_len = BLOCK
    block_count = tok_rows // block_len
    capacity = max(2, (seg_count + stores - 1) // stores)
    my_store = lax.axis_index("store")
    my_tensor = lax.axis_index(TENSOR)
    owners = segment_owner[:, 0]
    seg_of_block = block_segments(segment_blocks[0], block_count)
    all_owner, all_slot = rows_first((owners, segment_slot), "store", (0, 0))
    all_owner = all_owner.reshape(stores, seg_count)
    all_slot = all_slot.reshape(stores, seg_count)
    picked = pick_slots(all_owner, all_slot, my_store, capacity)
    send_down = jnp.take(adapter_down, picked, axis=0).reshape(
        stores, capacity, rank_size, local_feats
    )
    send_up = jnp.take(adapter_up, picked, axis=0).reshape(stores, capacity, rank_local, kv_width)
    got_down, got_up = in_one_piece((send_down, send_up), "store", 0, 0, 2)
    position = jnp.take(place_units(owners, capacity), seg_of_block, axis=0)
    down_blk = jnp.take(got_down.reshape(-1, rank_size, local_feats), position, axis=0)
    up_blk = jnp.take(got_up.reshape(-1, rank_local, kv_width), position, axis=0)
    token_blocks = tokens.reshape(block_count, block_len, local_feats)
    shrink_part = jnp.einsum(
        "btf,brf->btr", token_blocks, down_blk, preferred_element_type=jnp.float32
    )
    shrink_part = shrink_part.reshape(tok_rows, rank_size)
    rows_each = tok_rows // tensors
    first_row = my_tensor * rows_each
    shrink_mine = summed_on_arrival(shrink_part.astype(jnp.bfloat16), TENSOR, 0)
    shrink_mine = shrink_mine.astype(jnp.bfloat16)
    up_full = collect(up_blk, TENSOR, 1)
    row_block = (first_row + jnp.arange(rows_each, dtype=jnp.int32)) // block_len
    start_block = first_row // block_len
    block_span = (rows_each - 1) // block_len + 2
    adapter_term = jnp.zeros((rows_each, kv_width), jnp.float32)
    for offset in range(block_span):
        block_here = jnp.minimum(start_block + offset, block_count - 1)
        up_here = lax.dynamic_index_in_dim(up_full, block_here, 0, keepdims=False)
        partial_value = jnp.dot(shrink_mine, up_here, preferred_element_type=jnp.float32)
        adapter_term = adapter_term + jnp.where(
            (row_block == start_block + offset)[:, None], partial_value, 0.0
        )
    base_mine = summed_rows(
        jnp.dot(tokens, base_weight, preferred_element_type=jnp.float32), TENSOR
    )
    return (base_mine + adapter_term).astype(jnp.bfloat16)


def solution(mesh):
    split = Mesh(mesh.devices.reshape(mesh.shape["store"], 4, 4), ("store", "tensor_0", "tensor_1"))
    placed = (
        P("store", TENSOR),
        P(TENSOR, None),
        P("store", None, TENSOR),
        P("store", TENSOR, None),
        P("store", None),
        P("store", None),
        P("store"),
    )
    return jax.shard_map(
        local, mesh=split, in_specs=placed, out_specs=P(STORE_TENSOR, None), check_vma=False
    )
```

profile of v0, /device:TPU:64, one launch (start us, length us, event | category | flops | bytes accessed | tf_op | source)
XLA Modules:
  0.0 355.8 jit_solution(4644185960063389142)
XLA Ops:
  7.4 33.4 %all-gather = s32[32,22,2]{1,2,0:T(2,128)S(1)} all-gather(s32[1,22,2]{1,2,0:T(2,128)S(1)} %add_bitcast_fusion), channel_id=1, replica_groups=mesh['store'=32,'tensor_0'=4,'tensor_1'=4] {'store'}, dimensions={0}, use_global_device_ids=true | all-gather | bytes 5808 | tf_op jit(solution)/shard_map/all_gather | solution.py:16
  42.0 4.0 %gather_fusion.1 = bf16[64,64,512]{2,1,0:T(8,128)(2,1)} fusion(bf16[16,64,512]{2,1,0:T(8,128)(2,1)} %param.9, s32[1024]{0:T(1024)S(1)} %pad_clamp_fusion.1), kind=kCustom, calls=%fused_computation.1 | custom fusion | bytes 8388864 | tf_op jit(solution)/shard_map/jit(_take)/gather | solution.py:120
  46.8 2.6 broadcast_select_fusion
  49.6 2.6 pad_maximum_fusion
  52.2 7.9 %copy.40 = bf16[32,2,68,512]{3,1,2,0:T(2,128)(2,1)} copy(bf16[32,2,68,512]{3,2,1,0:T(8,128)(2,1)} %pad_maximum_fusion) | data formatting | bytes 8912896 | tf_op jit(solution)/shard_map/concatenate | solution.py:27
  60.1 9.5 %all-to-all-start = ((bf16[32,2,68,512]{3,1,2,0:T(2,128)(2,1)}), bf16[32,2,68,512]{3,1,2,0:T(2,128)(2,1)}, u32[]{:S(2)}, u32[]{:S(2)}) async-start(bf16[32,2,68,512]{3,1,2,0:T(2,128)(2,1)} %copy.40), calls=%async_computation.2 | async-start | bytes 8912896 | tf_op jit(solution)/shard_map/all_to_all | solution.py:29
  69.9 4.5 %convolution_convert_fusion = bf16[3072,512]{1,0:T(8,128)(2,1)} fusion(bf16[3072,512]{1,0:T(8,128)(2,1)S(1)} %copy-done, bf16[512,512]{1,0:T(8,128)(2,1)} %param.8), kind=kOutput, calls=%fused_computation.6 | convolution fusion | flops 1612185600 | bytes 6815744 | tf_op jit(solution)/shard_map/dot_general | solution.py:150
  75.7 193.1 %all-to-all-done = bf16[32,2,68,512]{3,1,2,0:T(2,128)(2,1)} async-done(((bf16[32,2,68,512]{3,1,2,0:T(2,128)(2,1)}), bf16[32,2,68,512]{3,1,2,0:T(2,128)(2,1)}, u32[]{:S(2)}, u32[]{:S(2)}) %all-to-all-start) | async-done | bytes 4456480 | tf_op jit(solution)/shard_map/all_to_all | solution.py:29
  268.9 9.1 %slice.18 = bf16[32,2,64,512]{3,1,2,0:T(2,128)(2,1)} slice(bf16[32,2,68,512]{3,1,2,0:T(2,128)(2,1)} %all-to-all-done), slice={[0:32], [0:2], [0:64], [0:512]} | slice | bytes 8388608 | tf_op jit(solution)/shard_map/slice | solution.py:34
  278.0 5.2 %copy.51 = bf16[32,2,64,512]{3,2,1,0:T(8,128)(2,1)} copy(bf16[32,2,64,512]{3,1,2,0:T(2,128)(2,1)} %slice.18) | data formatting | bytes 8388608
  283.2 4.1 %gather_fusion.3 = bf16[24,64,512]{2,1,0:T(8,128)(2,1)} fusion(bf16[64,64,512]{2,1,0:T(8,128)(2,1)} %bitcast.53, s32[1024]{0:T(1024)S(1)} %pad_clamp_fusion), kind=kCustom, calls=%fused_computation.3 | custom fusion | bytes 3145824 | tf_op jit(solution)/shard_map/jit(_take)/gather | solution.py:126
  287.3 2.6 fusion.8
  290.2 1.2 convert_element_type.54
  291.3 2.0 copy.43
  293.3 7.1 %all-to-all-start.1 = ((bf16[16,192,64]{1,2,0:T(8,128)(2,1)}), bf16[16,192,64]{1,2,0:T(8,128)(2,1)}, u32[]{:S(2)}, u32[]{:S(2)}) async-start(bf16[16,192,64]{1,2,0:T(8,128)(2,1)} %copy.43), calls=%async_computation.3 | async-start | bytes 1048576 | tf_op jit(solution)/shard_map/all_to_all | solution.py:46
  300.4 1.1 slice.19
  302.5 8.8 %all-to-all-done.1 = bf16[16,192,64]{1,2,0:T(8,128)(2,1)} async-done(((bf16[16,192,64]{1,2,0:T(8,128)(2,1)}), bf16[16,192,64]{1,2,0:T(8,128)(2,1)}, u32[]{:S(2)}, u32[]{:S(2)}) %all-to-all-start.1) | async-done | bytes 393248 | tf_op jit(solution)/shard_map/all_to_all | solution.py:46
  311.3 1.3 broadcast_in_dim.88
  312.6 4.4 %all-to-all-start.2 = ((bf16[16,24,4,512]{3,1,2,0:T(8,128)(2,1)}), bf16[16,24,4,512]{3,1,2,0:T(8,128)(2,1)}, u32[]{:S(2)}, u32[]{:S(2)}) async-start(bf16[16,24,4,512]{3,1,2,0:T(8,128)(2,1)} %broadcast_in_dim.88), calls=%async_computation.4 | async-start | bytes 3145728 | tf_op jit(solution)/shard_map/all_to_all | solution.py:52
  317.8 1.1 reduce_sum.45
  319.0 22.1 %all-to-all-done.2 = bf16[16,24,4,512]{3,1,2,0:T(8,128)(2,1)} async-done(((bf16[16,24,4,512]{3,1,2,0:T(8,128)(2,1)}), bf16[16,24,4,512]{3,1,2,0:T(8,128)(2,1)}, u32[]{:S(2)}, u32[]{:S(2)}) %all-to-all-start.2) | async-done | bytes 1572896 | tf_op jit(solution)/shard_map/all_to_all | solution.py:52
  341.1 2.5 constant_dynamic-slice_fusion
  344.8 2.3 reduce-scatter.5.cloned.1.call-done
  347.1 1.9 fusion.12
  (56 shorter events, 7.6 us)
Async XLA Ops:
  6.5 63.3 %copy-start = (bf16[3072,512]{1,0:T(8,128)(2,1)S(1)}, bf16[3072,512]{1,0:T(8,128)(2,1)}, u32[]{:S(2)}) copy-start(bf16[3072,512]{1,0:T(8,128)(2,1)} %param.7) | copy-start | bytes 9437188
  42.0 4.0 %copy-start.1 = (bf16[16,4,512]{2,1,0:T(4,128)(2,1)S(1)}, bf16[16,4,512]{2,1,0:T(4,128)(2,1)}, u32[]{:S(2)}) copy-start(bf16[16,4,512]{2,1,0:T(4,128)(2,1)} %param.10) | copy-start | bytes 196612
  60.1 208.7 %all-to-all-start = ((bf16[32,2,68,512]{3,1,2,0:T(2,128)(2,1)}), bf16[32,2,68,512]{3,1,2,0:T(2,128)(2,1)}, u32[]{:S(2)}, u32[]{:S(2)}) async-start(bf16[32,2,68,512]{3,1,2,0:T(2,128)(2,1)} %copy.40), calls=%async_computation.2 | async-start | bytes 8912896 | tf_op jit(solution)/shard_map/all_to_all | solution.py:29
  69.6 4.8 %copy-start.3 = (s32[1,22]{1,0:T(1,128)S(1)}, s32[1,22]{1,0:T(1,128)}, u32[]{:S(2)}) copy-start(s32[1,22]{1,0:T(1,128)} %param.11) | copy-start | bytes 268
  69.6 5.2 %copy-start.4 = (s32[22,1]{0,1:T(1,128)S(1)}, s32[22,1]{0,1:T(1,128)}, u32[]{:S(2)}) copy-start(s32[22,1]{0,1:T(1,128)} %param.12) | copy-start | bytes 268
  69.6 247.4 %reduce-scatter.3.cloned.1.call-start = ((), (), s32[]{:S(2)}) async-start(), calls=%async_computation.5 | async-start | bytes 3932160 | tf_op jit(solution)/shard_map/reduce_scatter | solution.py:69
  293.3 17.9 %all-to-all-start.1 = ((bf16[16,192,64]{1,2,0:T(8,128)(2,1)}), bf16[16,192,64]{1,2,0:T(8,128)(2,1)}, u32[]{:S(2)}, u32[]{:S(2)}) async-start(bf16[16,192,64]{1,2,0:T(8,128)(2,1)} %copy.43), calls=%async_computation.3 | async-start | bytes 1048576 | tf_op jit(solution)/shard_map/all_to_all | solution.py:46
  312.6 28.5 %all-to-all-start.2 = ((bf16[16,24,4,512]{3,1,2,0:T(8,128)(2,1)}), bf16[16,24,4,512]{3,1,2,0:T(8,128)(2,1)}, u32[]{:S(2)}, u32[]{:S(2)}) async-start(bf16[16,24,4,512]{3,1,2,0:T(8,128)(2,1)} %broadcast_in_dim.88), calls=%async_computation.4 | async-start | bytes 3145728 | tf_op jit(solution)/shard_map/all_to_all | solution.py:52
  317.0 30.1 %reduce-scatter.5.cloned.1.call-start = ((), (), s32[]{:S(2)}) async-start(), calls=%async_computation.6 | async-start | bytes 983040 | tf_op jit(solution)/shard_map/reduce_scatter | solution.py:69
  319.0 24.9 %copy-start.2 = (bf16[192,64]{0,1:T(8,128)(2,1)}, bf16[192,64]{0,1:T(8,128)(2,1)S(1)}, u32[]{:S(2)}) copy-start(bf16[192,64]{0,1:T(8,128)(2,1)S(1)} %reduce_sum.45) | copy-start | bytes 73732
Sparse Core Ops, SparseCore 0:
  74.5 47.0 reduce-scatter.2
  320.7 26.3 reduce-scatter.4
where the time goes:
time: 357 us; the launch traced here: 356 us
  waiting for transfers between devices  227 us (64%)
  local copies, waits for them, and re-layouts  41.9 us (12%)
  blocking collectives  33.4 us (9%)
  starting transfers between devices  21.2 us (6%)
  between operations  13.7 us (4%)
  matrix products  10.3 us (3%)
  other arithmetic  8.32 us (2%)
    all_to_all x1, waiting for transfers between devices, in_one_piece(): lax.all_to_all(both, axis, split_axis=split_dim, concat_axis=concat_dim,...  193 us
    all_gather x1, blocking collectives, rows_first(): filled = lax.all_gather(both, axis, axis=0, tiled=True)  33.4 us
    all_to_all x1, waiting for transfers between devices, sent_to_all(): return lax.all_to_all(copies, axis, split_axis=0, concat_axis=0, tiled=True)  22.1 us
    slice x3, local copies, waits for them, and re-layouts, in_one_piece(): done.append(lax.slice_in_dim(filled, at, at + a.shape[along], axis=along))  10.4 us
    all_to_all x1, starting transfers between devices, in_one_piece(): lax.all_to_all(both, axis, split_axis=split_dim, concat_axis=concat_dim,...  9.49 us
    all_to_all x1, waiting for transfers between devices, summed_on_arrival(): lax.all_to_all(blocks, axis, split_axis=0, concat_axis=0, tiled=True)  8.8 us
    concatenate x1, local copies, waits for them, and re-layouts, in_one_piece(): both = jnp.concatenate(arrays, axis=along)  7.88 us
  transfers between devices with their start and end apart: 5, of which 4 were waited for; matrix products, arithmetic and copies ran while one was open for 11% of the time, Pallas kernels for 0%

commit v1 on v0

v1 whole, which is shorter than its diff:
```python
import functools

import jax
import jax.numpy as jnp
from jax import lax
from jax.experimental import pallas as pl
from jax.experimental.pallas import tpu as pltpu
from jax.sharding import Mesh
from jax.sharding import PartitionSpec as P

BLOCK = 128
LANES = 128
TENSOR = ("ty", "tx")
STORE = ("z", "core")
EVERY = ("z", "core", "ty", "tx")
VMEM = pl.BlockSpec(memory_space=pltpu.VMEM)
SMEM = pl.BlockSpec(memory_space=pltpu.SMEM)
ANY = pl.BlockSpec(memory_space=pl.ANY)
BF16 = jnp.bfloat16
F32 = jnp.float32
I32 = jnp.int32


def params():
    return pltpu.CompilerParams(vmem_limit_bytes=48 << 20)


def shift(count, by):
    return [(i, (i + by) % count) for i in range(count)]


def pack_kernel(cols, rank, down_ref, up_ref, out_ref):
    for c in range(cols):
        out_ref[:, c * rank : (c + 1) * rank, :] = down_ref[:, :, c * LANES : (c + 1) * LANES]
    out_ref[:, cols * rank :, :] = up_ref[...]


def pack(down, up):
    held, rank, feats = down.shape
    cols = feats // LANES
    mine = up.shape[1]
    ucols = up.shape[2] // LANES
    up_rows = up.reshape(held, mine, ucols, LANES).transpose(0, 2, 1, 3).reshape(held, mine * ucols, LANES)
    rows = cols * rank + mine * ucols
    return pl.pallas_call(
        functools.partial(pack_kernel, cols, rank),
        out_shape=jax.ShapeDtypeStruct((held, rows, LANES), BF16),
        in_specs=[VMEM, VMEM],
        out_specs=VMEM,
        compiler_params=params(),
    )(down, up_rows)


def plan(owners, slots, chips, cores, held, core):
    chip = owners // cores
    lane = owners % cores
    count = owners.shape[0]
    ids = jnp.arange(count, dtype=I32)
    rank = jnp.sum(((chip[None, :] == chip[:, None]) & (ids[None, :] < ids[:, None])).astype(I32), axis=1)
    back = (chip[:, None] - chip[None, :]) % chips
    reach = jnp.arange(1, chips, dtype=I32)
    within = (back[:, None, :] >= 1) & (back[:, None, :] <= reach[None, :, None])
    excess = jnp.sum(within.astype(I32), axis=2) - cores * reach[None, :]
    carry = jnp.maximum(jnp.max(excess, axis=1), 0)
    queue = carry + rank
    hops = queue // cores
    sender = (chip + hops) % chips
    place = sender * cores + queue % cores
    bad = jnp.max((hops > 1).astype(I32))
    source = (hops * cores + (lane != core).astype(I32)) * held + slots
    spots = jnp.arange(chips * cores, dtype=I32)
    asked = jnp.sum(jnp.where(place[None, :] == spots[:, None], source[None, :], 0), axis=1)
    return place, asked, bad


def select_kernel(held, asked_ref, *refs):
    tables, out_ref, buf, sem_in, sem_out = refs[:-4], refs[-4], refs[-3], refs[-2], refs[-1]
    count = out_ref.shape[0]

    def begin(i, carry):
        want = asked_ref[i]
        which = want // held
        row = want - which * held
        for k, table in enumerate(tables):

            @pl.when(which == k)
            def _():
                pltpu.make_async_copy(table.at[row], buf.at[i], sem_in.at[i]).start()

        return carry

    def onward(i, carry):
        pltpu.make_async_copy(tables[0].at[0], buf.at[i], sem_in.at[i]).wait()
        pltpu.make_async_copy(buf.at[i], out_ref.at[i], sem_out.at[i]).start()
        return carry

    def finish(i, carry):
        pltpu.make_async_copy(buf.at[i], out_ref.at[i], sem_out.at[i]).wait()
        return carry

    lax.fori_loop(0, count, begin, 0)
    lax.fori_loop(0, count, onward, 0)
    lax.fori_loop(0, count, finish, 0)


def select(asked, tables):
    held, rows, lanes = tables[0].shape
    count = asked.shape[0]
    return pl.pallas_call(
        functools.partial(select_kernel, held),
        out_shape=jax.ShapeDtypeStruct((count, rows, lanes), BF16),
        in_specs=[SMEM] + [ANY] * len(tables),
        out_specs=ANY,
        scratch_shapes=[
            pltpu.VMEM((count, rows, lanes), BF16),
            pltpu.SemaphoreType.DMA((count,)),
            pltpu.SemaphoreType.DMA((count,)),
        ],
        compiler_params=params(),
    )(asked, *tables)


def go_round(own, owners, slots, places, stores, me):
    count = owners.shape[0]
    order = shift(stores, -1)

    def step(h, state):
        table, kept = state
        here = (me + h) % stores
        mine = jnp.take(table, slots, axis=0)
        kept = jnp.where((owners == here)[:, None, None], mine, kept)
        return lax.ppermute(table, STORE, order), kept

    kept = jnp.zeros((count, *own.shape[1:]), own.dtype)
    _, kept = lax.fori_loop(0, stores, step, (own, kept))
    return jnp.pad(kept, ((0, places - count), (0, 0), (0, 0)))


def shrink_kernel(cols, rank, group, at_ref, tok_ref, got_ref, out_ref, buf, sem):
    blocks, rows, lanes = buf.shape
    half = group
    for b in range(blocks):
        pltpu.make_async_copy(got_ref.at[at_ref[b]], buf.at[b], sem.at[b]).start()
    per = 3
    for u in range(blocks // per):
        parts = []
        for b in range(u * per, (u + 1) * per):
            pltpu.make_async_copy(got_ref.at[0], buf.at[b], sem.at[b]).wait()
            down = jnp.concatenate([buf[b, c * rank : (c + 1) * rank, :] for c in range(cols)], axis=1)
            part = lax.dot_general(
                tok_ref[b * BLOCK : (b + 1) * BLOCK, :], down, (((1,), (1,)), ((), ())), preferred_element_type=F32
            )
            parts.append(part)
        whole = jnp.concatenate(parts, axis=0)
        for k in range(2):
            t = 2 * u + k
            one = whole[2 * half * k : 2 * half * k + half]
            two = whole[2 * half * k + half : 2 * half * k + 2 * half]
            out_ref[t, :half, :] = jnp.concatenate([one, two], axis=1).astype(BF16)
            out_ref[t, half : half + rows - cols * rank, :] = buf[u * per + k, cols * rank :, :]
            out_ref[t, half + rows - cols * rank :, :] = buf[u * per + k + 1, cols * rank :, :]


def shrink(at, tokens, got, rank, tensors):
    tok_rows, feats = tokens.shape
    blocks = tok_rows // BLOCK
    cols = feats // LANES
    places, rows, lanes = got.shape
    half = tok_rows // tensors // 2
    ups = rows - cols * rank
    return pl.pallas_call(
        functools.partial(shrink_kernel, cols, rank, half),
        out_shape=jax.ShapeDtypeStruct((tensors, half + 2 * ups, lanes), BF16),
        in_specs=[SMEM, VMEM, ANY],
        out_specs=VMEM,
        scratch_shapes=[pltpu.VMEM((blocks, rows, lanes), BF16), pltpu.SemaphoreType.DMA((blocks,))],
        compiler_params=params(),
    )(at, tokens, got)


def finish_kernel(rank, mine, odd_ref, got_ref, base_ref, out_ref):
    tensors, msg_rows, lanes = got_ref.shape
    total, kv = out_ref.shape
    half = total // 2
    ups = (msg_rows - half) // 2
    ucols = ups // mine
    low = jnp.sum(got_ref[:, :half, :].astype(F32), axis=0).astype(BF16)
    line = lax.broadcasted_iota(I32, (rank, ucols * tensors * ups), 0)
    col = lax.broadcasted_iota(I32, (rank, ucols * tensors * ups), 1)
    c_want = col // (tensors * ups)
    inner = col % (tensors * ups)
    src = inner // ups
    c_have = (inner % ups) // mine
    q = inner % mine
    spread = ((c_want == c_have) & (line == src * mine + q)).astype(F32).astype(BF16)
    edge = jnp.where(odd_ref[0] == 1, BLOCK // 2, BLOCK)
    maps = [got_ref[:, half + j * ups : half + (j + 1) * ups, :].reshape(tensors * ups, lanes) for j in range(2)]
    for h in range(2):
        part = low[:, h * rank : (h + 1) * rank]
        wide = jnp.dot(part, spread, preferred_element_type=F32).astype(BF16)
        row = lax.broadcasted_iota(I32, (half, lanes), 0) + h * half
        for c in range(ucols):
            piece = wide[:, c * tensors * ups : (c + 1) * tensors * ups]
            first = jnp.dot(piece, maps[0], preferred_element_type=F32)
            second = jnp.dot(piece, maps[1], preferred_element_type=F32)
            term = jnp.where(row < edge, first, second)
            here = base_ref[h * half : (h + 1) * half, c * lanes : (c + 1) * lanes].astype(F32)
            out_ref[h * half : (h + 1) * half, c * lanes : (c + 1) * lanes] = (here + term).astype(BF16)


def finish(odd, got, base, rank, mine):
    return pl.pallas_call(
        functools.partial(finish_kernel, rank, mine),
        out_shape=jax.ShapeDtypeStruct(base.shape, BF16),
        in_specs=[SMEM, VMEM, VMEM],
        out_specs=VMEM,
        compiler_params=params(),
    )(odd, got, base)


def local(tokens, base_weight, adapter_down, adapter_up, segment_blocks, segment_owner, segment_slot):
    chips, cores = lax.axis_size("z"), lax.axis_size("core")
    tensors = lax.axis_size(TENSOR)
    held, rank, feats = adapter_down.shape
    mine = adapter_up.shape[1]
    blocks = tokens.shape[0] // BLOCK
    core = lax.axis_index("core")
    owners, slots = segment_owner[:, 0], segment_slot

    own = pack(adapter_down, adapter_up)
    before = lax.ppermute(own, "z", shift(chips, 1))
    other = lax.ppermute(own, "core", shift(cores, 1))
    other_before = lax.ppermute(before, "core", shift(cores, 1))

    place, asked, bad = plan(owners, slots, chips, cores, held, core)
    ask = jnp.concatenate([asked.reshape(chips, cores), jnp.full((chips, 1), bad, I32)], axis=1)
    ask = jnp.pad(ask, ((0, 0), (0, LANES - cores - 1)))[:, None, :]
    ask = jnp.broadcast_to(ask, (chips, 8, LANES))
    told = lax.all_to_all(ask, "z", 0, 0, tiled=True)[:, 0, :]

    base = jnp.dot(tokens, base_weight, preferred_element_type=F32).astype(BF16)
    for axis in TENSOR:
        base = lax.psum_scatter(base, axis, scatter_dimension=0, tiled=True)

    wanted = told[:, :cores].reshape(-1)
    rows = select(wanted, (own, other, before, other_before))
    sent = rows.reshape(chips, cores, *rows.shape[1:])
    got = lax.all_to_all(sent, "z", 0, 0, tiled=True).reshape(rows.shape)

    lane_bad = jnp.max(told[:, cores])
    far_bad = lax.ppermute(jnp.broadcast_to(lane_bad, (8, LANES)), "core", shift(cores, 1))[0, 0]
    any_bad = jnp.maximum(lane_bad, far_bad) > 0
    me = lax.axis_index(STORE)
    got = lax.cond(
        any_bad,
        lambda g: go_round(own, owners, slots, chips * cores, chips * cores, me),
        lambda g: g,
        got,
    )
    place = jnp.where(any_bad, jnp.arange(place.shape[0], dtype=I32), place)
    ends = jnp.cumsum(segment_blocks[0])
    seg = jnp.sum((ends[None, :] <= jnp.arange(blocks, dtype=I32)[:, None]).astype(I32), axis=1)
    at = jnp.sum(
        jnp.where(seg[:, None] == jnp.arange(place.shape[0], dtype=I32)[None, :], place[None, :], 0), axis=1
    )

    message = shrink(at, tokens, got, rank, tensors)
    got_low = lax.all_to_all(message, TENSOR, 0, 0, tiled=True)
    odd = (lax.axis_index(TENSOR) % 2).astype(I32).reshape(1)
    return finish(odd, got_low, base, rank, mine)


def solution(mesh):
    split = Mesh(mesh.devices.reshape(-1, 2, 4, 4), EVERY)
    placed = (
        P(STORE, TENSOR),
        P(TENSOR, None),
        P(STORE, None, TENSOR),
        P(STORE, TENSOR, None),
        P(STORE, None),
        P(STORE, None),
        P(STORE),
    )
    return jax.shard_map(local, mesh=split, in_specs=placed, out_specs=P(EVERY, None), check_vma=False)
```

time: 357 us -> 218 us (0.61)
  the two profiles are of different devices: /device:TPU:64 before, /device:TPU:2 now
where the time goes in v1:
time: 218 us; the launch traced here: 217 us
  waiting for transfers between devices  129 us (59%)
  blocking collectives  21.9 us (10%)
  starting transfers between devices  20.9 us (10%)
  Pallas kernels  16 us (7%)
  between operations  14.8 us (7%)
  local copies, waits for them, and re-layouts  6.45 us (3%)
  matrix products  5.36 us (2%)
  other arithmetic  3.36 us (2%)
    reduce_scatter x2, waiting for transfers between devices, local(): base = lax.psum_scatter(base, axis, scatter_dimension=0, tiled=True)  47.4 us
    all_to_all x1, waiting for transfers between devices, local(): got = lax.all_to_all(sent, 'z', 0, 0, tiled=True).reshape(rows.shape)  41.9 us
    ppermute x1, waiting for transfers between devices, local(): before = lax.ppermute(own, 'z', shift(chips, 1))  29.5 us
    all_to_all x1, blocking collectives, local(): told = lax.all_to_all(ask, 'z', 0, 0, tiled=True)[:, 0, :]  21.9 us
    pallas_call x1, Pallas kernels, shrink(): pl.pallas_call(functools.partial(shrink_kernel, cols, rank, half), out_sh...  9.14 us
    all_to_all x1, waiting for transfers between devices, local(): got_low = lax.all_to_all(message, TENSOR, 0, 0, tiled=True)  8.76 us
    all_to_all x1, starting transfers between devices, local(): got_low = lax.all_to_all(message, TENSOR, 0, 0, tiled=True)  7.49 us
    dot_general x1, matrix products, local(): base = jnp.dot(tokens, base_weight, preferred_element_type=F32).astype(BF16)  5.36 us
  transfers between devices with their start and end apart: 8, of which 5 were waited for; matrix products, arithmetic and copies ran while one was open for 5% of the time, Pallas kernels for 4%

profile of v1, /device:TPU:2, one launch (start us, length us, event | category | flops | bytes accessed | tf_op | source)
XLA Modules:
  0.0 217.3 jit_solution(15896219351830747758)
XLA Ops:
  6.5 1.3 copy-done.2
  7.8 0.8 copy-done.4
  8.7 1.2 shard_map.73.refs_0_
  9.9 3.8 %collective-permute-start.3 = (bf16[16,272,128]{2,1,0:T(8,128)(2,1)}, bf16[16,272,128]{2,1,0:T(8,128)(2,1)S(1)}, u32[]{:S(2)}, u32[]{:S(2)}) collective-permute-start(bf16[16,272,128]{2,1,0:T(8,128)(2,1)} %shard_map.73.refs_0_), channel_id=1, source_target_pairs={{0,32},{32,64},{64,96},{96,128},{128,160},{160,192},{192,224},{224... | collective-permute-start | bytes 3342344 | tf_op jit(solution)/shard_map/ppermute | solution.py:231
  13.7 1.9 collective-permute-start.2
  16.6 29.5 %collective-permute-done.3.refs_2_ = bf16[16,272,128]{2,1,0:T(8,128)(2,1)S(1)} collective-permute-done((bf16[16,272,128]{2,1,0:T(8,128)(2,1)}, bf16[16,272,128]{2,1,0:T(8,128)(2,1)S(1)}, u32[]{:S(2)}, u32[]{:S(2)}) %collective-permute-start.3) | collective-permute-done | bytes 1114144 | tf_op jit(solution)/shard_map/ppermute | solution.py:231
  46.0 1.9 collective-permute-start.4
  48.9 0.7 pad_select_fusion
  49.6 21.9 %all_to_all.16 = s32[16,8,128]{2,1,0:T(8,128)S(1)} all-to-all(s32[16,8,128]{2,1,0:T(8,128)S(1)} %broadcast_in_dim.105), channel_id=1, replica_groups=mesh['z'=16,'core'=2,'ty'=4,'tx'=4] {'z'}, dimensions={0} | all-to-all | bytes 131072 | tf_op jit(solution)/shard_map/all_to_all | solution.py:239
  71.6 4.3 %shard_map.74 = bf16[32,272,128]{2,1,0:T(8,128)(2,1)} custom-call(s32[32]{0:T(128)S(1)} %reshape.256.asked_ref, bf16[16,272,128]{2,1,0:T(8,128)(2,1)} %shard_map.73.refs_0_, bf16[16,272,128]{2,1,0:T(8,128)(2,1)S(1)} %collective-permute-done.2.refs_1_, bf16[16,272,128]{2,1,0:T(8,128)(2,1)S(1)} %collective-permute-done.3.refs_2_, ...), custom_call_target="tpu_custom_call" | custom-call | tf_op jit(solution)/shard_map/pallas_call | solution.py:109
  75.9 3.8 %all-to-all-start.1 = ((bf16[16,2,272,128]{3,2,1,0:T(8,128)(2,1)}), bf16[16,2,272,128]{3,2,1,0:T(8,128)(2,1)S(1)}, u32[]{:S(2)}, u32[]{:S(2)}) async-start(bf16[16,2,272,128]{3,2,1,0:T(8,128)(2,1)} %bitcast.10), calls=%async_computation.1 | async-start | bytes 4456448 | tf_op jit(solution)/shard_map/all_to_all | solution.py:248
  79.7 5.4 %convolution_convert_fusion = bf16[3072,512]{1,0:T(8,128)(2,1)} fusion(bf16[3072,512]{1,0:T(8,128)(2,1)} %tok_ref.1, bf16[512,512]{1,0:T(8,128)(2,1)S(1)} %copy-done), kind=kOutput, calls=%fused_computation.8 | convolution fusion | flops 1612185600 | bytes 6815744 | tf_op jit(solution)/shard_map/dot_general | solution.py:241
  85.1 47.3 %reduce-scatter.3.cloned.1.call-done = bf16[768,512]{1,0:T(8,128)(2,1)} async-done(((bf16[3072,512]{1,0:T(8,128)(2,1)}), bf16[768,512]{1,0:T(8,128)(2,1)}) %reduce-scatter.3.cloned.1.call-update) | async-done | bytes 786448 | tf_op jit(solution)/shard_map/reduce_scatter | solution.py:243
  132.8 0.7 slice_reduce_fusion
  133.5 0.6 broadcast_in_dim.106
  134.1 1.9 collective-permute-start.1
  136.2 1.0 collective-permute-done.1
  139.0 41.9 %all-to-all-done.1 = bf16[16,2,272,128]{3,2,1,0:T(8,128)(2,1)S(1)} async-done(((bf16[16,2,272,128]{3,2,1,0:T(8,128)(2,1)}), bf16[16,2,272,128]{3,2,1,0:T(8,128)(2,1)S(1)}, u32[]{:S(2)}, u32[]{:S(2)}) %all-to-all-start.1) | async-done | bytes 2228256 | tf_op jit(solution)/shard_map/all_to_all | solution.py:248
  180.9 1.9 copy-done.1
  182.8 9.1 %shard_map.75 = bf16[16,128,128]{2,1,0:T(8,128)(2,1)} custom-call(s32[24]{0:T(128)S(1)} %select_reduce_fusion.at_ref, bf16[3072,512]{1,0:T(8,128)(2,1)S(1)} %copy-done.1, bf16[32,272,128]{2,1,0:T(8,128)(2,1)S(1)} %get-tuple-element.296.got_ref), custom_call_target="tpu_custom_call" | custom-call | tf_op jit(solution)/shard_map/pallas_call | solution.py:171
  191.9 7.5 %all-to-all-start.2 = ((bf16[16,128,128]{2,1,0:T(8,128)(2,1)}), bf16[16,128,128]{2,1,0:T(8,128)(2,1)S(1)}, u32[]{:S(2)}, u32[]{:S(2)}) async-start(bf16[16,128,128]{2,1,0:T(8,128)(2,1)} %shard_map.75), calls=%async_computation.2 | async-start | bytes 1048576 | tf_op jit(solution)/shard_map/all_to_all | solution.py:268
  199.4 8.8 %all-to-all-done.2.got_ref = bf16[16,128,128]{2,1,0:T(8,128)(2,1)S(1)} async-done(((bf16[16,128,128]{2,1,0:T(8,128)(2,1)}), bf16[16,128,128]{2,1,0:T(8,128)(2,1)S(1)}, u32[]{:S(2)}, u32[]{:S(2)}) %all-to-all-start.2) | async-done | bytes 524320 | tf_op jit(solution)/shard_map/all_to_all | solution.py:268
  208.2 0.9 copy-done.3
  209.1 1.4 shard_map.76
  (43 shorter events, 3.0 us)
Async XLA Ops:
  6.5 73.2 %copy-start = (bf16[512,512]{1,0:T(8,128)(2,1)S(1)}, bf16[512,512]{1,0:T(8,128)(2,1)}, u32[]{:S(2)}) copy-start(bf16[512,512]{1,0:T(8,128)(2,1)} %param.12) | copy-start | bytes 1572868
  6.5 9.1 %copy-start.6 = (s32[22,1]{0,1:T(1,128)S(1)}, s32[22,1]{0,1:T(1,128)}, u32[]{:S(2)}) copy-start(s32[22,1]{0,1:T(1,128)} %param.16) | copy-start | bytes 268
  6.5 42.1 %copy-start.5 = (s32[22]{0:T(128)S(1)}, s32[22]{0:T(128)}, u32[]{:S(2)}) copy-start(s32[22]{0:T(128)} %param.17) | copy-start | bytes 268
  6.5 1.3 copy-start.2
  7.8 0.8 copy-start.4
  9.9 36.2 %collective-permute-start.3 = (bf16[16,272,128]{2,1,0:T(8,128)(2,1)}, bf16[16,272,128]{2,1,0:T(8,128)(2,1)S(1)}, u32[]{:S(2)}, u32[]{:S(2)}) collective-permute-start(bf16[16,272,128]{2,1,0:T(8,128)(2,1)} %shard_map.73.refs_0_), channel_id=1, source_target_pairs={{0,32},{32,64},{64,96},{96,128},{128,160},{160,192},{192,224},{224... | collective-permute-start | bytes 3342344 | tf_op jit(solution)/shard_map/ppermute | solution.py:231
  13.7 57.8 %collective-permute-start.2 = (bf16[16,272,128]{2,1,0:T(8,128)(2,1)}, bf16[16,272,128]{2,1,0:T(8,128)(2,1)S(1)}, u32[]{:S(2)}, u32[]{:S(2)}) collective-permute-start(bf16[16,272,128]{2,1,0:T(8,128)(2,1)} %shard_map.73.refs_0_), channel_id=1, source_target_pairs={{0,16},{16,0},{1,17},{17,1},{2,18},{18,2},{3,19},{19,3},{4,20},{20... | collective-permute-start | bytes 3342344 | tf_op jit(solution)/shard_map/ppermute | solution.py:232
  46.0 25.5 %collective-permute-start.4 = (bf16[16,272,128]{2,1,0:T(8,128)(2,1)S(1)}, bf16[16,272,128]{2,1,0:T(8,128)(2,1)}, u32[]{:S(2)}, u32[]{:S(2)}) collective-permute-start(bf16[16,272,128]{2,1,0:T(8,128)(2,1)S(1)} %collective-permute-done.3.refs_2_), channel_id=1, source_target_pairs={{0,16},{16,0},{1,17},{17,1},{2,18},{18,2},{3,19},{19,3},{4,20},{20... | collective-permute-start | bytes 3342344 | tf_op jit(solution)/shard_map/ppermute | solution.py:233
  75.9 105.0 %all-to-all-start.1 = ((bf16[16,2,272,128]{3,2,1,0:T(8,128)(2,1)}), bf16[16,2,272,128]{3,2,1,0:T(8,128)(2,1)S(1)}, u32[]{:S(2)}, u32[]{:S(2)}) async-start(bf16[16,2,272,128]{3,2,1,0:T(8,128)(2,1)} %bitcast.10), calls=%async_computation.1 | async-start | bytes 4456448 | tf_op jit(solution)/shard_map/all_to_all | solution.py:248
  79.6 52.8 %reduce-scatter.3.cloned.1.call-start = ((), (), s32[]{:S(2)}) async-start(), calls=%async_computation.5 | async-start | bytes 3932160 | tf_op jit(solution)/shard_map/reduce_scatter | solution.py:243
  85.1 47.4 %copy-start.7 = (s32[1,22]{1,0:T(1,128)S(1)}, s32[1,22]{1,0:T(1,128)}, u32[]{:S(2)}) copy-start(s32[1,22]{1,0:T(1,128)} %param.15) | copy-start | bytes 268
  85.1 114.3 %reduce-scatter.5.cloned.1.call-start = ((), (), s32[]{:S(2)}) async-start(), calls=%async_computation.6 | async-start | bytes 983040 | tf_op jit(solution)/shard_map/reduce_scatter | solution.py:243
  134.1 3.1 %collective-permute-start.1 = (s32[8,128]{1,0:T(8,128)S(1)}, s32[8,128]{1,0:T(8,128)S(1)}, u32[]{:S(2)}, u32[]{:S(2)}) collective-permute-start(s32[8,128]{1,0:T(8,128)S(1)} %broadcast_in_dim.106), channel_id=1, source_target_pairs={{0,16},{16,0},{1,17},{17,1},{2,18},{18,2},{3,19},{19,3},{4,20},{20... | collective-permute-start | bytes 12296 | tf_op jit(solution)/shard_map/ppermute | solution.py:251
  180.9 1.9 copy-start.1
  191.9 16.3 %all-to-all-start.2 = ((bf16[16,128,128]{2,1,0:T(8,128)(2,1)}), bf16[16,128,128]{2,1,0:T(8,128)(2,1)S(1)}, u32[]{:S(2)}, u32[]{:S(2)}) async-start(bf16[16,128,128]{2,1,0:T(8,128)(2,1)} %shard_map.75), calls=%async_computation.2 | async-start | bytes 1048576 | tf_op jit(solution)/shard_map/all_to_all | solution.py:268
  208.2 0.9 copy-start.3
Sparse Core Ops, SparseCore 0:
  85.2 47.2 reduce-scatter.2
  135.3 27.9 reduce-scatter.4

commit v2 on v1

--- a/solution.py
+++ b/solution.py
@@ -22,7 +22,25 @@
 
 
 def params():
-    return pltpu.CompilerParams(vmem_limit_bytes=48 << 20)
+    return pltpu.CompilerParams(vmem_limit_bytes=16 << 20)
+
+
+def summed_rows(terms, axes):
+    running = terms
+    for axis in axes:
+        count = lax.axis_size(axis)
+        me = lax.axis_index(axis)
+        size = running.shape[0] // count
+
+        def piece(d, x=running, me=me, count=count, size=size):
+            return lax.dynamic_slice_in_dim(x, (me + d) % count * size, size, 0)
+
+        came = [lax.ppermute(piece(d), axis, shift(count, d)) for d in range(1, count)]
+        total = piece(0).astype(F32)
+        for one in came:
+            total = total + one.astype(F32)
+        running = total.astype(BF16)
+    return running
 
 
 def shift(count, by):
@@ -73,11 +91,11 @@
     return place, asked, bad
 
 
-def select_kernel(held, asked_ref, *refs):
-    tables, out_ref, buf, sem_in, sem_out = refs[:-4], refs[-4], refs[-3], refs[-2], refs[-1]
-    count = out_ref.shape[0]
-
-    def begin(i, carry):
+def select_kernel(asked_ref, *refs):
+    tables, out_ref = refs[:-1], refs[-1]
+    held = tables[0].shape[0]
+
+    def one(i, carry):
         want = asked_ref[i]
         which = want // held
         row = want - which * held
@@ -85,37 +103,20 @@
 
             @pl.when(which == k)
             def _():
-                pltpu.make_async_copy(table.at[row], buf.at[i], sem_in.at[i]).start()
+                out_ref[i] = table[row]
 
         return carry
 
-    def onward(i, carry):
-        pltpu.make_async_copy(tables[0].at[0], buf.at[i], sem_in.at[i]).wait()
-        pltpu.make_async_copy(buf.at[i], out_ref.at[i], sem_out.at[i]).start()
-        return carry
-
-    def finish(i, carry):
-        pltpu.make_async_copy(buf.at[i], out_ref.at[i], sem_out.at[i]).wait()
-        return carry
-
-    lax.fori_loop(0, count, begin, 0)
-    lax.fori_loop(0, count, onward, 0)
-    lax.fori_loop(0, count, finish, 0)
+    lax.fori_loop(0, out_ref.shape[0], one, 0)
 
 
 def select(asked, tables):
-    held, rows, lanes = tables[0].shape
-    count = asked.shape[0]
-    return pl.pallas_call(
-        functools.partial(select_kernel, held),
-        out_shape=jax.ShapeDtypeStruct((count, rows, lanes), BF16),
-        in_specs=[SMEM] + [ANY] * len(tables),
-        out_specs=ANY,
-        scratch_shapes=[
-            pltpu.VMEM((count, rows, lanes), BF16),
-            pltpu.SemaphoreType.DMA((count,)),
-            pltpu.SemaphoreType.DMA((count,)),
-        ],
+    _, rows, lanes = tables[0].shape
+    return pl.pallas_call(
+        select_kernel,
+        out_shape=jax.ShapeDtypeStruct((asked.shape[0], rows, lanes), BF16),
+        in_specs=[SMEM] + [VMEM] * len(tables),
+        out_specs=VMEM,
         compiler_params=params(),
     )(asked, *tables)
 
@@ -136,17 +137,15 @@
     return jnp.pad(kept, ((0, places - count), (0, 0), (0, 0)))
 
 
-def shrink_kernel(cols, rank, group, at_ref, tok_ref, got_ref, out_ref, buf, sem):
-    blocks, rows, lanes = buf.shape
-    half = group
-    for b in range(blocks):
-        pltpu.make_async_copy(got_ref.at[at_ref[b]], buf.at[b], sem.at[b]).start()
+def shrink_kernel(cols, rank, half, at_ref, tok_ref, got_ref, out_ref):
+    blocks = tok_ref.shape[0] // BLOCK
+    ups = got_ref.shape[1] - cols * rank
     per = 3
     for u in range(blocks // per):
         parts = []
         for b in range(u * per, (u + 1) * per):
-            pltpu.make_async_copy(got_ref.at[0], buf.at[b], sem.at[b]).wait()
-            down = jnp.concatenate([buf[b, c * rank : (c + 1) * rank, :] for c in range(cols)], axis=1)
+            place = at_ref[b]
+            down = jnp.concatenate([got_ref[place, c * rank : (c + 1) * rank, :] for c in range(cols)], axis=1)
             part = lax.dot_general(
                 tok_ref[b * BLOCK : (b + 1) * BLOCK, :], down, (((1,), (1,)), ((), ())), preferred_element_type=F32
             )
@@ -157,30 +156,28 @@
             one = whole[2 * half * k : 2 * half * k + half]
             two = whole[2 * half * k + half : 2 * half * k + 2 * half]
             out_ref[t, :half, :] = jnp.concatenate([one, two], axis=1).astype(BF16)
-            out_ref[t, half : half + rows - cols * rank, :] = buf[u * per + k, cols * rank :, :]
-            out_ref[t, half + rows - cols * rank :, :] = buf[u * per + k + 1, cols * rank :, :]
+            out_ref[t, half : half + ups, :] = got_ref[at_ref[u * per + k], cols * rank :, :]
+            out_ref[t, half + ups :, :] = got_ref[at_ref[u * per + k + 1], cols * rank :, :]
 
 
 def shrink(at, tokens, got, rank, tensors):
     tok_rows, feats = tokens.shape
-    blocks = tok_rows // BLOCK
     cols = feats // LANES
-    places, rows, lanes = got.shape
+    _, rows, lanes = got.shape
     half = tok_rows // tensors // 2
     ups = rows - cols * rank
     return pl.pallas_call(
         functools.partial(shrink_kernel, cols, rank, half),
         out_shape=jax.ShapeDtypeStruct((tensors, half + 2 * ups, lanes), BF16),
-        in_specs=[SMEM, VMEM, ANY],
-        out_specs=VMEM,
-        scratch_shapes=[pltpu.VMEM((blocks, rows, lanes), BF16), pltpu.SemaphoreType.DMA((blocks,))],
+        in_specs=[SMEM, VMEM, VMEM],
+        out_specs=VMEM,
         compiler_params=params(),
     )(at, tokens, got)
 
 
 def finish_kernel(rank, mine, odd_ref, got_ref, base_ref, out_ref):
     tensors, msg_rows, lanes = got_ref.shape
-    total, kv = out_ref.shape
+    total, _ = out_ref.shape
     half = total // 2
     ups = (msg_rows - half) // 2
     ucols = ups // mine
@@ -218,10 +215,10 @@
     )(odd, got, base)
 
 
-def local(tokens, base_weight, adapter_down, adapter_up, segment_blocks, segment_owner, segment_slot):
+def device_part(tokens, base_weight, adapter_down, adapter_up, segment_blocks, segment_owner, segment_slot):
     chips, cores = lax.axis_size("z"), lax.axis_size("core")
     tensors = lax.axis_size(TENSOR)
-    held, rank, feats = adapter_down.shape
+    held, rank, _ = adapter_down.shape
     mine = adapter_up.shape[1]
     blocks = tokens.shape[0] // BLOCK
     core = lax.axis_index("core")
@@ -230,22 +227,24 @@
     own = pack(adapter_down, adapter_up)
     before = lax.ppermute(own, "z", shift(chips, 1))
     other = lax.ppermute(own, "core", shift(cores, 1))
-    other_before = lax.ppermute(before, "core", shift(cores, 1))
 
     place, asked, bad = plan(owners, slots, chips, cores, held, core)
     ask = jnp.concatenate([asked.reshape(chips, cores), jnp.full((chips, 1), bad, I32)], axis=1)
     ask = jnp.pad(ask, ((0, 0), (0, LANES - cores - 1)))[:, None, :]
     ask = jnp.broadcast_to(ask, (chips, 8, LANES))
-    told = lax.all_to_all(ask, "z", 0, 0, tiled=True)[:, 0, :]
-
-    base = jnp.dot(tokens, base_weight, preferred_element_type=F32).astype(BF16)
-    for axis in TENSOR:
-        base = lax.psum_scatter(base, axis, scatter_dimension=0, tiled=True)
-
+    told = lax.all_to_all(ask, "z", 0, 0, tiled=True)
+    told = jnp.clip(told[:, 0, :], 0, 2 * cores * held)
+
+    other_before = lax.ppermute(before, "core", shift(cores, 1))
     wanted = told[:, :cores].reshape(-1)
     rows = select(wanted, (own, other, before, other_before))
+    rows, base_weight = lax.optimization_barrier((rows, base_weight))
     sent = rows.reshape(chips, cores, *rows.shape[1:])
-    got = lax.all_to_all(sent, "z", 0, 0, tiled=True).reshape(rows.shape)
+    got = lax.all_to_all(sent, "z", 0, 0, tiled=True)
+    got = got.reshape(rows.shape)
+
+    base = jnp.dot(tokens, base_weight, preferred_element_type=F32).astype(BF16)
+    base = summed_rows(base, TENSOR)
 
     lane_bad = jnp.max(told[:, cores])
     far_bad = lax.ppermute(jnp.broadcast_to(lane_bad, (8, LANES)), "core", shift(cores, 1))[0, 0]
@@ -281,4 +280,4 @@
         P(STORE, None),
         P(STORE),
     )
-    return jax.shard_map(local, mesh=split, in_specs=placed, out_specs=P(EVERY, None), check_vma=False)
+    return jax.shard_map(device_part, mesh=split, in_specs=placed, out_specs=P(EVERY, None), check_vma=False)

time: 218 us -> 207 us (0.950)
  the two profiles are of different devices: /device:TPU:2 before, /device:TPU:8 now
where the time goes in v2:
time: 207 us; the launch traced here: 206 us
  waiting for transfers between devices  108 us (52%)
  starting transfers between devices  41.4 us (20%)
  blocking collectives  21.9 us (11%)
  other arithmetic  10.1 us (5%)
  local copies, waits for them, and re-layouts  9.31 us (4%)
  Pallas kernels  9.2 us (4%)
  matrix products  3.69 us (2%)
    all_to_all x1, waiting for transfers between devices, device_part(): got = lax.all_to_all(sent, 'z', 0, 0, tiled=True)  50 us
    ppermute x1, waiting for transfers between devices, device_part(): before = lax.ppermute(own, 'z', shift(chips, 1))  32 us
    ppermute x6, waiting for transfers between devices, summed_rows(): lax.ppermute(piece(d), axis, shift(count, d))  26 us
    all_to_all x1, blocking collectives, device_part(): told = lax.all_to_all(ask, 'z', 0, 0, tiled=True)  21.9 us
    ppermute x6, starting transfers between devices, summed_rows(): lax.ppermute(piece(d), axis, shift(count, d))  20.8 us
    all_to_all x1, starting transfers between devices, device_part(): got_low = lax.all_to_all(message, TENSOR, 0, 0, tiled=True)  7.4 us
    unnamed x22, local copies, waits for them, and re-layouts  5.68 us
    pallas_call x1, Pallas kernels, select(): pl.pallas_call(select_kernel, out_shape=jax.ShapeDtypeStruct((asked.shape...  4.24 us
  transfers between devices with their start and end apart: 12, of which 8 were waited for; matrix products, arithmetic and copies ran while one was open for 8% of the time, Pallas kernels for 0%

profile of v2, /device:TPU:8, one launch (start us, length us, event | category | flops | bytes accessed | tf_op | source)
XLA Modules:
  0.0 205.6 jit_solution(11279372266109063288)
XLA Ops:
  3.4 1.9 collective-permute-start.2
  5.3 3.8 %collective-permute-start.3 = (bf16[16,272,128]{2,1,0:T(8,128)(2,1)}, bf16[16,272,128]{2,1,0:T(8,128)(2,1)S(1)}, u32[]{:S(2)}, u32[]{:S(2)}) collective-permute-start(bf16[16,272,128]{2,1,0:T(8,128)(2,1)} %shard_map.73.refs_0_), channel_id=1, source_target_pairs={{0,32},{32,64},{64,96},{96,128},{128,160},{160,192},{192,224},{224... | collective-permute-start | bytes 3342344 | tf_op jit(solution)/shard_map/ppermute | solution.py:228
  10.1 32.0 %collective-permute-done.3.refs_2_ = bf16[16,272,128]{2,1,0:T(8,128)(2,1)S(1)} collective-permute-done((bf16[16,272,128]{2,1,0:T(8,128)(2,1)}, bf16[16,272,128]{2,1,0:T(8,128)(2,1)S(1)}, u32[]{:S(2)}, u32[]{:S(2)}) %collective-permute-start.3) | collective-permute-done | bytes 1114144 | tf_op jit(solution)/shard_map/ppermute | solution.py:228
  42.1 1.9 collective-permute-start.4
  45.6 21.9 %all_to_all.16 = s32[16,8,128]{2,1,0:T(8,128)S(1)} all-to-all(s32[16,8,128]{2,1,0:T(8,128)S(1)} %broadcast_in_dim.105), channel_id=1, replica_groups=mesh['z'=16,'core'=2,'ty'=4,'tx'=4] {'z'}, dimensions={0} | all-to-all | bytes 131072 | tf_op jit(solution)/shard_map/all_to_all | solution.py:235
  67.5 4.2 %shard_map.74 = bf16[32,272,128]{2,1,0:T(8,128)(2,1)} custom-call(s32[32]{0:T(128)S(1)} %reshape.259.asked_ref, bf16[16,272,128]{2,1,0:T(8,128)(2,1)} %shard_map.73.refs_0_, bf16[16,272,128]{2,1,0:T(8,128)(2,1)S(1)} %collective-permute-done.2.refs_1_, bf16[16,272,128]{2,1,0:T(8,128)(2,1)S(1)} %collective-permute-done.3.refs_2_, ...), custom_call_target="tpu_custom_call" | custom-call | tf_op jit(solution)/shard_map/pallas_call | solution.py:115
  71.8 3.7 %all-to-all-start.1 = ((bf16[16,2,272,128]{3,2,1,0:T(8,128)(2,1)}), bf16[16,2,272,128]{3,2,1,0:T(8,128)(2,1)S(1)}, u32[]{:S(2)}, u32[]{:S(2)}) async-start(bf16[16,2,272,128]{3,2,1,0:T(8,128)(2,1)} %bitcast.10), calls=%async_computation.1 | async-start | bytes 4456448 | tf_op jit(solution)/shard_map/all_to_all | solution.py:243
  75.6 3.7 %convolution_convert_fusion = bf16[512,3072]{0,1:T(8,128)(2,1)S(1)} fusion(bf16[3072,512]{1,0:T(8,128)(2,1)} %tok_ref.1, bf16[512,512]{1,0:T(8,128)(2,1)S(1)} %copy-done), kind=kOutput, calls=%fused_computation.8 | convolution fusion | flops 1612185600 | bytes 6815744 | tf_op jit(solution)/shard_map/dot_general | solution.py:246
  82.4 2.3 %collective-permute-start.7 = (bf16[768,512]{1,0:T(8,128)(2,1)}, bf16[768,512]{1,0:T(8,128)(2,1)S(1)}, u32[]{:S(2)}, u32[]{:S(2)}) collective-permute-start(bf16[768,512]{1,0:T(8,128)(2,1)} %get-tuple-element.226), channel_id=1, source_target_pairs={{0,12},{4,0},{8,4},{12,8},{1,13},{5,1},{9,5},{13,9},{2,14},{6,2},{... | collective-permute-start | bytes 2359304 | tf_op jit(solution)/shard_map/ppermute | solution.py:38
  84.8 4.5 %collective-permute-start.6 = (bf16[768,512]{1,0:T(8,128)(2,1)}, bf16[768,512]{1,0:T(8,128)(2,1)}, u32[]{:S(2)}, u32[]{:S(2)}) collective-permute-start(bf16[768,512]{1,0:T(8,128)(2,1)} %get-tuple-element.227), channel_id=1, source_target_pairs={{0,8},{4,12},{8,0},{12,4},{1,9},{5,13},{9,1},{13,5},{2,10},{6,14},... | collective-permute-start | bytes 2359304 | tf_op jit(solution)/shard_map/ppermute | solution.py:38
  89.3 3.8 %collective-permute-start.5 = (bf16[768,512]{1,0:T(8,128)(2,1)}, bf16[768,512]{1,0:T(8,128)(2,1)}, u32[]{:S(2)}, u32[]{:S(2)}) collective-permute-start(bf16[768,512]{1,0:T(8,128)(2,1)} %get-tuple-element.225), channel_id=1, source_target_pairs={{0,4},{4,8},{8,12},{12,0},{1,5},{5,9},{9,13},{13,1},{2,6},{6,10},{... | collective-permute-start | bytes 2359304 | tf_op jit(solution)/shard_map/ppermute | solution.py:38
  97.8 1.9 collective-permute-start.1
  103.9 16.7 %collective-permute-done.6 = bf16[768,512]{1,0:T(8,128)(2,1)} collective-permute-done((bf16[768,512]{1,0:T(8,128)(2,1)}, bf16[768,512]{1,0:T(8,128)(2,1)}, u32[]{:S(2)}, u32[]{:S(2)}) %collective-permute-start.6) | collective-permute-done | bytes 786464 | tf_op jit(solution)/shard_map/ppermute | solution.py:38
  120.6 2.7 %collective-permute-done.5 = bf16[768,512]{1,0:T(8,128)(2,1)} collective-permute-done((bf16[768,512]{1,0:T(8,128)(2,1)}, bf16[768,512]{1,0:T(8,128)(2,1)}, u32[]{:S(2)}, u32[]{:S(2)}) %collective-permute-start.5) | collective-permute-done | bytes 786464 | tf_op jit(solution)/shard_map/ppermute | solution.py:38
  123.3 2.9 %fusion.3 = bf16[768,512]{1,0:T(8,128)(2,1)} fusion(bf16[768,512]{1,0:T(8,128)(2,1)S(1)} %collective-permute-done.7, bf16[768,512]{1,0:T(8,128)(2,1)} %collective-permute-done.6, bf16[768,512]{1,0:T(8,128)(2,1)} %collective-permute-done.5, bf16[512,3072]{0,1:T(8,128)(2,1)} %copy-done.5, s32[]{:T(128)S(6)} %select_n.231), kind=kLoop, calls=%fused_computation.12 | loop fusion | flops 3145728 | bytes 3932164 | tf_op jit(solution)/shard_map/convert_element_type | solution.py:42
  126.3 50.0 %all-to-all-done.1 = bf16[16,2,272,128]{3,2,1,0:T(8,128)(2,1)S(1)} async-done(((bf16[16,2,272,128]{3,2,1,0:T(8,128)(2,1)}), bf16[16,2,272,128]{3,2,1,0:T(8,128)(2,1)S(1)}, u32[]{:S(2)}, u32[]{:S(2)}) %all-to-all-start.1) | async-done | bytes 2228256 | tf_op jit(solution)/shard_map/all_to_all | solution.py:243
  176.3 1.9 copy-done.1
  178.2 2.4 %shard_map.75 = bf16[16,128,128]{2,1,0:T(8,128)(2,1)} custom-call(s32[24]{0:T(128)S(1)} %select_reduce_fusion.at_ref, bf16[3072,512]{1,0:T(8,128)(2,1)S(1)} %copy-done.1, bf16[32,272,128]{2,1,0:T(8,128)(2,1)S(1)} %get-tuple-element.306.got_ref), custom_call_target="tpu_custom_call" | custom-call | tf_op jit(solution)/shard_map/pallas_call | solution.py:169
  180.6 7.4 %all-to-all-start.2 = ((bf16[16,128,128]{2,1,0:T(8,128)(2,1)}), bf16[16,128,128]{2,1,0:T(8,128)(2,1)S(1)}, u32[]{:S(2)}, u32[]{:S(2)}) async-start(bf16[16,128,128]{2,1,0:T(8,128)(2,1)} %shard_map.75), calls=%async_computation.2 | async-start | bytes 1048576 | tf_op jit(solution)/shard_map/all_to_all | solution.py:267
  188.0 4.6 %collective-permute-start.10 = (bf16[192,512]{1,0:T(8,128)(2,1)S(1)}, bf16[192,512]{1,0:T(8,128)(2,1)S(1)}, u32[]{:S(2)}, u32[]{:S(2)}) collective-permute-start(bf16[192,512]{1,0:T(8,128)(2,1)S(1)} %get-tuple-element.229), channel_id=1, source_target_pairs={{0,3},{1,0},{2,1},{3,2},{4,7},{5,4},{6,5},{7,6},{8,11},{9,8},{10,9... | collective-permute-start | bytes 589832 | tf_op jit(solution)/shard_map/ppermute | solution.py:38
  192.6 2.8 %collective-permute-start.9 = (bf16[192,512]{1,0:T(8,128)(2,1)S(1)}, bf16[192,512]{1,0:T(8,128)(2,1)S(1)}, u32[]{:S(2)}, u32[]{:S(2)}) collective-permute-start(bf16[192,512]{1,0:T(8,128)(2,1)S(1)} %get-tuple-element.230), channel_id=1, source_target_pairs={{0,2},{1,3},{2,0},{3,1},{4,6},{5,7},{6,4},{7,5},{8,10},{9,11},{10,... | collective-permute-start | bytes 589832 | tf_op jit(solution)/shard_map/ppermute | solution.py:38
  195.4 2.8 %collective-permute-start.8 = (bf16[192,512]{1,0:T(8,128)(2,1)S(1)}, bf16[192,512]{1,0:T(8,128)(2,1)S(1)}, u32[]{:S(2)}, u32[]{:S(2)}) collective-permute-start(bf16[192,512]{1,0:T(8,128)(2,1)S(1)} %get-tuple-element.228), channel_id=1, source_target_pairs={{0,1},{1,2},{2,3},{3,0},{4,5},{5,6},{6,7},{7,4},{8,9},{9,10},{10,1... | collective-permute-start | bytes 589832 | tf_op jit(solution)/shard_map/ppermute | solution.py:38
  198.2 3.6 %collective-permute-done.9 = bf16[192,512]{1,0:T(8,128)(2,1)S(1)} collective-permute-done((bf16[192,512]{1,0:T(8,128)(2,1)S(1)}, bf16[192,512]{1,0:T(8,128)(2,1)S(1)}, u32[]{:S(2)}, u32[]{:S(2)}) %collective-permute-start.9) | collective-permute-done | bytes 196640 | tf_op jit(solution)/shard_map/ppermute | solution.py:38
  201.8 2.3 %collective-permute-done.8 = bf16[192,512]{1,0:T(8,128)(2,1)S(1)} collective-permute-done((bf16[192,512]{1,0:T(8,128)(2,1)S(1)}, bf16[192,512]{1,0:T(8,128)(2,1)S(1)}, u32[]{:S(2)}, u32[]{:S(2)}) %collective-permute-start.8) | collective-permute-done | bytes 196640 | tf_op jit(solution)/shard_map/ppermute | solution.py:38
  (59 shorter events, 18.2 us)
Async XLA Ops:
  0.0 75.6 %copy-start = (bf16[512,512]{1,0:T(8,128)(2,1)S(1)}, bf16[512,512]{1,0:T(8,128)(2,1)}, u32[]{:S(2)}) copy-start(bf16[512,512]{1,0:T(8,128)(2,1)} %param.12) | copy-start | bytes 1572868
  0.0 9.1 %copy-start.7 = (s32[22,1]{0,1:T(1,128)S(1)}, s32[22,1]{0,1:T(1,128)}, u32[]{:S(2)}) copy-start(s32[22,1]{0,1:T(1,128)} %param.16) | copy-start | bytes 268
  0.0 44.7 %copy-start.6 = (s32[22]{0:T(128)S(1)}, s32[22]{0:T(128)}, u32[]{:S(2)}) copy-start(s32[22]{0:T(128)} %param.17) | copy-start | bytes 268
  0.0 1.3 copy-start.2
  1.3 0.8 copy-start.3
  3.4 64.2 %collective-permute-start.2 = (bf16[16,272,128]{2,1,0:T(8,128)(2,1)}, bf16[16,272,128]{2,1,0:T(8,128)(2,1)S(1)}, u32[]{:S(2)}, u32[]{:S(2)}) collective-permute-start(bf16[16,272,128]{2,1,0:T(8,128)(2,1)} %shard_map.73.refs_0_), channel_id=1, source_target_pairs={{0,16},{16,0},{1,17},{17,1},{2,18},{18,2},{3,19},{19,3},{4,20},{20... | collective-permute-start | bytes 3342344 | tf_op jit(solution)/shard_map/ppermute | solution.py:229
  5.3 36.8 %collective-permute-start.3 = (bf16[16,272,128]{2,1,0:T(8,128)(2,1)}, bf16[16,272,128]{2,1,0:T(8,128)(2,1)S(1)}, u32[]{:S(2)}, u32[]{:S(2)}) collective-permute-start(bf16[16,272,128]{2,1,0:T(8,128)(2,1)} %shard_map.73.refs_0_), channel_id=1, source_target_pairs={{0,32},{32,64},{64,96},{96,128},{128,160},{160,192},{192,224},{224... | collective-permute-start | bytes 3342344 | tf_op jit(solution)/shard_map/ppermute | solution.py:228
  42.1 25.4 %collective-permute-start.4 = (bf16[16,272,128]{2,1,0:T(8,128)(2,1)S(1)}, bf16[16,272,128]{2,1,0:T(8,128)(2,1)}, u32[]{:S(2)}, u32[]{:S(2)}) collective-permute-start(bf16[16,272,128]{2,1,0:T(8,128)(2,1)S(1)} %collective-permute-done.3.refs_2_), channel_id=1, source_target_pairs={{0,16},{16,0},{1,17},{17,1},{2,18},{18,2},{3,19},{19,3},{4,20},{20... | collective-permute-start | bytes 3342344 | tf_op jit(solution)/shard_map/ppermute | solution.py:238
  44.7 27.1 %copy-start.10 = (s32[22]{0:T(128)}, s32[22]{0:T(128)S(1)}, u32[]{:S(2)}) copy-start(s32[22]{0:T(128)S(1)} %get-tuple-element.234) | copy-start | bytes 268
  71.8 104.5 %all-to-all-start.1 = ((bf16[16,2,272,128]{3,2,1,0:T(8,128)(2,1)}), bf16[16,2,272,128]{3,2,1,0:T(8,128)(2,1)S(1)}, u32[]{:S(2)}, u32[]{:S(2)}) async-start(bf16[16,2,272,128]{3,2,1,0:T(8,128)(2,1)} %bitcast.10), calls=%async_computation.1 | async-start | bytes 4456448 | tf_op jit(solution)/shard_map/all_to_all | solution.py:243
  79.3 1.7 copy-start.5
  80.9 12.1 %copy-start.9 = (s32[1,22]{1,0:T(1,128)S(1)}, s32[1,22]{1,0:T(1,128)}, u32[]{:S(2)}) copy-start(s32[1,22]{1,0:T(1,128)} %param.15) | copy-start | bytes 268
  82.4 21.5 %collective-permute-start.7 = (bf16[768,512]{1,0:T(8,128)(2,1)}, bf16[768,512]{1,0:T(8,128)(2,1)S(1)}, u32[]{:S(2)}, u32[]{:S(2)}) collective-permute-start(bf16[768,512]{1,0:T(8,128)(2,1)} %get-tuple-element.226), channel_id=1, source_target_pairs={{0,12},{4,0},{8,4},{12,8},{1,13},{5,1},{9,5},{13,9},{2,14},{6,2},{... | collective-permute-start | bytes 2359304 | tf_op jit(solution)/shard_map/ppermute | solution.py:38
  84.8 35.8 %collective-permute-start.6 = (bf16[768,512]{1,0:T(8,128)(2,1)}, bf16[768,512]{1,0:T(8,128)(2,1)}, u32[]{:S(2)}, u32[]{:S(2)}) collective-permute-start(bf16[768,512]{1,0:T(8,128)(2,1)} %get-tuple-element.227), channel_id=1, source_target_pairs={{0,8},{4,12},{8,0},{12,4},{1,9},{5,13},{9,1},{13,5},{2,10},{6,14},... | collective-permute-start | bytes 2359304 | tf_op jit(solution)/shard_map/ppermute | solution.py:38
  89.3 34.1 %collective-permute-start.5 = (bf16[768,512]{1,0:T(8,128)(2,1)}, bf16[768,512]{1,0:T(8,128)(2,1)}, u32[]{:S(2)}, u32[]{:S(2)}) collective-permute-start(bf16[768,512]{1,0:T(8,128)(2,1)} %get-tuple-element.225), channel_id=1, source_target_pairs={{0,4},{4,8},{8,12},{12,0},{1,5},{5,9},{9,13},{13,1},{2,6},{6,10},{... | collective-permute-start | bytes 2359304 | tf_op jit(solution)/shard_map/ppermute | solution.py:38
  97.8 3.1 %collective-permute-start.1 = (s32[8,128]{1,0:T(8,128)S(1)}, s32[8,128]{1,0:T(8,128)S(1)}, u32[]{:S(2)}, u32[]{:S(2)}) collective-permute-start(s32[8,128]{1,0:T(8,128)S(1)} %broadcast_in_dim.106), channel_id=1, source_target_pairs={{0,16},{16,0},{1,17},{17,1},{2,18},{18,2},{3,19},{19,3},{4,20},{20... | collective-permute-start | bytes 12296 | tf_op jit(solution)/shard_map/ppermute | solution.py:250
  103.3 23.0 %copy-start.8 = (s32[22,1]{0,1:T(1,128)S(1)}, s32[22,1]{0,1:T(1,128)}, u32[]{:S(2)}) copy-start(s32[22,1]{0,1:T(1,128)} %param.16) | copy-start | bytes 268
  176.3 1.9 copy-start.1
  178.2 9.8 %copy-start.4 = (bf16[768,512]{1,0:T(8,128)(2,1)S(1)}, bf16[768,512]{1,0:T(8,128)(2,1)}, u32[]{:S(2)}) copy-start(bf16[768,512]{1,0:T(8,128)(2,1)} %fusion.3) | copy-start | bytes 2359300
  180.6 23.7 %all-to-all-start.2 = ((bf16[16,128,128]{2,1,0:T(8,128)(2,1)}), bf16[16,128,128]{2,1,0:T(8,128)(2,1)S(1)}, u32[]{:S(2)}, u32[]{:S(2)}) async-start(bf16[16,128,128]{2,1,0:T(8,128)(2,1)} %shard_map.75), calls=%async_computation.2 | async-start | bytes 1048576 | tf_op jit(solution)/shard_map/all_to_all | solution.py:267
  188.0 10.2 %collective-permute-start.10 = (bf16[192,512]{1,0:T(8,128)(2,1)S(1)}, bf16[192,512]{1,0:T(8,128)(2,1)S(1)}, u32[]{:S(2)}, u32[]{:S(2)}) collective-permute-start(bf16[192,512]{1,0:T(8,128)(2,1)S(1)} %get-tuple-element.229), channel_id=1, source_target_pairs={{0,3},{1,0},{2,1},{3,2},{4,7},{5,4},{6,5},{7,6},{8,11},{9,8},{10,9... | collective-permute-start | bytes 589832 | tf_op jit(solution)/shard_map/ppermute | solution.py:38
  192.6 9.2 %collective-permute-start.9 = (bf16[192,512]{1,0:T(8,128)(2,1)S(1)}, bf16[192,512]{1,0:T(8,128)(2,1)S(1)}, u32[]{:S(2)}, u32[]{:S(2)}) collective-permute-start(bf16[192,512]{1,0:T(8,128)(2,1)S(1)} %get-tuple-element.230), channel_id=1, source_target_pairs={{0,2},{1,3},{2,0},{3,1},{4,6},{5,7},{6,4},{7,5},{8,10},{9,11},{10,... | collective-permute-start | bytes 589832 | tf_op jit(solution)/shard_map/ppermute | solution.py:38
  195.4 8.8 %collective-permute-start.8 = (bf16[192,512]{1,0:T(8,128)(2,1)S(1)}, bf16[192,512]{1,0:T(8,128)(2,1)S(1)}, u32[]{:S(2)}, u32[]{:S(2)}) collective-permute-start(bf16[192,512]{1,0:T(8,128)(2,1)S(1)} %get-tuple-element.228), channel_id=1, source_target_pairs={{0,1},{1,2},{2,3},{3,0},{4,5},{5,6},{6,7},{7,4},{8,9},{9,10},{10,1... | collective-permute-start | bytes 589832 | tf_op jit(solution)/shard_map/ppermute | solution.py:38

commit v3 on v2

--- a/solution.py
+++ b/solution.py
@@ -21,8 +21,8 @@
 I32 = jnp.int32
 
 
-def params():
-    return pltpu.CompilerParams(vmem_limit_bytes=16 << 20)
+def params(mib=16):
+    return pltpu.CompilerParams(vmem_limit_bytes=mib << 20)
 
 
 def summed_rows(terms, axes):
@@ -53,13 +53,16 @@
     out_ref[:, cols * rank :, :] = up_ref[...]
 
 
-def pack(down, up):
+def rows_of(up):
+    held, mine, kv = up.shape
+    ucols = kv // LANES
+    return up.reshape(held, mine, ucols, LANES).transpose(0, 2, 1, 3).reshape(held, mine * ucols, LANES)
+
+
+def pack(down, up_rows):
     held, rank, feats = down.shape
     cols = feats // LANES
-    mine = up.shape[1]
-    ucols = up.shape[2] // LANES
-    up_rows = up.reshape(held, mine, ucols, LANES).transpose(0, 2, 1, 3).reshape(held, mine * ucols, LANES)
-    rows = cols * rank + mine * ucols
+    rows = cols * rank + up_rows.shape[1]
     return pl.pallas_call(
         functools.partial(pack_kernel, cols, rank),
         out_shape=jax.ShapeDtypeStruct((held, rows, LANES), BF16),
@@ -92,31 +95,53 @@
 
 
 def select_kernel(asked_ref, *refs):
-    tables, out_ref = refs[:-1], refs[-1]
-    held = tables[0].shape[0]
+    tables = list(zip(refs[0:8:2], refs[1:8:2], strict=True))
+    out_ref, buf, sem = refs[8:]
+    held, rank, feats = tables[0][0].shape
+    cols = feats // LANES
+    count = out_ref.shape[0]
+    group = count // sem.shape[0]
 
     def one(i, carry):
         want = asked_ref[i]
         which = want // held
         row = want - which * held
-        for k, table in enumerate(tables):
+        for k, (down_ref, up_ref) in enumerate(tables):
 
             @pl.when(which == k)
             def _():
-                out_ref[i] = table[row]
+                for c in range(cols):
+                    buf[i, c * rank : (c + 1) * rank, :] = down_ref[row, :, c * LANES : (c + 1) * LANES]
+                buf[i, cols * rank :, :] = up_ref[row]
 
         return carry
 
-    lax.fori_loop(0, out_ref.shape[0], one, 0)
-
-
-def select(asked, tables):
-    _, rows, lanes = tables[0].shape
+    def some(g, carry):
+        lax.fori_loop(g * group, (g + 1) * group, one, 0)
+        part = pl.ds(g * group, group)
+        pltpu.make_async_copy(buf.at[part], out_ref.at[part], sem.at[g]).start()
+        return carry
+
+    def end(g, carry):
+        part = pl.ds(g * group, group)
+        pltpu.make_async_copy(buf.at[part], out_ref.at[part], sem.at[g]).wait()
+        return carry
+
+    lax.fori_loop(0, sem.shape[0], some, 0)
+    lax.fori_loop(0, sem.shape[0], end, 0)
+
+
+def select(asked, *tables):
+    _, rank, feats = tables[0].shape
+    lanes = tables[1].shape[2]
+    rows = rank * (feats // lanes) + tables[1].shape[1]
+    count = asked.shape[0]
     return pl.pallas_call(
         select_kernel,
-        out_shape=jax.ShapeDtypeStruct((asked.shape[0], rows, lanes), BF16),
+        out_shape=jax.ShapeDtypeStruct((count, rows, lanes), BF16),
         in_specs=[SMEM] + [VMEM] * len(tables),
-        out_specs=VMEM,
+        out_specs=ANY,
+        scratch_shapes=[pltpu.VMEM((count, rows, lanes), BF16), pltpu.SemaphoreType.DMA((8,))],
         compiler_params=params(),
     )(asked, *tables)
 
@@ -137,19 +162,25 @@
     return jnp.pad(kept, ((0, places - count), (0, 0), (0, 0)))
 
 
-def shrink_kernel(cols, rank, half, at_ref, tok_ref, got_ref, out_ref):
-    blocks = tok_ref.shape[0] // BLOCK
+def shrink_kernel(cols, rank, half, at_ref, tok_ref, got_ref, out_ref, tok, sem):
+    blocks = tok.shape[0] // BLOCK
     ups = got_ref.shape[1] - cols * rank
     per = 3
+    size = per * BLOCK
     for u in range(blocks // per):
+        part = pl.ds(u * size, size)
+        pltpu.make_async_copy(tok_ref.at[part], tok.at[part], sem.at[u]).start()
+    for u in range(blocks // per):
+        part = pl.ds(u * size, size)
+        pltpu.make_async_copy(tok_ref.at[part], tok.at[part], sem.at[u]).wait()
         parts = []
         for b in range(u * per, (u + 1) * per):
             place = at_ref[b]
             down = jnp.concatenate([got_ref[place, c * rank : (c + 1) * rank, :] for c in range(cols)], axis=1)
-            part = lax.dot_general(
-                tok_ref[b * BLOCK : (b + 1) * BLOCK, :], down, (((1,), (1,)), ((), ())), preferred_element_type=F32
+            term = lax.dot_general(
+                tok[b * BLOCK : (b + 1) * BLOCK, :], down, (((1,), (1,)), ((), ())), preferred_element_type=F32
             )
-            parts.append(part)
+            parts.append(term)
         whole = jnp.concatenate(parts, axis=0)
         for k in range(2):
             t = 2 * u + k
@@ -166,12 +197,14 @@
     _, rows, lanes = got.shape
     half = tok_rows // tensors // 2
     ups = rows - cols * rank
+    blocks = tok_rows // BLOCK
     return pl.pallas_call(
         functools.partial(shrink_kernel, cols, rank, half),
         out_shape=jax.ShapeDtypeStruct((tensors, half + 2 * ups, lanes), BF16),
-        in_specs=[SMEM, VMEM, VMEM],
+        in_specs=[SMEM, ANY, VMEM],
         out_specs=VMEM,
-        compiler_params=params(),
+        scratch_shapes=[pltpu.VMEM((tok_rows, feats), BF16), pltpu.SemaphoreType.DMA((blocks // 3,))],
+        compiler_params=params(59),
     )(at, tokens, got)
 
 
@@ -224,20 +257,26 @@
     core = lax.axis_index("core")
     owners, slots = segment_owner[:, 0], segment_slot
 
-    own = pack(adapter_down, adapter_up)
-    before = lax.ppermute(own, "z", shift(chips, 1))
-    other = lax.ppermute(own, "core", shift(cores, 1))
+    forward = shift(chips, 1)
+    before_down = lax.ppermute(adapter_down, "z", forward)
 
     place, asked, bad = plan(owners, slots, chips, cores, held, core)
     ask = jnp.concatenate([asked.reshape(chips, cores), jnp.full((chips, 1), bad, I32)], axis=1)
     ask = jnp.pad(ask, ((0, 0), (0, LANES - cores - 1)))[:, None, :]
-    ask = jnp.broadcast_to(ask, (chips, 8, LANES))
     told = lax.all_to_all(ask, "z", 0, 0, tiled=True)
     told = jnp.clip(told[:, 0, :], 0, 2 * cores * held)
 
-    other_before = lax.ppermute(before, "core", shift(cores, 1))
+    up_rows = rows_of(adapter_up)
+    across = shift(cores, 1)
+    before_up = lax.ppermute(up_rows, "z", forward)
+    other_down = lax.ppermute(adapter_down, "core", across)
+    other_up = lax.ppermute(up_rows, "core", across)
+    far_down = lax.ppermute(before_down, "core", across)
+    far_up = lax.ppermute(before_up, "core", across)
     wanted = told[:, :cores].reshape(-1)
-    rows = select(wanted, (own, other, before, other_before))
+    rows = select(
+        wanted, adapter_down, up_rows, other_down, other_up, before_down, before_up, far_down, far_up
+    )
     rows, base_weight = lax.optimization_barrier((rows, base_weight))
     sent = rows.reshape(chips, cores, *rows.shape[1:])
     got = lax.all_to_all(sent, "z", 0, 0, tiled=True)
@@ -245,14 +284,13 @@
 
     base = jnp.dot(tokens, base_weight, preferred_element_type=F32).astype(BF16)
     base = summed_rows(base, TENSOR)
-
     lane_bad = jnp.max(told[:, cores])
     far_bad = lax.ppermute(jnp.broadcast_to(lane_bad, (8, LANES)), "core", shift(cores, 1))[0, 0]
     any_bad = jnp.maximum(lane_bad, far_bad) > 0
     me = lax.axis_index(STORE)
     got = lax.cond(
         any_bad,
-        lambda g: go_round(own, owners, slots, chips * cores, chips * cores, me),
+        lambda g: go_round(pack(adapter_down, up_rows), owners, slots, chips * cores, chips * cores, me),
         lambda g: g,
         got,
     )

time: 207 us -> 205 us (level)
  the two profiles are of different devices: /device:TPU:8 before, /device:TPU:32 now
where the time goes in v3:
time: 205 us; the launch traced here: 204 us
  waiting for transfers between devices  105 us (51%)
  starting transfers between devices  64.8 us (32%)
  other arithmetic  12.8 us (6%)
  Pallas kernels  10.7 us (5%)
  local copies, waits for them, and re-layouts  5.42 us (3%)
  matrix products  3.69 us (2%)
    all_to_all x1, waiting for transfers between devices, device_part(): got = lax.all_to_all(sent, 'z', 0, 0, tiled=True)  44.9 us
    ppermute x6, waiting for transfers between devices, summed_rows(): lax.ppermute(piece(d), axis, shift(count, d))  30.9 us
    ppermute x1, waiting for transfers between devices, device_part(): before_down = lax.ppermute(adapter_down, 'z', forward)  21.8 us
    ppermute x6, starting transfers between devices, summed_rows(): lax.ppermute(piece(d), axis, shift(count, d))  20.9 us
    all_to_all x1, starting transfers between devices, device_part(): told = lax.all_to_all(ask, 'z', 0, 0, tiled=True)  13 us
    all_to_all x1, starting transfers between devices, device_part(): got_low = lax.all_to_all(message, TENSOR, 0, 0, tiled=True)  7.04 us
    all_to_all x1, waiting for transfers between devices, device_part(): told = lax.all_to_all(ask, 'z', 0, 0, tiled=True)  6.73 us
    all_to_all x1, starting transfers between devices, device_part(): got = lax.all_to_all(sent, 'z', 0, 0, tiled=True)  6.05 us
  transfers between devices with their start and end apart: 16, of which 9 were waited for; matrix products, arithmetic and copies ran while one was open for 10% of the time, Pallas kernels for 0%

profile of v3, /device:TPU:32, one launch (start us, length us, event | category | flops | bytes accessed | tf_op | source)
XLA Modules:
  0.0 203.9 jit_solution(18272892008541767721)
XLA Ops:
  2.1 3.8 %collective-permute-start.4 = (bf16[16,64,512]{2,1,0:T(8,128)(2,1)}, bf16[16,64,512]{2,1,0:T(8,128)(2,1)S(1)}, u32[]{:S(2)}, u32[]{:S(2)}) collective-permute-start(bf16[16,64,512]{2,1,0:T(8,128)(2,1)} %refs_0_.1), channel_id=1, source_target_pairs={{0,32},{32,64},{64,96},{96,128},{128,160},{160,192},{192,224},{224... | collective-permute-start | bytes 3145736 | tf_op jit(solution)/shard_map/ppermute | solution.py:261
  5.9 3.8 %collective-permute-start.5 = (bf16[16,16,128]{2,1,0:T(8,128)(2,1)}, bf16[16,16,128]{2,1,0:T(8,128)(2,1)S(1)}, u32[]{:S(2)}, u32[]{:S(2)}) collective-permute-start(bf16[16,16,128]{2,1,0:T(8,128)(2,1)} %bitcast.51), channel_id=1, source_target_pairs={{0,32},{32,64},{64,96},{96,128},{128,160},{160,192},{192,224},{224... | collective-permute-start | bytes 196616 | tf_op jit(solution)/shard_map/ppermute | solution.py:271
  11.9 21.8 %collective-permute-done.4.refs_4_ = bf16[16,64,512]{2,1,0:T(8,128)(2,1)S(1)} collective-permute-done((bf16[16,64,512]{2,1,0:T(8,128)(2,1)}, bf16[16,64,512]{2,1,0:T(8,128)(2,1)S(1)}, u32[]{:S(2)}, u32[]{:S(2)}) %collective-permute-start.4) | collective-permute-done | bytes 1048608 | tf_op jit(solution)/shard_map/ppermute | solution.py:261
  38.6 13.0 %all-to-all-start = ((s32[16,1,128]{2,1,0:T(1,128)}), s32[16,1,128]{2,1,0:T(1,128)S(1)}, u32[]{:S(2)}, u32[]{:S(2)}) async-start(s32[16,1,128]{2,1,0:T(1,128)} %bitcast.6), calls=%async_computation | async-start | bytes 16384 | tf_op jit(solution)/shard_map/all_to_all | solution.py:266
  53.5 2.4 %collective-permute-start.7 = (bf16[16,16,128]{2,1,0:T(8,128)(2,1)S(1)}, bf16[16,16,128]{2,1,0:T(8,128)(2,1)S(1)}, u32[]{:S(2)}, u32[]{:S(2)}) collective-permute-start(bf16[16,16,128]{2,1,0:T(8,128)(2,1)S(1)} %collective-permute-done.5.refs_5_), channel_id=1, source_target_pairs={{0,16},{16,0},{1,17},{17,1},{2,18},{18,2},{3,19},{19,3},{4,20},{20... | collective-permute-start | bytes 196616 | tf_op jit(solution)/shard_map/ppermute | solution.py:275
  55.9 6.7 %all-to-all-done = s32[16,1,128]{2,1,0:T(1,128)S(1)} async-done(((s32[16,1,128]{2,1,0:T(1,128)}), s32[16,1,128]{2,1,0:T(1,128)S(1)}, u32[]{:S(2)}, u32[]{:S(2)}) %all-to-all-start) | async-done | bytes 8224 | tf_op jit(solution)/shard_map/all_to_all | solution.py:266
  62.8 3.9 %shard_map.73 = bf16[32,272,128]{2,1,0:T(8,128)(2,1)} custom-call(s32[32]{0:T(128)S(1)} %reshape.258.asked_ref, bf16[16,64,512]{2,1,0:T(8,128)(2,1)} %refs_0_.1, bf16[16,16,128]{2,1,0:T(8,128)(2,1)} %bitcast.53, bf16[16,64,512]{2,1,0:T(8,128)(2,1)S(1)} %collective-permute-done.2.refs_2_, bf16[16,16,128]{2,1,0:T(8,128)(2,1)S(1)} %collective-permute-done.3.refs_3_, ...), custom_call_target="tpu_custom_call" | custom-call | tf_op jit(solution)/shard_map/pallas_call | solution.py:139
  66.6 6.1 %all-to-all-start.1 = ((bf16[16,2,272,128]{3,2,1,0:T(8,128)(2,1)}), bf16[16,2,272,128]{3,2,1,0:T(8,128)(2,1)S(1)}, u32[]{:S(2)}, u32[]{:S(2)}) async-start(bf16[16,2,272,128]{3,2,1,0:T(8,128)(2,1)} %bitcast.14), calls=%async_computation.1 | async-start | bytes 4456448 | tf_op jit(solution)/shard_map/all_to_all | solution.py:282
  72.7 3.7 %convolution_convert_fusion = bf16[512,3072]{0,1:T(8,128)(2,1)S(1)} fusion(bf16[3072,512]{1,0:T(8,128)(2,1)} %tok_ref.1, bf16[512,512]{1,0:T(8,128)(2,1)S(1)} %copy-done), kind=kOutput, calls=%fused_computation.8 | convolution fusion | flops 1612185600 | bytes 6815744 | tf_op jit(solution)/shard_map/dot_general | solution.py:285
  79.6 4.9 %collective-permute-start.10 = (bf16[768,512]{1,0:T(8,128)(2,1)}, bf16[768,512]{1,0:T(8,128)(2,1)S(1)}, u32[]{:S(2)}, u32[]{:S(2)}) collective-permute-start(bf16[768,512]{1,0:T(8,128)(2,1)} %get-tuple-element.227), channel_id=1, source_target_pairs={{0,12},{4,0},{8,4},{12,8},{1,13},{5,1},{9,5},{13,9},{2,14},{6,2},{... | collective-permute-start | bytes 2359304 | tf_op jit(solution)/shard_map/ppermute | solution.py:38
  84.5 2.5 %collective-permute-start.9 = (bf16[768,512]{1,0:T(8,128)(2,1)}, bf16[768,512]{1,0:T(8,128)(2,1)}, u32[]{:S(2)}, u32[]{:S(2)}) collective-permute-start(bf16[768,512]{1,0:T(8,128)(2,1)} %get-tuple-element.228), channel_id=1, source_target_pairs={{0,8},{4,12},{8,0},{12,4},{1,9},{5,13},{9,1},{13,5},{2,10},{6,14},... | collective-permute-start | bytes 2359304 | tf_op jit(solution)/shard_map/ppermute | solution.py:38
  87.0 2.9 %collective-permute-start.8 = (bf16[768,512]{1,0:T(8,128)(2,1)}, bf16[768,512]{1,0:T(8,128)(2,1)}, u32[]{:S(2)}, u32[]{:S(2)}) collective-permute-start(bf16[768,512]{1,0:T(8,128)(2,1)} %get-tuple-element.226), channel_id=1, source_target_pairs={{0,4},{4,8},{8,12},{12,0},{1,5},{5,9},{9,13},{13,1},{2,6},{6,10},{... | collective-permute-start | bytes 2359304 | tf_op jit(solution)/shard_map/ppermute | solution.py:38
  100.3 18.1 %collective-permute-done.10 = bf16[768,512]{1,0:T(8,128)(2,1)S(1)} collective-permute-done((bf16[768,512]{1,0:T(8,128)(2,1)}, bf16[768,512]{1,0:T(8,128)(2,1)S(1)}, u32[]{:S(2)}, u32[]{:S(2)}) %collective-permute-start.10) | collective-permute-done | bytes 786464 | tf_op jit(solution)/shard_map/ppermute | solution.py:38
  118.4 5.6 %collective-permute-done.8 = bf16[768,512]{1,0:T(8,128)(2,1)} collective-permute-done((bf16[768,512]{1,0:T(8,128)(2,1)}, bf16[768,512]{1,0:T(8,128)(2,1)}, u32[]{:S(2)}, u32[]{:S(2)}) %collective-permute-start.8) | collective-permute-done | bytes 786464 | tf_op jit(solution)/shard_map/ppermute | solution.py:38
  124.0 2.9 %fusion.3 = bf16[768,512]{1,0:T(8,128)(2,1)} fusion(bf16[768,512]{1,0:T(8,128)(2,1)S(1)} %collective-permute-done.10, bf16[768,512]{1,0:T(8,128)(2,1)} %collective-permute-done.9, bf16[768,512]{1,0:T(8,128)(2,1)} %collective-permute-done.8, bf16[512,3072]{0,1:T(8,128)(2,1)} %copy-done.2, s32[]{:T(128)S(6)} %select_n.231), kind=kLoop, calls=%fused_computation.12 | loop fusion | flops 3145728 | bytes 3932164 | tf_op jit(solution)/shard_map/convert_element_type | solution.py:42
  127.0 44.9 %all-to-all-done.1 = bf16[16,2,272,128]{3,2,1,0:T(8,128)(2,1)S(1)} async-done(((bf16[16,2,272,128]{3,2,1,0:T(8,128)(2,1)}), bf16[16,2,272,128]{3,2,1,0:T(8,128)(2,1)S(1)}, u32[]{:S(2)}, u32[]{:S(2)}) %all-to-all-start.1) | async-done | bytes 2228256 | tf_op jit(solution)/shard_map/all_to_all | solution.py:282
  171.8 5.5 %shard_map.74 = bf16[16,128,128]{2,1,0:T(8,128)(2,1)} custom-call(s32[24]{0:T(128)} %select_reduce_fusion.at_ref, bf16[3072,512]{1,0:T(8,128)(2,1)} %tok_ref.1, bf16[32,272,128]{2,1,0:T(8,128)(2,1)S(1)} %get-tuple-element.307.got_ref), custom_call_target="tpu_custom_call" | custom-call | tf_op jit(solution)/shard_map/pallas_call | solution.py:201
  177.4 7.0 %all-to-all-start.2 = ((bf16[16,128,128]{2,1,0:T(8,128)(2,1)}), bf16[16,128,128]{2,1,0:T(8,128)(2,1)S(1)}, u32[]{:S(2)}, u32[]{:S(2)}) async-start(bf16[16,128,128]{2,1,0:T(8,128)(2,1)} %shard_map.74), calls=%async_computation.2 | async-start | bytes 1048576 | tf_op jit(solution)/shard_map/all_to_all | solution.py:305
  184.5 5.0 %collective-permute-start.13 = (bf16[192,512]{1,0:T(8,128)(2,1)S(1)}, bf16[192,512]{1,0:T(8,128)(2,1)S(1)}, u32[]{:S(2)}, u32[]{:S(2)}) collective-permute-start(bf16[192,512]{1,0:T(8,128)(2,1)S(1)} %get-tuple-element.230), channel_id=1, source_target_pairs={{0,3},{1,0},{2,1},{3,2},{4,7},{5,4},{6,5},{7,6},{8,11},{9,8},{10,9... | collective-permute-start | bytes 589832 | tf_op jit(solution)/shard_map/ppermute | solution.py:38
  189.5 2.8 %collective-permute-start.12 = (bf16[192,512]{1,0:T(8,128)(2,1)S(1)}, bf16[192,512]{1,0:T(8,128)(2,1)S(1)}, u32[]{:S(2)}, u32[]{:S(2)}) collective-permute-start(bf16[192,512]{1,0:T(8,128)(2,1)S(1)} %get-tuple-element.231), channel_id=1, source_target_pairs={{0,2},{1,3},{2,0},{3,1},{4,6},{5,7},{6,4},{7,5},{8,10},{9,11},{10,... | collective-permute-start | bytes 589832 | tf_op jit(solution)/shard_map/ppermute | solution.py:38
  192.3 2.8 %collective-permute-start.11 = (bf16[192,512]{1,0:T(8,128)(2,1)S(1)}, bf16[192,512]{1,0:T(8,128)(2,1)S(1)}, u32[]{:S(2)}, u32[]{:S(2)}) collective-permute-start(bf16[192,512]{1,0:T(8,128)(2,1)S(1)} %get-tuple-element.229), channel_id=1, source_target_pairs={{0,1},{1,2},{2,3},{3,0},{4,5},{5,6},{6,7},{7,4},{8,9},{9,10},{10,1... | collective-permute-start | bytes 589832 | tf_op jit(solution)/shard_map/ppermute | solution.py:38
  195.1 2.8 %collective-permute-done.13 = bf16[192,512]{1,0:T(8,128)(2,1)S(1)} collective-permute-done((bf16[192,512]{1,0:T(8,128)(2,1)S(1)}, bf16[192,512]{1,0:T(8,128)(2,1)S(1)}, u32[]{:S(2)}, u32[]{:S(2)}) %collective-permute-start.13) | collective-permute-done | bytes 196640 | tf_op jit(solution)/shard_map/ppermute | solution.py:38
  197.9 2.4 %collective-permute-done.12 = bf16[192,512]{1,0:T(8,128)(2,1)S(1)} collective-permute-done((bf16[192,512]{1,0:T(8,128)(2,1)S(1)}, bf16[192,512]{1,0:T(8,128)(2,1)S(1)}, u32[]{:S(2)}, u32[]{:S(2)}) %collective-permute-start.12) | collective-permute-done | bytes 196640 | tf_op jit(solution)/shard_map/ppermute | solution.py:38
  200.3 2.1 %collective-permute-done.11 = bf16[192,512]{1,0:T(8,128)(2,1)S(1)} collective-permute-done((bf16[192,512]{1,0:T(8,128)(2,1)S(1)}, bf16[192,512]{1,0:T(8,128)(2,1)S(1)}, u32[]{:S(2)}, u32[]{:S(2)}) %collective-permute-start.11) | collective-permute-done | bytes 196640 | tf_op jit(solution)/shard_map/ppermute | solution.py:38
  (54 shorter events, 24.9 us)
Async XLA Ops:
  0.0 72.7 %copy-start = (bf16[512,512]{1,0:T(8,128)(2,1)S(1)}, bf16[512,512]{1,0:T(8,128)(2,1)}, u32[]{:S(2)}) copy-start(bf16[512,512]{1,0:T(8,128)(2,1)} %param.12) | copy-start | bytes 1572868
  0.0 62.7 %collective-permute-start.2 = (bf16[16,64,512]{2,1,0:T(8,128)(2,1)}, bf16[16,64,512]{2,1,0:T(8,128)(2,1)S(1)}, u32[]{:S(2)}, u32[]{:S(2)}) collective-permute-start(bf16[16,64,512]{2,1,0:T(8,128)(2,1)} %refs_0_.1), channel_id=1, source_target_pairs={{0,16},{16,0},{1,17},{17,1},{2,18},{18,2},{3,19},{19,3},{4,20},{20... | collective-permute-start | bytes 3145736 | tf_op jit(solution)/shard_map/ppermute | solution.py:272
  2.1 31.6 %collective-permute-start.4 = (bf16[16,64,512]{2,1,0:T(8,128)(2,1)}, bf16[16,64,512]{2,1,0:T(8,128)(2,1)S(1)}, u32[]{:S(2)}, u32[]{:S(2)}) collective-permute-start(bf16[16,64,512]{2,1,0:T(8,128)(2,1)} %refs_0_.1), channel_id=1, source_target_pairs={{0,32},{32,64},{64,96},{96,128},{128,160},{160,192},{192,224},{224... | collective-permute-start | bytes 3145736 | tf_op jit(solution)/shard_map/ppermute | solution.py:261
  5.9 47.6 %collective-permute-start.5 = (bf16[16,16,128]{2,1,0:T(8,128)(2,1)}, bf16[16,16,128]{2,1,0:T(8,128)(2,1)S(1)}, u32[]{:S(2)}, u32[]{:S(2)}) collective-permute-start(bf16[16,16,128]{2,1,0:T(8,128)(2,1)} %bitcast.51), channel_id=1, source_target_pairs={{0,32},{32,64},{64,96},{96,128},{128,160},{160,192},{192,224},{224... | collective-permute-start | bytes 196616 | tf_op jit(solution)/shard_map/ppermute | solution.py:271
  33.6 29.1 %collective-permute-start.6 = (bf16[16,64,512]{2,1,0:T(8,128)(2,1)S(1)}, bf16[16,64,512]{2,1,0:T(8,128)(2,1)}, u32[]{:S(2)}, u32[]{:S(2)}) collective-permute-start(bf16[16,64,512]{2,1,0:T(8,128)(2,1)S(1)} %collective-permute-done.4.refs_4_), channel_id=1, source_target_pairs={{0,16},{16,0},{1,17},{17,1},{2,18},{18,2},{3,19},{19,3},{4,20},{20... | collective-permute-start | bytes 3145736 | tf_op jit(solution)/shard_map/ppermute | solution.py:274
  38.6 24.1 %all-to-all-start = ((s32[16,1,128]{2,1,0:T(1,128)}), s32[16,1,128]{2,1,0:T(1,128)S(1)}, u32[]{:S(2)}, u32[]{:S(2)}) async-start(s32[16,1,128]{2,1,0:T(1,128)} %bitcast.6), calls=%async_computation | async-start | bytes 16384 | tf_op jit(solution)/shard_map/all_to_all | solution.py:266
  51.5 11.2 %collective-permute-start.3 = (bf16[16,16,128]{2,1,0:T(8,128)(2,1)}, bf16[16,16,128]{2,1,0:T(8,128)(2,1)S(1)}, u32[]{:S(2)}, u32[]{:S(2)}) collective-permute-start(bf16[16,16,128]{2,1,0:T(8,128)(2,1)} %bitcast.52), channel_id=1, source_target_pairs={{0,16},{16,0},{1,17},{17,1},{2,18},{18,2},{3,19},{19,3},{4,20},{20... | collective-permute-start | bytes 196616 | tf_op jit(solution)/shard_map/ppermute | solution.py:273
  53.5 9.3 %collective-permute-start.7 = (bf16[16,16,128]{2,1,0:T(8,128)(2,1)S(1)}, bf16[16,16,128]{2,1,0:T(8,128)(2,1)S(1)}, u32[]{:S(2)}, u32[]{:S(2)}) collective-permute-start(bf16[16,16,128]{2,1,0:T(8,128)(2,1)S(1)} %collective-permute-done.5.refs_5_), channel_id=1, source_target_pairs={{0,16},{16,0},{1,17},{17,1},{2,18},{18,2},{3,19},{19,3},{4,20},{20... | collective-permute-start | bytes 196616 | tf_op jit(solution)/shard_map/ppermute | solution.py:275
  66.6 105.2 %all-to-all-start.1 = ((bf16[16,2,272,128]{3,2,1,0:T(8,128)(2,1)}), bf16[16,2,272,128]{3,2,1,0:T(8,128)(2,1)S(1)}, u32[]{:S(2)}, u32[]{:S(2)}) async-start(bf16[16,2,272,128]{3,2,1,0:T(8,128)(2,1)} %bitcast.14), calls=%async_computation.1 | async-start | bytes 4456448 | tf_op jit(solution)/shard_map/all_to_all | solution.py:282
  76.4 1.7 copy-start.2
  78.0 11.9 %copy-start.5 = (s32[1,22]{1,0:T(1,128)S(1)}, s32[1,22]{1,0:T(1,128)}, u32[]{:S(2)}) copy-start(s32[1,22]{1,0:T(1,128)} %param.15) | copy-start | bytes 268
  79.6 38.8 %collective-permute-start.10 = (bf16[768,512]{1,0:T(8,128)(2,1)}, bf16[768,512]{1,0:T(8,128)(2,1)S(1)}, u32[]{:S(2)}, u32[]{:S(2)}) collective-permute-start(bf16[768,512]{1,0:T(8,128)(2,1)} %get-tuple-element.227), channel_id=1, source_target_pairs={{0,12},{4,0},{8,4},{12,8},{1,13},{5,1},{9,5},{13,9},{2,14},{6,2},{... | collective-permute-start | bytes 2359304 | tf_op jit(solution)/shard_map/ppermute | solution.py:38
  84.5 33.9 %collective-permute-start.9 = (bf16[768,512]{1,0:T(8,128)(2,1)}, bf16[768,512]{1,0:T(8,128)(2,1)}, u32[]{:S(2)}, u32[]{:S(2)}) collective-permute-start(bf16[768,512]{1,0:T(8,128)(2,1)} %get-tuple-element.228), channel_id=1, source_target_pairs={{0,8},{4,12},{8,0},{12,4},{1,9},{5,13},{9,1},{13,5},{2,10},{6,14},... | collective-permute-start | bytes 2359304 | tf_op jit(solution)/shard_map/ppermute | solution.py:38
  87.0 37.0 %collective-permute-start.8 = (bf16[768,512]{1,0:T(8,128)(2,1)}, bf16[768,512]{1,0:T(8,128)(2,1)}, u32[]{:S(2)}, u32[]{:S(2)}) collective-permute-start(bf16[768,512]{1,0:T(8,128)(2,1)} %get-tuple-element.226), channel_id=1, source_target_pairs={{0,4},{4,8},{8,12},{12,0},{1,5},{5,9},{9,13},{13,1},{2,6},{6,10},{... | collective-permute-start | bytes 2359304 | tf_op jit(solution)/shard_map/ppermute | solution.py:38
  94.1 3.1 %collective-permute-start.1 = (s32[8,128]{1,0:T(8,128)S(1)}, s32[8,128]{1,0:T(8,128)S(1)}, u32[]{:S(2)}, u32[]{:S(2)}) collective-permute-start(s32[8,128]{1,0:T(8,128)S(1)} %broadcast_in_dim.103), channel_id=1, source_target_pairs={{0,16},{16,0},{1,17},{17,1},{2,18},{18,2},{3,19},{19,3},{4,20},{20... | collective-permute-start | bytes 12296 | tf_op jit(solution)/shard_map/ppermute | solution.py:288
  100.3 26.6 %copy-start.3 = (s32[22]{0:T(128)S(1)}, s32[22]{0:T(128)}, u32[]{:S(2)}) copy-start(s32[22]{0:T(128)} %param.17) | copy-start | bytes 268
  100.3 26.6 %copy-start.4 = (s32[22,1]{0,1:T(1,128)S(1)}, s32[22,1]{0,1:T(1,128)}, u32[]{:S(2)}) copy-start(s32[22,1]{0,1:T(1,128)} %param.16) | copy-start | bytes 268
  171.8 12.6 %copy-start.1 = (bf16[768,512]{1,0:T(8,128)(2,1)S(1)}, bf16[768,512]{1,0:T(8,128)(2,1)}, u32[]{:S(2)}) copy-start(bf16[768,512]{1,0:T(8,128)(2,1)} %fusion.3) | copy-start | bytes 2359300
  177.4 25.1 %all-to-all-start.2 = ((bf16[16,128,128]{2,1,0:T(8,128)(2,1)}), bf16[16,128,128]{2,1,0:T(8,128)(2,1)S(1)}, u32[]{:S(2)}, u32[]{:S(2)}) async-start(bf16[16,128,128]{2,1,0:T(8,128)(2,1)} %shard_map.74), calls=%async_computation.2 | async-start | bytes 1048576 | tf_op jit(solution)/shard_map/all_to_all | solution.py:305
  184.5 13.4 %collective-permute-start.13 = (bf16[192,512]{1,0:T(8,128)(2,1)S(1)}, bf16[192,512]{1,0:T(8,128)(2,1)S(1)}, u32[]{:S(2)}, u32[]{:S(2)}) collective-permute-start(bf16[192,512]{1,0:T(8,128)(2,1)S(1)} %get-tuple-element.230), channel_id=1, source_target_pairs={{0,3},{1,0},{2,1},{3,2},{4,7},{5,4},{6,5},{7,6},{8,11},{9,8},{10,9... | collective-permute-start | bytes 589832 | tf_op jit(solution)/shard_map/ppermute | solution.py:38
  189.5 10.8 %collective-permute-start.12 = (bf16[192,512]{1,0:T(8,128)(2,1)S(1)}, bf16[192,512]{1,0:T(8,128)(2,1)S(1)}, u32[]{:S(2)}, u32[]{:S(2)}) collective-permute-start(bf16[192,512]{1,0:T(8,128)(2,1)S(1)} %get-tuple-element.231), channel_id=1, source_target_pairs={{0,2},{1,3},{2,0},{3,1},{4,6},{5,7},{6,4},{7,5},{8,10},{9,11},{10,... | collective-permute-start | bytes 589832 | tf_op jit(solution)/shard_map/ppermute | solution.py:38
  192.3 10.1 %collective-permute-start.11 = (bf16[192,512]{1,0:T(8,128)(2,1)S(1)}, bf16[192,512]{1,0:T(8,128)(2,1)S(1)}, u32[]{:S(2)}, u32[]{:S(2)}) collective-permute-start(bf16[192,512]{1,0:T(8,128)(2,1)S(1)} %get-tuple-element.229), channel_id=1, source_target_pairs={{0,1},{1,2},{2,3},{3,0},{4,5},{5,6},{6,7},{7,4},{8,9},{9,10},{10,1... | collective-permute-start | bytes 589832 | tf_op jit(solution)/shard_map/ppermute | solution.py:38

commit v4 on v3

v4 whole, which is shorter than its diff:
```python
import functools

import jax
import jax.numpy as jnp
from jax import lax
from jax.experimental import pallas as pl
from jax.experimental.pallas import tpu as pltpu
from jax.sharding import Mesh
from jax.sharding import PartitionSpec as P

BLOCK = 128
LANES = 128
TENSOR = ("ty", "tx")
STORE = ("z", "core")
EVERY = ("z", "core", "ty", "tx")
VMEM = pl.BlockSpec(memory_space=pltpu.VMEM)
SMEM = pl.BlockSpec(memory_space=pltpu.SMEM)
ANY = pl.BlockSpec(memory_space=pl.ANY)
BF16 = jnp.bfloat16
F32 = jnp.float32
I32 = jnp.int32


def params(mib=16):
    return pltpu.CompilerParams(vmem_limit_bytes=mib << 20)


def summed_rows(terms, axes):
    running = terms
    for axis in axes:
        count = lax.axis_size(axis)
        me = lax.axis_index(axis)
        size = running.shape[0] // count

        def piece(d, x=running, me=me, count=count, size=size):
            return lax.dynamic_slice_in_dim(x, (me + d) % count * size, size, 0)

        came = [lax.ppermute(piece(d), axis, shift(count, d)) for d in range(1, count)]
        total = piece(0).astype(F32)
        for one in came:
            total = total + one.astype(F32)
        running = total.astype(BF16)
    return running


def shift(count, by):
    return [(i, (i + by) % count) for i in range(count)]


def rows_of(up):
    held, mine, kv = up.shape
    ucols = kv // LANES
    return up.reshape(held, mine, ucols, LANES).transpose(0, 2, 1, 3).reshape(held, mine * ucols, LANES)


def plan_kernel(chips, held, core_ref, owner_ref, slot_ref, ask_ref, place_ref):
    owner = owner_ref[...]
    slot = slot_ref[...]
    core = core_ref[0]
    count = owner.shape[0]
    chip = owner // 2
    lane = owner % 2
    z = lax.broadcasted_iota(I32, (count, LANES), 1)
    i = lax.broadcasted_iota(I32, (count, LANES), 0)
    here = chip == z % chips
    on_a = jnp.where(here & (lane == 0), 1.0, 0.0).astype(F32)
    on_b = jnp.where(here & (lane == 1), 1.0, 0.0).astype(F32)
    wide = (8, LANES)
    a = jnp.broadcast_to(jnp.sum(on_a, axis=0, keepdims=True), wide)
    b = jnp.broadcast_to(jnp.sum(on_b, axis=0, keepdims=True), wide)

    def ahead(x):
        return pltpu.roll(x, LANES - 1, 1)

    h, d = -ahead(b), a + b - 2.0
    step = 1
    while step < chips:
        h = jnp.maximum(h, pltpu.roll(h, step, 1) + d)
        d = d + pltpu.roll(d, step, 1)
        step *= 2
    h_back = pltpu.roll(h, 1, 1)
    bad = jnp.max(jnp.where(h > a, 1.0, 0.0), axis=(0, 1), keepdims=True)
    stay_a = a - jnp.maximum(h, 0.0)
    stay_b = b - jnp.maximum(-h_back, 0.0)
    stay = stay_a + stay_b
    move_a = ahead(stay)
    move_b = pltpu.roll(stay + jnp.maximum(h_back, 0.0), 1, 1)

    def pick(for_a, for_b):
        both = on_a * for_a[:1] + on_b * for_b[:1]
        return jnp.sum(jnp.where(z < chips, both, 0.0), axis=1, keepdims=True).astype(I32)

    zero = jnp.zeros_like(a)
    limit = pick(stay_a, stay_b)
    base = pick(zero, stay_a)
    base_moved = pick(move_a, move_b)
    base_plain = pick(zero, a)
    same = owner == z % (2 * chips)
    first = jnp.min(jnp.where(same, i, count).astype(F32), axis=0, keepdims=True)
    later = jnp.where(same & (z < 2 * chips) & (i.astype(F32) > first), 1.0, 0.0)
    rank = jnp.sum(later, axis=1, keepdims=True).astype(I32)

    moved = rank >= limit
    sender = jnp.where(moved, (chip + jnp.where(lane == 0, 1, chips - 1)) % chips, chip)
    place = 2 * sender + jnp.where(moved, base_moved + rank - limit, base + rank)
    far = jnp.where(lane == core, 0, 1)
    source = (far + jnp.where(moved, 2, 0)) * held + slot
    order = base_plain + rank
    plain = 2 * chip + order % 2 + jnp.where(order >= 2, 2 * chips, 0)
    broken = bad.astype(I32) > 0
    place = jnp.where(broken, plain, place)
    source = jnp.where(broken, far * held + slot, source)
    asked = jnp.sum(jnp.where(place == z, source, 0).astype(F32), axis=0, keepdims=True).astype(I32)
    column = lax.broadcasted_iota(I32, (1, LANES), 1)
    asked = jnp.where(column == 4 * chips, bad.astype(I32), asked)
    ask_ref[...] = jnp.broadcast_to(asked[None], ask_ref.shape)
    place_ref[...] = place


def plan(core, owners, slots, chips, held):
    count = owners.shape[0]
    return pl.pallas_call(
        functools.partial(plan_kernel, chips, held),
        out_shape=(
            jax.ShapeDtypeStruct((chips, 1, LANES), I32),
            jax.ShapeDtypeStruct((count, 1), I32),
        ),
        in_specs=[SMEM, VMEM, VMEM],
        out_specs=(VMEM, VMEM),
        compiler_params=params(4),
    )(core, owners, slots)


def select_kernel(at_ref, told_ref, *refs):
    tables = list(zip(refs[:-3:2], refs[1:-3:2], strict=True))
    out_ref, buf, sem = refs[-3:]
    held, rank, feats = tables[0][0].shape
    cols = feats // LANES
    count = out_ref.shape[0]
    group = count // sem.shape[0]

    def one(i, carry):
        want = told_ref[i // 2, at_ref[0] + i % 2]
        which = want // held
        row = want - which * held
        for k, (down_ref, up_ref) in enumerate(tables):

            @pl.when(which == k)
            def _():
                for c in range(cols):
                    buf[i, c * rank : (c + 1) * rank, :] = down_ref[row, :, c * LANES : (c + 1) * LANES]
                buf[i, cols * rank :, :] = up_ref[row]

        return carry

    def some(g, carry):
        lax.fori_loop(g * group, (g + 1) * group, one, 0)
        part = pl.ds(g * group, group)
        pltpu.make_async_copy(buf.at[part], out_ref.at[part], sem.at[g]).start()
        return carry

    def end(g, carry):
        part = pl.ds(g * group, group)
        pltpu.make_async_copy(buf.at[part], out_ref.at[part], sem.at[g]).wait()
        return carry

    lax.fori_loop(0, sem.shape[0], some, 0)
    lax.fori_loop(0, sem.shape[0], end, 0)


def select(at, told, *tables):
    _, rank, feats = tables[0].shape
    lanes = tables[1].shape[2]
    rows = rank * (feats // lanes) + tables[1].shape[1]
    count = 2 * told.shape[0]
    return pl.pallas_call(
        select_kernel,
        out_shape=jax.ShapeDtypeStruct((count, rows, lanes), BF16),
        in_specs=[SMEM, SMEM] + [VMEM] * len(tables),
        out_specs=ANY,
        scratch_shapes=[pltpu.VMEM((count, rows, lanes), BF16), pltpu.SemaphoreType.DMA((8,))],
        compiler_params=params(),
    )(at, told, *tables)


def shrink_kernel(cols, rank, half, at_ref, tok_ref, got_ref, out_ref):
    blocks = tok_ref.shape[0] // BLOCK
    ups = got_ref.shape[1] - cols * rank
    per = 3
    for u in range(blocks // per):
        parts = []
        for b in range(u * per, (u + 1) * per):
            place = at_ref[b]
            down = jnp.concatenate([got_ref[place, c * rank : (c + 1) * rank, :] for c in range(cols)], axis=1)
            part = lax.dot_general(
                tok_ref[b * BLOCK : (b + 1) * BLOCK, :], down, (((1,), (1,)), ((), ())), preferred_element_type=F32
            )
            parts.append(part)
        whole = jnp.concatenate(parts, axis=0)
        for k in range(2):
            t = 2 * u + k
            one = whole[2 * half * k : 2 * half * k + half]
            two = whole[2 * half * k + half : 2 * half * k + 2 * half]
            out_ref[t, :half, :] = jnp.concatenate([one, two], axis=1).astype(BF16)
            out_ref[t, half : half + ups, :] = got_ref[at_ref[u * per + k], cols * rank :, :]
            out_ref[t, half + ups :, :] = got_ref[at_ref[u * per + k + 1], cols * rank :, :]


def shrink(at, tokens, got, rank, tensors):
    tok_rows, feats = tokens.shape
    cols = feats // LANES
    _, rows, lanes = got.shape
    half = tok_rows // tensors // 2
    ups = rows - cols * rank
    return pl.pallas_call(
        functools.partial(shrink_kernel, cols, rank, half),
        out_shape=jax.ShapeDtypeStruct((tensors, half + 2 * ups, lanes), BF16),
        in_specs=[SMEM, VMEM, VMEM],
        out_specs=VMEM,
        compiler_params=params(),
    )(at, tokens, got)


def finish_kernel(rank, mine, odd_ref, got_ref, base_ref, out_ref):
    tensors, msg_rows, lanes = got_ref.shape
    total, _ = out_ref.shape
    half = total // 2
    ups = (msg_rows - half) // 2
    ucols = ups // mine
    low = jnp.sum(got_ref[:, :half, :].astype(F32), axis=0).astype(BF16)
    line = lax.broadcasted_iota(I32, (rank, ucols * tensors * ups), 0)
    col = lax.broadcasted_iota(I32, (rank, ucols * tensors * ups), 1)
    c_want = col // (tensors * ups)
    inner = col % (tensors * ups)
    src = inner // ups
    c_have = (inner % ups) // mine
    q = inner % mine
    spread = ((c_want == c_have) & (line == src * mine + q)).astype(F32).astype(BF16)
    edge = jnp.where(odd_ref[0] == 1, BLOCK // 2, BLOCK)
    maps = [got_ref[:, half + j * ups : half + (j + 1) * ups, :].reshape(tensors * ups, lanes) for j in range(2)]
    for h in range(2):
        part = low[:, h * rank : (h + 1) * rank]
        wide = jnp.dot(part, spread, preferred_element_type=F32).astype(BF16)
        row = lax.broadcasted_iota(I32, (half, lanes), 0) + h * half
        for c in range(ucols):
            piece = wide[:, c * tensors * ups : (c + 1) * tensors * ups]
            first = jnp.dot(piece, maps[0], preferred_element_type=F32)
            second = jnp.dot(piece, maps[1], preferred_element_type=F32)
            term = jnp.where(row < edge, first, second)
            here = base_ref[h * half : (h + 1) * half, c * lanes : (c + 1) * lanes].astype(F32)
            out_ref[h * half : (h + 1) * half, c * lanes : (c + 1) * lanes] = (here + term).astype(BF16)


def finish(odd, got, base, rank, mine):
    return pl.pallas_call(
        functools.partial(finish_kernel, rank, mine),
        out_shape=jax.ShapeDtypeStruct(base.shape, BF16),
        in_specs=[SMEM, VMEM, VMEM],
        out_specs=VMEM,
        compiler_params=params(),
    )(odd, got, base)


def device_part(tokens, base_weight, adapter_down, adapter_up, segment_blocks, segment_owner, segment_slot):
    chips, cores = lax.axis_size("z"), lax.axis_size("core")
    tensors = lax.axis_size(TENSOR)
    held, rank, _ = adapter_down.shape
    mine = adapter_up.shape[1]
    blocks = tokens.shape[0] // BLOCK
    core = lax.axis_index("core").astype(I32).reshape(1)
    spot = (2 * lax.axis_index("z")).astype(I32).reshape(1)
    up_rows = rows_of(adapter_up)
    across = shift(cores, 1)
    apart = [(2 * z + c, 2 * ((z + (1, -1)[c]) % chips) + c) for z in range(chips) for c in range(cores)]
    moved_down = lax.ppermute(adapter_down, STORE, apart)
    moved_up = lax.ppermute(up_rows, STORE, apart)

    ask, place = plan(core, segment_owner, segment_slot[:, None], chips, held)
    told = lax.all_to_all(ask, "z", 0, 0, tiled=True)
    told = jnp.clip(told[:, 0, :], 0, 4 * held)
    other_down = lax.ppermute(adapter_down, "core", across)
    other_up = lax.ppermute(up_rows, "core", across)
    far_up = lax.ppermute(moved_up, "core", across)
    far_down = lax.ppermute(moved_down, "core", across)
    tables = (adapter_down, up_rows, other_down, other_up, moved_down, moved_up, far_down, far_up)
    rows = select(spot, told, *tables)
    rows, base_weight = lax.optimization_barrier((rows, base_weight))

    def exchange(x):
        return lax.all_to_all(x.reshape(chips, cores, *x.shape[1:]), "z", 0, 0, tiled=True).reshape(x.shape)

    got = exchange(rows)

    base = jnp.dot(tokens, base_weight, preferred_element_type=F32).astype(BF16)
    base = summed_rows(base, TENSOR)

    lane_bad = jnp.max(told[:, 4 * chips])
    far_bad = lax.ppermute(jnp.broadcast_to(lane_bad, (8, LANES)), "core", across)[0, 0]
    any_bad = jnp.maximum(lane_bad, far_bad) > 0
    place = place[:, 0]
    count = place.shape[0]

    def twice(g):
        mine = (adapter_down, up_rows)
        theirs = tuple(lax.ppermute(x, "core", across) for x in mine)
        second = exchange(select(spot + 2 * chips, told, *mine, *theirs))
        needed = jnp.take(jnp.concatenate([g, second]), place, axis=0)
        return jnp.pad(needed, ((0, g.shape[0] - count), (0, 0), (0, 0)))

    got = lax.cond(any_bad, twice, lambda g: g, got)
    place = jnp.where(any_bad, jnp.arange(count, dtype=I32), place)
    ends = jnp.cumsum(segment_blocks[0])
    seg = jnp.sum((ends[None, :] <= jnp.arange(blocks, dtype=I32)[:, None]).astype(I32), axis=1)
    at = jnp.sum(
        jnp.where(seg[:, None] == jnp.arange(count, dtype=I32)[None, :], place[None, :], 0), axis=1
    )

    message = shrink(at, tokens, got, rank, tensors)
    got_low = lax.all_to_all(message, TENSOR, 0, 0, tiled=True)
    odd = (lax.axis_index(TENSOR) % 2).astype(I32).reshape(1)
    return finish(odd, got_low, base, rank, mine)


def solution(mesh):
    split = Mesh(mesh.devices.reshape(-1, 2, 4, 4), EVERY)
    placed = (
        P(STORE, TENSOR),
        P(TENSOR, None),
        P(STORE, None, TENSOR),
        P(STORE, TENSOR, None),
        P(STORE, None),
        P(STORE, None),
        P(STORE),
    )
    return jax.shard_map(device_part, mesh=split, in_specs=placed, out_specs=P(EVERY, None), check_vma=False)
```

time: 205 us -> 193 us (0.941)
  waiting for transfers between devices: 105 us -> 94.8 us
  local copies, waits for them, and re-layouts: 5.42 us -> 9.4 us
  other arithmetic: 12.8 us -> 9.75 us
    ppermute x5, waiting for transfers between devices: 22.3 us -> 14.6 us  [the longest x1 14.6 us: device_part(): moved_down = lax.ppermute(adapter_down, STORE, apart)]
    ppermute x6, waiting for transfers between devices: 30.9 us -> 27.2 us  [summed_rows(): lax.ppermute(piece(d), axis, shift(count, d))]
    pallas_call x1, Pallas kernels: 5.53 us -> 2.38 us  [shrink(): pl.pallas_call(functools.partial(shrink_kernel, cols, rank, half), out_sh...]
    unnamed x12 -> x15, local copies, waits for them, and re-layouts: 1.67 us -> 4.48 us
  transfers between devices with their start and end apart: 16 -> 16, of which waited for: 9 -> 8; matrix products, arithmetic and copies ran while one was open for 10% -> 10% of each run, Pallas kernels for 0% -> 1%
where the time goes in v4:
time: 193 us; the launch traced here: 192 us
  waiting for transfers between devices  94.8 us (49%)
  starting transfers between devices  63.6 us (33%)
  other arithmetic  9.75 us (5%)
  local copies, waits for them, and re-layouts  9.4 us (5%)
  Pallas kernels  9.22 us (5%)
  matrix products  3.68 us (2%)
    all_to_all x1, waiting for transfers between devices, exchange(): lax.all_to_all(x.reshape(chips, cores, *x.shape[1:]), 'z', 0, 0, tiled=True)  46.3 us
    ppermute x6, waiting for transfers between devices, summed_rows(): lax.ppermute(piece(d), axis, shift(count, d))  27.2 us
    ppermute x6, starting transfers between devices, summed_rows(): lax.ppermute(piece(d), axis, shift(count, d))  20.9 us
    ppermute x1, waiting for transfers between devices, device_part(): moved_down = lax.ppermute(adapter_down, STORE, apart)  14.6 us
    all_to_all x1, starting transfers between devices, device_part(): told = lax.all_to_all(ask, 'z', 0, 0, tiled=True)  13.5 us
    all_to_all x1, starting transfers between devices, device_part(): got_low = lax.all_to_all(message, TENSOR, 0, 0, tiled=True)  7.04 us
    all_to_all x1, waiting for transfers between devices, device_part(): told = lax.all_to_all(ask, 'z', 0, 0, tiled=True)  6.7 us
    all_to_all x1, starting transfers between devices, exchange(): lax.all_to_all(x.reshape(chips, cores, *x.shape[1:]), 'z', 0, 0, tiled=True)  6.17 us
  transfers between devices with their start and end apart: 16, of which 8 were waited for; matrix products, arithmetic and copies ran while one was open for 10% of the time, Pallas kernels for 1%

profile of v4, /device:TPU:32, one launch (start us, length us, event | category | flops | bytes accessed | tf_op | source)
XLA Modules:
  0.0 192.0 jit_solution(18280288562297429714)
XLA Ops:
  0.0 3.9 %collective-permute-start.5 = (bf16[16,64,512]{2,1,0:T(8,128)(2,1)}, bf16[16,64,512]{2,1,0:T(8,128)(2,1)S(1)}, u32[]{:S(2)}, u32[]{:S(2)}) collective-permute-start(bf16[16,64,512]{2,1,0:T(8,128)(2,1)} %refs_0_.1), channel_id=1, source_target_pairs={{0,32},{16,496},{32,64},{48,16},{64,96},{80,48},{96,128},{112,80},... | collective-permute-start | bytes 3145736 | tf_op jit(solution)/shard_map/ppermute | solution.py:275
  4.0 1.9 %collective-permute-start.3 = (bf16[16,64,512]{2,1,0:T(8,128)(2,1)}, bf16[16,64,512]{2,1,0:T(8,128)(2,1)S(1)}, u32[]{:S(2)}, u32[]{:S(2)}) collective-permute-start(bf16[16,64,512]{2,1,0:T(8,128)(2,1)} %refs_0_.1), channel_id=1, source_target_pairs={{0,16},{16,0},{1,17},{17,1},{2,18},{18,2},{3,19},{19,3},{4,20},{20... | collective-permute-start | bytes 3145736 | tf_op jit(solution)/shard_map/ppermute | solution.py:281
  5.9 14.6 %collective-permute-done.5.refs_4_ = bf16[16,64,512]{2,1,0:T(8,128)(2,1)S(1)} collective-permute-done((bf16[16,64,512]{2,1,0:T(8,128)(2,1)}, bf16[16,64,512]{2,1,0:T(8,128)(2,1)S(1)}, u32[]{:S(2)}, u32[]{:S(2)}) %collective-permute-start.5) | collective-permute-done | bytes 1048608 | tf_op jit(solution)/shard_map/ppermute | solution.py:275
  27.2 13.5 %all-to-all-start.1 = ((s32[16,1,128]{2,1,0:T(1,128)}), s32[16,1,128]{2,1,0:T(1,128)S(1)}, u32[]{:S(2)}, u32[]{:S(2)}) async-start(s32[16,1,128]{2,1,0:T(1,128)} %get-tuple-element.31), calls=%async_computation.1 | async-start | bytes 16384 | tf_op jit(solution)/shard_map/all_to_all | solution.py:279
  42.6 2.4 %collective-permute-start.8 = (bf16[16,16,128]{2,1,0:T(8,128)(2,1)S(1)}, bf16[16,16,128]{2,1,0:T(8,128)(2,1)S(1)}, u32[]{:S(2)}, u32[]{:S(2)}) collective-permute-start(bf16[16,16,128]{2,1,0:T(8,128)(2,1)S(1)} %collective-permute-done.6.refs_5_), channel_id=1, source_target_pairs={{0,16},{16,0},{1,17},{17,1},{2,18},{18,2},{3,19},{19,3},{4,20},{20... | collective-permute-start | bytes 196616 | tf_op jit(solution)/shard_map/ppermute | solution.py:283
  45.0 6.7 %all-to-all-done.1 = s32[16,1,128]{2,1,0:T(1,128)S(1)} async-done(((s32[16,1,128]{2,1,0:T(1,128)}), s32[16,1,128]{2,1,0:T(1,128)S(1)}, u32[]{:S(2)}, u32[]{:S(2)}) %all-to-all-start.1) | async-done | bytes 8224 | tf_op jit(solution)/shard_map/all_to_all | solution.py:279
  51.8 4.1 %shard_map.74 = bf16[32,272,128]{2,1,0:T(8,128)(2,1)} custom-call(s32[1]{0:T(128)} %bitcast.9.at_ref, s32[16,128]{1,0:T(8,128)S(1)} %clamp_bitcast_fusion.told_ref, bf16[16,64,512]{2,1,0:T(8,128)(2,1)} %refs_0_.1, bf16[16,16,128]{2,1,0:T(8,128)(2,1)} %bitcast.38, bf16[16,64,512]{2,1,0:T(8,128)(2,1)S(1)} %collective-permute-done.3.refs_2_, ...), custom_call_target="tpu_custom_call" | custom-call | tf_op jit(solution)/shard_map/pallas_call | solution.py:176
  55.9 6.2 %all-to-all-start.2 = ((bf16[16,2,272,128]{3,2,1,0:T(8,128)(2,1)}), bf16[16,2,272,128]{3,2,1,0:T(8,128)(2,1)S(1)}, u32[]{:S(2)}, u32[]{:S(2)}) async-start(bf16[16,2,272,128]{3,2,1,0:T(8,128)(2,1)} %bitcast.15), calls=%async_computation.2 | async-start | bytes 4456448 | tf_op jit(solution)/shard_map/all_to_all | solution.py:290
  62.1 3.7 %convolution_convert_fusion = bf16[512,3072]{0,1:T(8,128)(2,1)S(1)} fusion(bf16[3072,512]{1,0:T(8,128)(2,1)} %tok_ref.1, bf16[512,512]{1,0:T(8,128)(2,1)S(1)} %copy-done), kind=kOutput, calls=%fused_computation.6 | convolution fusion | flops 1612185600 | bytes 6815744 | tf_op jit(solution)/shard_map/dot_general | solution.py:294
  68.3 4.9 %collective-permute-start.11 = (bf16[768,512]{1,0:T(8,128)(2,1)}, bf16[768,512]{1,0:T(8,128)(2,1)S(1)}, u32[]{:S(2)}, u32[]{:S(2)}) collective-permute-start(bf16[768,512]{1,0:T(8,128)(2,1)} %get-tuple-element.36), channel_id=1, source_target_pairs={{0,12},{4,0},{8,4},{12,8},{1,13},{5,1},{9,5},{13,9},{2,14},{6,2},{... | collective-permute-start | bytes 2359304 | tf_op jit(solution)/shard_map/ppermute | solution.py:38
  73.2 2.5 %collective-permute-start.10 = (bf16[768,512]{1,0:T(8,128)(2,1)}, bf16[768,512]{1,0:T(8,128)(2,1)}, u32[]{:S(2)}, u32[]{:S(2)}) collective-permute-start(bf16[768,512]{1,0:T(8,128)(2,1)} %get-tuple-element.37), channel_id=1, source_target_pairs={{0,8},{4,12},{8,0},{12,4},{1,9},{5,13},{9,1},{13,5},{2,10},{6,14},... | collective-permute-start | bytes 2359304 | tf_op jit(solution)/shard_map/ppermute | solution.py:38
  75.7 2.9 %collective-permute-start.9 = (bf16[768,512]{1,0:T(8,128)(2,1)}, bf16[768,512]{1,0:T(8,128)(2,1)}, u32[]{:S(2)}, u32[]{:S(2)}) collective-permute-start(bf16[768,512]{1,0:T(8,128)(2,1)} %get-tuple-element.35), channel_id=1, source_target_pairs={{0,4},{4,8},{8,12},{12,0},{1,5},{5,9},{9,13},{13,1},{2,6},{6,10},{... | collective-permute-start | bytes 2359304 | tf_op jit(solution)/shard_map/ppermute | solution.py:38
  91.8 15.3 %collective-permute-done.11 = bf16[768,512]{1,0:T(8,128)(2,1)S(1)} collective-permute-done((bf16[768,512]{1,0:T(8,128)(2,1)}, bf16[768,512]{1,0:T(8,128)(2,1)S(1)}, u32[]{:S(2)}, u32[]{:S(2)}) %collective-permute-start.11) | collective-permute-done | bytes 786464 | tf_op jit(solution)/shard_map/ppermute | solution.py:38
  108.1 4.7 %collective-permute-done.9 = bf16[768,512]{1,0:T(8,128)(2,1)} collective-permute-done((bf16[768,512]{1,0:T(8,128)(2,1)}, bf16[768,512]{1,0:T(8,128)(2,1)}, u32[]{:S(2)}, u32[]{:S(2)}) %collective-permute-start.9) | collective-permute-done | bytes 786464 | tf_op jit(solution)/shard_map/ppermute | solution.py:38
  112.7 2.3 %fusion.2 = bf16[768,512]{1,0:T(8,128)(2,1)S(1)} fusion(bf16[768,512]{1,0:T(8,128)(2,1)} %copy-done.3, bf16[768,512]{1,0:T(8,128)(2,1)} %collective-permute-done.10, bf16[768,512]{1,0:T(8,128)(2,1)} %collective-permute-done.9, bf16[512,3072]{0,1:T(8,128)(2,1)} %copy-done.2, s32[]{:T(128)S(6)} %select_n.93), kind=kLoop, calls=%fused_computation.10 | loop fusion | flops 3145728 | bytes 3932164 | tf_op jit(solution)/shard_map/convert_element_type | solution.py:42
  115.0 46.3 %all-to-all-done.2 = bf16[16,2,272,128]{3,2,1,0:T(8,128)(2,1)S(1)} async-done(((bf16[16,2,272,128]{3,2,1,0:T(8,128)(2,1)}), bf16[16,2,272,128]{3,2,1,0:T(8,128)(2,1)S(1)}, u32[]{:S(2)}, u32[]{:S(2)}) %all-to-all-start.2) | async-done | bytes 2228256 | tf_op jit(solution)/shard_map/all_to_all | solution.py:290
  163.2 2.4 %shard_map.75 = bf16[16,128,128]{2,1,0:T(8,128)(2,1)} custom-call(s32[24]{0:T(128)S(1)} %select_reduce_fusion.at_ref, bf16[3072,512]{1,0:T(8,128)(2,1)S(1)} %copy-done.1, bf16[32,272,128]{2,1,0:T(8,128)(2,1)S(1)} %get-tuple-element.41.got_ref), custom_call_target="tpu_custom_call" | custom-call | tf_op jit(solution)/shard_map/pallas_call | solution.py:215
  165.5 7.0 %all-to-all-start.3 = ((bf16[16,128,128]{2,1,0:T(8,128)(2,1)}), bf16[16,128,128]{2,1,0:T(8,128)(2,1)S(1)}, u32[]{:S(2)}, u32[]{:S(2)}) async-start(bf16[16,128,128]{2,1,0:T(8,128)(2,1)} %shard_map.75), calls=%async_computation.3 | async-start | bytes 1048576 | tf_op jit(solution)/shard_map/all_to_all | solution.py:319
  172.6 5.0 %collective-permute-start.14 = (bf16[192,512]{1,0:T(8,128)(2,1)S(1)}, bf16[192,512]{1,0:T(8,128)(2,1)S(1)}, u32[]{:S(2)}, u32[]{:S(2)}) collective-permute-start(bf16[192,512]{1,0:T(8,128)(2,1)S(1)} %get-tuple-element.39), channel_id=1, source_target_pairs={{0,3},{1,0},{2,1},{3,2},{4,7},{5,4},{6,5},{7,6},{8,11},{9,8},{10,9... | collective-permute-start | bytes 589832 | tf_op jit(solution)/shard_map/ppermute | solution.py:38
  177.7 2.8 %collective-permute-start.13 = (bf16[192,512]{1,0:T(8,128)(2,1)S(1)}, bf16[192,512]{1,0:T(8,128)(2,1)S(1)}, u32[]{:S(2)}, u32[]{:S(2)}) collective-permute-start(bf16[192,512]{1,0:T(8,128)(2,1)S(1)} %get-tuple-element.40), channel_id=1, source_target_pairs={{0,2},{1,3},{2,0},{3,1},{4,6},{5,7},{6,4},{7,5},{8,10},{9,11},{10,... | collective-permute-start | bytes 589832 | tf_op jit(solution)/shard_map/ppermute | solution.py:38
  180.5 2.8 %collective-permute-start.12 = (bf16[192,512]{1,0:T(8,128)(2,1)S(1)}, bf16[192,512]{1,0:T(8,128)(2,1)S(1)}, u32[]{:S(2)}, u32[]{:S(2)}) collective-permute-start(bf16[192,512]{1,0:T(8,128)(2,1)S(1)} %get-tuple-element.38), channel_id=1, source_target_pairs={{0,1},{1,2},{2,3},{3,0},{4,5},{5,6},{6,7},{7,4},{8,9},{9,10},{10,1... | collective-permute-start | bytes 589832 | tf_op jit(solution)/shard_map/ppermute | solution.py:38
  183.3 2.8 %collective-permute-done.14 = bf16[192,512]{1,0:T(8,128)(2,1)S(1)} collective-permute-done((bf16[192,512]{1,0:T(8,128)(2,1)S(1)}, bf16[192,512]{1,0:T(8,128)(2,1)S(1)}, u32[]{:S(2)}, u32[]{:S(2)}) %collective-permute-start.14) | collective-permute-done | bytes 196640 | tf_op jit(solution)/shard_map/ppermute | solution.py:38
  186.1 2.4 %collective-permute-done.13 = bf16[192,512]{1,0:T(8,128)(2,1)S(1)} collective-permute-done((bf16[192,512]{1,0:T(8,128)(2,1)S(1)}, bf16[192,512]{1,0:T(8,128)(2,1)S(1)}, u32[]{:S(2)}, u32[]{:S(2)}) %collective-permute-start.13) | collective-permute-done | bytes 196640 | tf_op jit(solution)/shard_map/ppermute | solution.py:38
  188.4 2.1 %collective-permute-done.12 = bf16[192,512]{1,0:T(8,128)(2,1)S(1)} collective-permute-done((bf16[192,512]{1,0:T(8,128)(2,1)S(1)}, bf16[192,512]{1,0:T(8,128)(2,1)S(1)}, u32[]{:S(2)}, u32[]{:S(2)}) %collective-permute-start.12) | collective-permute-done | bytes 196640 | tf_op jit(solution)/shard_map/ppermute | solution.py:38
  (45 shorter events, 27.3 us)
Async XLA Ops:
  0.0 62.1 %copy-start = (bf16[512,512]{1,0:T(8,128)(2,1)S(1)}, bf16[512,512]{1,0:T(8,128)(2,1)}, u32[]{:S(2)}) copy-start(bf16[512,512]{1,0:T(8,128)(2,1)} %param.10) | copy-start | bytes 1572868
  0.0 20.5 %collective-permute-start.5 = (bf16[16,64,512]{2,1,0:T(8,128)(2,1)}, bf16[16,64,512]{2,1,0:T(8,128)(2,1)S(1)}, u32[]{:S(2)}, u32[]{:S(2)}) collective-permute-start(bf16[16,64,512]{2,1,0:T(8,128)(2,1)} %refs_0_.1), channel_id=1, source_target_pairs={{0,32},{16,496},{32,64},{48,16},{64,96},{80,48},{96,128},{112,80},... | collective-permute-start | bytes 3145736 | tf_op jit(solution)/shard_map/ppermute | solution.py:275
  4.0 47.8 %collective-permute-start.3 = (bf16[16,64,512]{2,1,0:T(8,128)(2,1)}, bf16[16,64,512]{2,1,0:T(8,128)(2,1)S(1)}, u32[]{:S(2)}, u32[]{:S(2)}) collective-permute-start(bf16[16,64,512]{2,1,0:T(8,128)(2,1)} %refs_0_.1), channel_id=1, source_target_pairs={{0,16},{16,0},{1,17},{17,1},{2,18},{18,2},{3,19},{19,3},{4,20},{20... | collective-permute-start | bytes 3145736 | tf_op jit(solution)/shard_map/ppermute | solution.py:281
  20.5 31.3 %collective-permute-start.7 = (bf16[16,64,512]{2,1,0:T(8,128)(2,1)S(1)}, bf16[16,64,512]{2,1,0:T(8,128)(2,1)}, u32[]{:S(2)}, u32[]{:S(2)}) collective-permute-start(bf16[16,64,512]{2,1,0:T(8,128)(2,1)S(1)} %collective-permute-done.5.refs_4_), channel_id=1, source_target_pairs={{0,16},{16,0},{1,17},{17,1},{2,18},{18,2},{3,19},{19,3},{4,20},{20... | collective-permute-start | bytes 3145736 | tf_op jit(solution)/shard_map/ppermute | solution.py:284
  22.4 20.2 %collective-permute-start.6 = (bf16[16,16,128]{2,1,0:T(8,128)(2,1)}, bf16[16,16,128]{2,1,0:T(8,128)(2,1)S(1)}, u32[]{:S(2)}, u32[]{:S(2)}) collective-permute-start(bf16[16,16,128]{2,1,0:T(8,128)(2,1)} %bitcast.36), channel_id=1, source_target_pairs={{0,32},{16,496},{32,64},{48,16},{64,96},{80,48},{96,128},{112,80},... | collective-permute-start | bytes 196616 | tf_op jit(solution)/shard_map/ppermute | solution.py:276
  27.2 24.6 %all-to-all-start.1 = ((s32[16,1,128]{2,1,0:T(1,128)}), s32[16,1,128]{2,1,0:T(1,128)S(1)}, u32[]{:S(2)}, u32[]{:S(2)}) async-start(s32[16,1,128]{2,1,0:T(1,128)} %get-tuple-element.31), calls=%async_computation.1 | async-start | bytes 16384 | tf_op jit(solution)/shard_map/all_to_all | solution.py:279
  40.7 11.1 %collective-permute-start.4 = (bf16[16,16,128]{2,1,0:T(8,128)(2,1)}, bf16[16,16,128]{2,1,0:T(8,128)(2,1)S(1)}, u32[]{:S(2)}, u32[]{:S(2)}) collective-permute-start(bf16[16,16,128]{2,1,0:T(8,128)(2,1)} %bitcast.37), channel_id=1, source_target_pairs={{0,16},{16,0},{1,17},{17,1},{2,18},{18,2},{3,19},{19,3},{4,20},{20... | collective-permute-start | bytes 196616 | tf_op jit(solution)/shard_map/ppermute | solution.py:282
  42.6 9.1 %collective-permute-start.8 = (bf16[16,16,128]{2,1,0:T(8,128)(2,1)S(1)}, bf16[16,16,128]{2,1,0:T(8,128)(2,1)S(1)}, u32[]{:S(2)}, u32[]{:S(2)}) collective-permute-start(bf16[16,16,128]{2,1,0:T(8,128)(2,1)S(1)} %collective-permute-done.6.refs_5_), channel_id=1, source_target_pairs={{0,16},{16,0},{1,17},{17,1},{2,18},{18,2},{3,19},{19,3},{4,20},{20... | collective-permute-start | bytes 196616 | tf_op jit(solution)/shard_map/ppermute | solution.py:283
  51.8 4.2 %copy-start.4 = (s32[16,128]{1,0:T(8,128)}, s32[16,128]{1,0:T(8,128)S(1)}, u32[]{:S(2)}) copy-start(s32[16,128]{1,0:T(8,128)S(1)} %clamp_bitcast_fusion.told_ref) | copy-start | bytes 24580
  55.9 105.3 %all-to-all-start.2 = ((bf16[16,2,272,128]{3,2,1,0:T(8,128)(2,1)}), bf16[16,2,272,128]{3,2,1,0:T(8,128)(2,1)S(1)}, u32[]{:S(2)}, u32[]{:S(2)}) async-start(bf16[16,2,272,128]{3,2,1,0:T(8,128)(2,1)} %bitcast.15), calls=%async_computation.2 | async-start | bytes 4456448 | tf_op jit(solution)/shard_map/all_to_all | solution.py:290
  65.8 2.5 %copy-start.2 = (bf16[512,3072]{0,1:T(8,128)(2,1)}, bf16[512,3072]{0,1:T(8,128)(2,1)S(1)}, u32[]{:S(2)}) copy-start(bf16[512,3072]{0,1:T(8,128)(2,1)S(1)} %convolution_convert_fusion) | copy-start | bytes 9437188
  65.8 12.8 %copy-start.5 = (s32[1,22]{1,0:T(1,128)S(1)}, s32[1,22]{1,0:T(1,128)}, u32[]{:S(2)}) copy-start(s32[1,22]{1,0:T(1,128)} %param.13) | copy-start | bytes 268
  68.3 38.8 %collective-permute-start.11 = (bf16[768,512]{1,0:T(8,128)(2,1)}, bf16[768,512]{1,0:T(8,128)(2,1)S(1)}, u32[]{:S(2)}, u32[]{:S(2)}) collective-permute-start(bf16[768,512]{1,0:T(8,128)(2,1)} %get-tuple-element.36), channel_id=1, source_target_pairs={{0,12},{4,0},{8,4},{12,8},{1,13},{5,1},{9,5},{13,9},{2,14},{6,2},{... | collective-permute-start | bytes 2359304 | tf_op jit(solution)/shard_map/ppermute | solution.py:38
  73.2 33.9 %collective-permute-start.10 = (bf16[768,512]{1,0:T(8,128)(2,1)}, bf16[768,512]{1,0:T(8,128)(2,1)}, u32[]{:S(2)}, u32[]{:S(2)}) collective-permute-start(bf16[768,512]{1,0:T(8,128)(2,1)} %get-tuple-element.37), channel_id=1, source_target_pairs={{0,8},{4,12},{8,0},{12,4},{1,9},{5,13},{9,1},{13,5},{2,10},{6,14},... | collective-permute-start | bytes 2359304 | tf_op jit(solution)/shard_map/ppermute | solution.py:38
  75.7 37.0 %collective-permute-start.9 = (bf16[768,512]{1,0:T(8,128)(2,1)}, bf16[768,512]{1,0:T(8,128)(2,1)}, u32[]{:S(2)}, u32[]{:S(2)}) collective-permute-start(bf16[768,512]{1,0:T(8,128)(2,1)} %get-tuple-element.35), channel_id=1, source_target_pairs={{0,4},{4,8},{8,12},{12,0},{1,5},{5,9},{9,13},{13,1},{2,6},{6,10},{... | collective-permute-start | bytes 2359304 | tf_op jit(solution)/shard_map/ppermute | solution.py:38
  84.1 3.8 %collective-permute-start.2 = (s32[8,128]{1,0:T(8,128)S(1)}, s32[8,128]{1,0:T(8,128)}, u32[]{:S(2)}, u32[]{:S(2)}) collective-permute-start(s32[8,128]{1,0:T(8,128)S(1)} %broadcast_in_dim.36), channel_id=1, source_target_pairs={{0,16},{16,0},{1,17},{17,1},{2,18},{18,2},{3,19},{19,3},{4,20},{20... | collective-permute-start | bytes 12296 | tf_op jit(solution)/shard_map/ppermute | solution.py:298
  87.9 73.4 %copy-start.6 = (s32[22]{0:T(128)S(1)}, s32[22]{0:T(128)}, u32[]{:S(2)}) copy-start(s32[22]{0:T(128)} %reduce.2) | copy-start | bytes 268
  107.1 1.0 copy-start.3
  161.3 1.9 copy-start.1
  165.5 25.1 %all-to-all-start.3 = ((bf16[16,128,128]{2,1,0:T(8,128)(2,1)}), bf16[16,128,128]{2,1,0:T(8,128)(2,1)S(1)}, u32[]{:S(2)}, u32[]{:S(2)}) async-start(bf16[16,128,128]{2,1,0:T(8,128)(2,1)} %shard_map.75), calls=%async_computation.3 | async-start | bytes 1048576 | tf_op jit(solution)/shard_map/all_to_all | solution.py:319
  172.6 13.4 %collective-permute-start.14 = (bf16[192,512]{1,0:T(8,128)(2,1)S(1)}, bf16[192,512]{1,0:T(8,128)(2,1)S(1)}, u32[]{:S(2)}, u32[]{:S(2)}) collective-permute-start(bf16[192,512]{1,0:T(8,128)(2,1)S(1)} %get-tuple-element.39), channel_id=1, source_target_pairs={{0,3},{1,0},{2,1},{3,2},{4,7},{5,4},{6,5},{7,6},{8,11},{9,8},{10,9... | collective-permute-start | bytes 589832 | tf_op jit(solution)/shard_map/ppermute | solution.py:38
  177.7 10.8 %collective-permute-start.13 = (bf16[192,512]{1,0:T(8,128)(2,1)S(1)}, bf16[192,512]{1,0:T(8,128)(2,1)S(1)}, u32[]{:S(2)}, u32[]{:S(2)}) collective-permute-start(bf16[192,512]{1,0:T(8,128)(2,1)S(1)} %get-tuple-element.40), channel_id=1, source_target_pairs={{0,2},{1,3},{2,0},{3,1},{4,6},{5,7},{6,4},{7,5},{8,10},{9,11},{10,... | collective-permute-start | bytes 589832 | tf_op jit(solution)/shard_map/ppermute | solution.py:38
  180.5 10.1 %collective-permute-start.12 = (bf16[192,512]{1,0:T(8,128)(2,1)S(1)}, bf16[192,512]{1,0:T(8,128)(2,1)S(1)}, u32[]{:S(2)}, u32[]{:S(2)}) collective-permute-start(bf16[192,512]{1,0:T(8,128)(2,1)S(1)} %get-tuple-element.38), channel_id=1, source_target_pairs={{0,1},{1,2},{2,3},{3,0},{4,5},{5,6},{6,7},{7,4},{8,9},{9,10},{10,1... | collective-permute-start | bytes 589832 | tf_op jit(solution)/shard_map/ppermute | solution.py:38

commit v5 on v4

--- a/solution.py
+++ b/solution.py
@@ -54,10 +54,16 @@
 
 
 def plan_kernel(chips, held, core_ref, owner_ref, slot_ref, ask_ref, place_ref):
-    owner = owner_ref[...]
-    slot = slot_ref[...]
+    count = owner_ref.shape[1]
     core = core_ref[0]
-    count = owner.shape[0]
+    line = lax.broadcasted_iota(I32, (count, count), 0)
+    across = lax.broadcasted_iota(I32, (count, count), 1)
+
+    def column_of(ref):
+        spread = jnp.where(line == across, jnp.broadcast_to(ref[...], (count, count)), 0)
+        return jnp.sum(spread.astype(F32), axis=1, keepdims=True).astype(I32)
+
+    owner, slot = column_of(owner_ref), column_of(slot_ref)
     chip = owner // 2
     lane = owner % 2
     z = lax.broadcasted_iota(I32, (count, LANES), 1)
@@ -110,7 +116,8 @@
     broken = bad.astype(I32) > 0
     place = jnp.where(broken, plain, place)
     source = jnp.where(broken, far * held + slot, source)
-    asked = jnp.sum(jnp.where(place == z, source, 0).astype(F32), axis=0, keepdims=True).astype(I32)
+    empty = 4 * held
+    asked = jnp.sum(jnp.where(place == z, source - empty, 0).astype(F32), axis=0, keepdims=True).astype(I32) + empty
     column = lax.broadcasted_iota(I32, (1, LANES), 1)
     asked = jnp.where(column == 4 * chips, bad.astype(I32), asked)
     ask_ref[...] = jnp.broadcast_to(asked[None], ask_ref.shape)
@@ -118,7 +125,7 @@
 
 
 def plan(core, owners, slots, chips, held):
-    count = owners.shape[0]
+    count = owners.shape[1]
     return pl.pallas_call(
         functools.partial(plan_kernel, chips, held),
         out_shape=(
@@ -132,18 +139,44 @@
 
 
 def select_kernel(at_ref, told_ref, *refs):
-    tables = list(zip(refs[:-3:2], refs[1:-3:2], strict=True))
-    out_ref, buf, sem = refs[-3:]
+    tables = list(zip(refs[0:8:2], refs[1:8:2], strict=True))
+    out_ref, buf, sem_in, sem_out = refs[8:]
     held, rank, feats = tables[0][0].shape
     cols = feats // LANES
     count = out_ref.shape[0]
-    group = count // sem.shape[0]
-
-    def one(i, carry):
+    groups = sem_out.shape[0]
+    group = count // groups
+
+    def wanted(i):
         want = told_ref[i // 2, at_ref[0] + i % 2]
         which = want // held
-        row = want - which * held
-        for k, (down_ref, up_ref) in enumerate(tables):
+        return which, want - which * held
+
+    def by_copy(which):
+        return jnp.logical_or(which == 0, which == 3)
+
+    def begin(i, carry):
+        which, row = wanted(i)
+        for k in (0, 3):
+            down_ref, up_ref = tables[k]
+
+            @pl.when(which == k)
+            def _():
+                for c in range(cols):
+                    pltpu.make_async_copy(
+                        down_ref.at[row, :, pl.ds(c * LANES, LANES)],
+                        buf.at[i, pl.ds(c * rank, rank)],
+                        sem_in.at[i],
+                    ).start()
+                ups = pl.ds(cols * rank, buf.shape[1] - cols * rank)
+                pltpu.make_async_copy(up_ref.at[row], buf.at[i, ups], sem_in.at[i]).start()
+
+        return carry
+
+    def move(i, carry):
+        which, row = wanted(i)
+        for k in (1, 2):
+            down_ref, up_ref = tables[k]
 
             @pl.when(which == k)
             def _():
@@ -153,19 +186,30 @@
 
         return carry
 
-    def some(g, carry):
-        lax.fori_loop(g * group, (g + 1) * group, one, 0)
+    def arrive(i, carry):
+        which, _ = wanted(i)
+
+        @pl.when(by_copy(which))
+        def _():
+            pltpu.make_async_copy(out_ref.at[i], buf.at[i], sem_in.at[i]).wait()
+
+        return carry
+
+    def leave(g, carry):
+        lax.fori_loop(g * group, (g + 1) * group, move, 0)
+        lax.fori_loop(g * group, (g + 1) * group, arrive, 0)
         part = pl.ds(g * group, group)
-        pltpu.make_async_copy(buf.at[part], out_ref.at[part], sem.at[g]).start()
+        pltpu.make_async_copy(buf.at[part], out_ref.at[part], sem_out.at[g]).start()
         return carry
 
     def end(g, carry):
         part = pl.ds(g * group, group)
-        pltpu.make_async_copy(buf.at[part], out_ref.at[part], sem.at[g]).wait()
-        return carry
-
-    lax.fori_loop(0, sem.shape[0], some, 0)
-    lax.fori_loop(0, sem.shape[0], end, 0)
+        pltpu.make_async_copy(buf.at[part], out_ref.at[part], sem_out.at[g]).wait()
+        return carry
+
+    lax.fori_loop(0, count, begin, 0)
+    lax.fori_loop(0, groups, leave, 0)
+    lax.fori_loop(0, groups, end, 0)
 
 
 def select(at, told, *tables):
@@ -176,34 +220,81 @@
     return pl.pallas_call(
         select_kernel,
         out_shape=jax.ShapeDtypeStruct((count, rows, lanes), BF16),
-        in_specs=[SMEM, SMEM] + [VMEM] * len(tables),
+        in_specs=[SMEM, SMEM, ANY, ANY, VMEM, VMEM, VMEM, VMEM, ANY, ANY],
         out_specs=ANY,
-        scratch_shapes=[pltpu.VMEM((count, rows, lanes), BF16), pltpu.SemaphoreType.DMA((8,))],
+        scratch_shapes=[
+            pltpu.VMEM((count, rows, lanes), BF16),
+            pltpu.SemaphoreType.DMA((count,)),
+            pltpu.SemaphoreType.DMA((8,)),
+        ],
         compiler_params=params(),
     )(at, told, *tables)
 
 
-def shrink_kernel(cols, rank, half, at_ref, tok_ref, got_ref, out_ref):
-    blocks = tok_ref.shape[0] // BLOCK
-    ups = got_ref.shape[1] - cols * rank
+def merge_kernel(place_ref, first_ref, second_ref, out_ref):
+    held = first_ref.shape[0]
+
+    def one(i, carry):
+        place = place_ref[i]
+
+        @pl.when(place < held)
+        def _():
+            out_ref[i] = first_ref[place]
+
+        @pl.when(place >= held)
+        def _():
+            out_ref[i] = second_ref[place - held]
+
+        return carry
+
+    lax.fori_loop(0, place_ref.shape[0], one, 0)
+
+
+def merge(place, first, second):
+    return pl.pallas_call(
+        merge_kernel,
+        out_shape=jax.ShapeDtypeStruct(first.shape, first.dtype),
+        in_specs=[SMEM, VMEM, VMEM],
+        out_specs=VMEM,
+        compiler_params=params(),
+    )(place, first, second)
+
+
+def shrink_kernel(cols, rank, half, at_ref, tok_ref, got_ref, out_ref, tok, maps, tok_sem, map_sem):
+    blocks, rows, _ = maps.shape
+    ups = rows - cols * rank
     per = 3
-    for u in range(blocks // per):
-        parts = []
-        for b in range(u * per, (u + 1) * per):
-            place = at_ref[b]
-            down = jnp.concatenate([got_ref[place, c * rank : (c + 1) * rank, :] for c in range(cols)], axis=1)
-            part = lax.dot_general(
-                tok_ref[b * BLOCK : (b + 1) * BLOCK, :], down, (((1,), (1,)), ((), ())), preferred_element_type=F32
-            )
-            parts.append(part)
-        whole = jnp.concatenate(parts, axis=0)
-        for k in range(2):
-            t = 2 * u + k
-            one = whole[2 * half * k : 2 * half * k + half]
-            two = whole[2 * half * k + half : 2 * half * k + 2 * half]
-            out_ref[t, :half, :] = jnp.concatenate([one, two], axis=1).astype(BF16)
-            out_ref[t, half : half + ups, :] = got_ref[at_ref[u * per + k], cols * rank :, :]
-            out_ref[t, half + ups :, :] = got_ref[at_ref[u * per + k + 1], cols * rank :, :]
+    edges = (0, blocks // 4, blocks // 4 + 9, blocks)
+    stages = list(zip(edges[:-1], edges[1:], strict=True))
+
+    def tokens_of(k):
+        part = pl.ds(stages[k][0] * BLOCK, (stages[k][1] - stages[k][0]) * BLOCK)
+        return pltpu.make_async_copy(tok_ref.at[part], tok.at[part], tok_sem.at[k])
+
+    for k, (low, high) in enumerate(stages):
+        tokens_of(k).start()
+        for b in range(low, high):
+            pltpu.make_async_copy(got_ref.at[at_ref[b]], maps.at[b], map_sem.at[b]).start()
+    for k, (low, high) in enumerate(stages):
+        tokens_of(k).wait()
+        for b in range(low, high):
+            pltpu.make_async_copy(got_ref.at[0], maps.at[b], map_sem.at[b]).wait()
+        for u in range(low // per, high // per):
+            parts = []
+            for b in range(u * per, (u + 1) * per):
+                down = jnp.concatenate([maps[b, c * rank : (c + 1) * rank, :] for c in range(cols)], axis=1)
+                part = lax.dot_general(
+                    tok[b * BLOCK : (b + 1) * BLOCK, :], down, (((1,), (1,)), ((), ())), preferred_element_type=F32
+                )
+                parts.append(part)
+            whole = jnp.concatenate(parts, axis=0)
+            for j in range(2):
+                t = 2 * u + j
+                one = whole[2 * half * j : 2 * half * j + half]
+                two = whole[2 * half * j + half : 2 * half * j + 2 * half]
+                out_ref[t, :half, :] = jnp.concatenate([one, two], axis=1).astype(BF16)
+                out_ref[t, half : half + ups, :] = maps[u * per + j, cols * rank :, :]
+                out_ref[t, half + ups :, :] = maps[u * per + j + 1, cols * rank :, :]
 
 
 def shrink(at, tokens, got, rank, tensors):
@@ -212,12 +303,19 @@
     _, rows, lanes = got.shape
     half = tok_rows // tensors // 2
     ups = rows - cols * rank
+    blocks = tok_rows // BLOCK
     return pl.pallas_call(
         functools.partial(shrink_kernel, cols, rank, half),
         out_shape=jax.ShapeDtypeStruct((tensors, half + 2 * ups, lanes), BF16),
-        in_specs=[SMEM, VMEM, VMEM],
+        in_specs=[SMEM, ANY, ANY],
         out_specs=VMEM,
-        compiler_params=params(),
+        scratch_shapes=[
+            pltpu.VMEM((tok_rows, feats), BF16),
+            pltpu.VMEM((blocks, rows, lanes), BF16),
+            pltpu.SemaphoreType.DMA((3,)),
+            pltpu.SemaphoreType.DMA((blocks,)),
+        ],
+        compiler_params=params(59),
     )(at, tokens, got)
 
 
@@ -275,7 +373,7 @@
     moved_down = lax.ppermute(adapter_down, STORE, apart)
     moved_up = lax.ppermute(up_rows, STORE, apart)
 
-    ask, place = plan(core, segment_owner, segment_slot[:, None], chips, held)
+    ask, place = plan(core, segment_owner.reshape(1, -1), segment_slot.reshape(1, -1), chips, held)
     told = lax.all_to_all(ask, "z", 0, 0, tiled=True)
     told = jnp.clip(told[:, 0, :], 0, 4 * held)
     other_down = lax.ppermute(adapter_down, "core", across)
@@ -303,9 +401,8 @@
     def twice(g):
         mine = (adapter_down, up_rows)
         theirs = tuple(lax.ppermute(x, "core", across) for x in mine)
-        second = exchange(select(spot + 2 * chips, told, *mine, *theirs))
-        needed = jnp.take(jnp.concatenate([g, second]), place, axis=0)
-        return jnp.pad(needed, ((0, g.shape[0] - count), (0, 0), (0, 0)))
+        second = exchange(select(spot + 2 * chips, told, *mine, *theirs, *theirs, *mine))
+        return merge(place, g, second)
 
     got = lax.cond(any_bad, twice, lambda g: g, got)
     place = jnp.where(any_bad, jnp.arange(count, dtype=I32), place)

time: 193 us -> 193 us (level)
  other arithmetic: 9.75 us -> 3.87 us
  waiting for transfers between devices: 94.8 us -> 99.6 us
  Pallas kernels: 9.22 us -> 12.3 us
  local copies, waits for them, and re-layouts: 9.4 us -> 6.64 us
    all_to_all x1, waiting for transfers between devices: 46.3 us -> 49.4 us  [exchange(): lax.all_to_all(x.reshape(chips, cores, *x.shape[1:]), 'z', 0, 0, tiled=True)]
    pallas_call x1, Pallas kernels: 2.38 us -> 4.94 us  [shrink(): pl.pallas_call(functools.partial(shrink_kernel, cols, rank, half), out_sh...]
    another operation x2, other arithmetic: 2.66 us -> 0.16 us
    unnamed x15 -> x18, local copies, waits for them, and re-layouts: 4.48 us -> 3.84 us
  transfers between devices with their start and end apart: 16 -> 16, of which waited for: 8 -> 9; matrix products, arithmetic and copies ran while one was open for 10% -> 5% of each run, Pallas kernels for 1% -> 1%
where the time goes in v5:
time: 193 us
  waiting for transfers between devices  99.6 us (52%)
  starting transfers between devices  64.9 us (34%)
  Pallas kernels  12.3 us (6%)
  local copies, waits for them, and re-layouts  6.64 us (3%)
  other arithmetic  3.87 us (2%)
  matrix products  3.68 us (2%)
    all_to_all x1, waiting for transfers between devices, exchange(): lax.all_to_all(x.reshape(chips, cores, *x.shape[1:]), 'z', 0, 0, tiled=True)  49.4 us
    ppermute x6, waiting for transfers between devices, summed_rows(): lax.ppermute(piece(d), axis, shift(count, d))  28.1 us
    ppermute x6, starting transfers between devices, summed_rows(): lax.ppermute(piece(d), axis, shift(count, d))  22.2 us
    ppermute x1, waiting for transfers between devices, device_part(): moved_down = lax.ppermute(adapter_down, STORE, apart)  14.6 us
    all_to_all x1, starting transfers between devices, device_part(): told = lax.all_to_all(ask, 'z', 0, 0, tiled=True)  13.5 us
    all_to_all x1, starting transfers between devices, device_part(): got_low = lax.all_to_all(message, TENSOR, 0, 0, tiled=True)  7.05 us
    all_to_all x1, waiting for transfers between devices, device_part(): told = lax.all_to_all(ask, 'z', 0, 0, tiled=True)  6.7 us
    all_to_all x1, starting transfers between devices, exchange(): lax.all_to_all(x.reshape(chips, cores, *x.shape[1:]), 'z', 0, 0, tiled=True)  6.17 us
  transfers between devices with their start and end apart: 16, of which 9 were waited for; matrix products, arithmetic and copies ran while one was open for 5% of the time, Pallas kernels for 1%

profile of v5, /device:TPU:32, one launch (start us, length us, event | category | flops | bytes accessed | tf_op | source)
XLA Modules:
  0.0 192.6 jit_solution(97706460061384236)
XLA Ops:
  0.0 3.9 %collective-permute-start.5 = (bf16[16,64,512]{2,1,0:T(8,128)(2,1)}, bf16[16,64,512]{2,1,0:T(8,128)(2,1)S(1)}, u32[]{:S(2)}, u32[]{:S(2)}) collective-permute-start(bf16[16,64,512]{2,1,0:T(8,128)(2,1)} %refs_0_.1), channel_id=1, source_target_pairs={{0,32},{16,496},{32,64},{48,16},{64,96},{80,48},{96,128},{112,80},... | collective-permute-start | bytes 3145736 | tf_op jit(solution)/shard_map/ppermute | solution.py:373
  4.0 1.9 collective-permute-start.3
  5.9 14.6 %collective-permute-done.5.refs_4_ = bf16[16,64,512]{2,1,0:T(8,128)(2,1)S(1)} collective-permute-done((bf16[16,64,512]{2,1,0:T(8,128)(2,1)}, bf16[16,64,512]{2,1,0:T(8,128)(2,1)S(1)}, u32[]{:S(2)}, u32[]{:S(2)}) %collective-permute-start.5) | collective-permute-done | bytes 1048608 | tf_op jit(solution)/shard_map/ppermute | solution.py:373
  26.9 13.5 %all-to-all-start.1 = ((s32[16,1,128]{2,1,0:T(1,128)}), s32[16,1,128]{2,1,0:T(1,128)S(1)}, u32[]{:S(2)}, u32[]{:S(2)}) async-start(s32[16,1,128]{2,1,0:T(1,128)} %get-tuple-element.31), calls=%async_computation.1 | async-start | bytes 16384 | tf_op jit(solution)/shard_map/all_to_all | solution.py:377
  42.4 2.4 %collective-permute-start.8 = (bf16[16,16,128]{2,1,0:T(8,128)(2,1)S(1)}, bf16[16,16,128]{2,1,0:T(8,128)(2,1)S(1)}, u32[]{:S(2)}, u32[]{:S(2)}) collective-permute-start(bf16[16,16,128]{2,1,0:T(8,128)(2,1)S(1)} %collective-permute-done.6.refs_5_), channel_id=1, source_target_pairs={{0,16},{16,0},{1,17},{17,1},{2,18},{18,2},{3,19},{19,3},{4,20},{20... | collective-permute-start | bytes 196616 | tf_op jit(solution)/shard_map/ppermute | solution.py:381
  44.8 6.7 %all-to-all-done.1 = s32[16,1,128]{2,1,0:T(1,128)S(1)} async-done(((s32[16,1,128]{2,1,0:T(1,128)}), s32[16,1,128]{2,1,0:T(1,128)S(1)}, u32[]{:S(2)}, u32[]{:S(2)}) %all-to-all-start.1) | async-done | bytes 8224 | tf_op jit(solution)/shard_map/all_to_all | solution.py:377
  51.6 4.7 %shard_map.74 = bf16[32,272,128]{2,1,0:T(8,128)(2,1)} custom-call(s32[1]{0:T(128)} %bitcast.10.at_ref, s32[16,128]{1,0:T(8,128)S(1)} %clamp_bitcast_fusion.told_ref, bf16[16,64,512]{2,1,0:T(8,128)(2,1)} %refs_0_.1, bf16[16,16,128]{2,1,0:T(8,128)(2,1)} %bitcast.40, bf16[16,64,512]{2,1,0:T(8,128)(2,1)S(1)} %collective-permute-done.3.refs_2_, ...), custom_call_target="tpu_custom_call" | custom-call | tf_op jit(solution)/shard_map/pallas_call | solution.py:220
  56.3 6.2 %all-to-all-start.2 = ((bf16[16,2,272,128]{3,2,1,0:T(8,128)(2,1)}), bf16[16,2,272,128]{3,2,1,0:T(8,128)(2,1)}, u32[]{:S(2)}, u32[]{:S(2)}) async-start(bf16[16,2,272,128]{3,2,1,0:T(8,128)(2,1)} %bitcast.16), calls=%async_computation.2 | async-start | bytes 4456448 | tf_op jit(solution)/shard_map/all_to_all | solution.py:388
  62.5 3.7 %convolution_convert_fusion = bf16[512,3072]{0,1:T(8,128)(2,1)S(1)} fusion(bf16[3072,512]{1,0:T(8,128)(2,1)} %tok_ref.1, bf16[512,512]{1,0:T(8,128)(2,1)S(1)} %copy-done), kind=kOutput, calls=%fused_computation | convolution fusion | flops 1612185600 | bytes 6815744 | tf_op jit(solution)/shard_map/dot_general | solution.py:392
  69.4 3.6 %collective-permute-start.9 = (bf16[768,512]{1,0:T(8,128)(2,1)}, bf16[768,512]{1,0:T(8,128)(2,1)S(1)}, u32[]{:S(2)}, u32[]{:S(2)}) collective-permute-start(bf16[768,512]{1,0:T(8,128)(2,1)} %get-tuple-element.35), channel_id=1, source_target_pairs={{0,4},{4,8},{8,12},{12,0},{1,5},{5,9},{9,13},{13,1},{2,6},{6,10},{... | collective-permute-start | bytes 2359304 | tf_op jit(solution)/shard_map/ppermute | solution.py:38
  73.0 3.6 %collective-permute-start.11 = (bf16[768,512]{1,0:T(8,128)(2,1)}, bf16[768,512]{1,0:T(8,128)(2,1)S(1)}, u32[]{:S(2)}, u32[]{:S(2)}) collective-permute-start(bf16[768,512]{1,0:T(8,128)(2,1)} %get-tuple-element.36), channel_id=1, source_target_pairs={{0,12},{4,0},{8,4},{12,8},{1,13},{5,1},{9,5},{13,9},{2,14},{6,2},{... | collective-permute-start | bytes 2359304 | tf_op jit(solution)/shard_map/ppermute | solution.py:38
  76.5 3.9 %collective-permute-start.10 = (bf16[768,512]{1,0:T(8,128)(2,1)}, bf16[768,512]{1,0:T(8,128)(2,1)}, u32[]{:S(2)}, u32[]{:S(2)}) collective-permute-start(bf16[768,512]{1,0:T(8,128)(2,1)} %get-tuple-element.37), channel_id=1, source_target_pairs={{0,8},{4,12},{8,0},{12,4},{1,9},{5,13},{9,1},{13,5},{2,10},{6,14},... | collective-permute-start | bytes 2359304 | tf_op jit(solution)/shard_map/ppermute | solution.py:38
  87.4 4.8 %collective-permute-done.9 = bf16[768,512]{1,0:T(8,128)(2,1)S(1)} collective-permute-done((bf16[768,512]{1,0:T(8,128)(2,1)}, bf16[768,512]{1,0:T(8,128)(2,1)S(1)}, u32[]{:S(2)}, u32[]{:S(2)}) %collective-permute-start.9) | collective-permute-done | bytes 786464 | tf_op jit(solution)/shard_map/ppermute | solution.py:38
  92.2 3.3 %collective-permute-done.11 = bf16[768,512]{1,0:T(8,128)(2,1)S(1)} collective-permute-done((bf16[768,512]{1,0:T(8,128)(2,1)}, bf16[768,512]{1,0:T(8,128)(2,1)S(1)}, u32[]{:S(2)}, u32[]{:S(2)}) %collective-permute-start.11) | collective-permute-done | bytes 786464 | tf_op jit(solution)/shard_map/ppermute | solution.py:38
  96.4 14.0 %collective-permute-done.10 = bf16[768,512]{1,0:T(8,128)(2,1)} collective-permute-done((bf16[768,512]{1,0:T(8,128)(2,1)}, bf16[768,512]{1,0:T(8,128)(2,1)}, u32[]{:S(2)}, u32[]{:S(2)}) %collective-permute-start.10) | collective-permute-done | bytes 786464 | tf_op jit(solution)/shard_map/ppermute | solution.py:38
  110.3 2.1 %fusion.2 = bf16[768,512]{1,0:T(8,128)(2,1)S(1)} fusion(bf16[768,512]{1,0:T(8,128)(2,1)} %copy-done.6, bf16[768,512]{1,0:T(8,128)(2,1)} %collective-permute-done.10, bf16[768,512]{1,0:T(8,128)(2,1)S(1)} %collective-permute-done.9, bf16[512,3072]{0,1:T(8,128)(2,1)} %copy-done.5, s32[]{:T(128)S(6)} %select_n.84), kind=kLoop, calls=%fused_computation.4 | loop fusion | flops 3145728 | bytes 3932164 | tf_op jit(solution)/shard_map/convert_element_type | solution.py:42
  112.4 49.4 %all-to-all-done.2 = bf16[16,2,272,128]{3,2,1,0:T(8,128)(2,1)} async-done(((bf16[16,2,272,128]{3,2,1,0:T(8,128)(2,1)}), bf16[16,2,272,128]{3,2,1,0:T(8,128)(2,1)}, u32[]{:S(2)}, u32[]{:S(2)}) %all-to-all-start.2) | async-done | bytes 2228256 | tf_op jit(solution)/shard_map/all_to_all | solution.py:388
  161.8 4.9 %shard_map.75 = bf16[16,128,128]{2,1,0:T(8,128)(2,1)} custom-call(s32[24]{0:T(128)} %select_reduce_fusion.at_ref, bf16[3072,512]{1,0:T(8,128)(2,1)} %tok_ref.1, bf16[32,272,128]{2,1,0:T(8,128)(2,1)} %get-tuple-element.41.got_ref), custom_call_target="tpu_custom_call" | custom-call | tf_op jit(solution)/shard_map/pallas_call | solution.py:307
  166.8 7.0 %all-to-all-start.3 = ((bf16[16,128,128]{2,1,0:T(8,128)(2,1)}), bf16[16,128,128]{2,1,0:T(8,128)(2,1)S(1)}, u32[]{:S(2)}, u32[]{:S(2)}) async-start(bf16[16,128,128]{2,1,0:T(8,128)(2,1)} %shard_map.75), calls=%async_computation.3 | async-start | bytes 1048576 | tf_op jit(solution)/shard_map/all_to_all | solution.py:416
  173.9 3.8 %collective-permute-start.12 = (bf16[192,512]{1,0:T(8,128)(2,1)S(1)}, bf16[192,512]{1,0:T(8,128)(2,1)S(1)}, u32[]{:S(2)}, u32[]{:S(2)}) collective-permute-start(bf16[192,512]{1,0:T(8,128)(2,1)S(1)} %get-tuple-element.38), channel_id=1, source_target_pairs={{0,1},{1,2},{2,3},{3,0},{4,5},{5,6},{6,7},{7,4},{8,9},{9,10},{10,1... | collective-permute-start | bytes 589832 | tf_op jit(solution)/shard_map/ppermute | solution.py:38
  177.7 3.2 %collective-permute-start.14 = (bf16[192,512]{1,0:T(8,128)(2,1)S(1)}, bf16[192,512]{1,0:T(8,128)(2,1)S(1)}, u32[]{:S(2)}, u32[]{:S(2)}) collective-permute-start(bf16[192,512]{1,0:T(8,128)(2,1)S(1)} %get-tuple-element.39), channel_id=1, source_target_pairs={{0,3},{1,0},{2,1},{3,2},{4,7},{5,4},{6,5},{7,6},{8,11},{9,8},{10,9... | collective-permute-start | bytes 589832 | tf_op jit(solution)/shard_map/ppermute | solution.py:38
  180.9 4.1 %collective-permute-start.13 = (bf16[192,512]{1,0:T(8,128)(2,1)S(1)}, bf16[192,512]{1,0:T(8,128)(2,1)S(1)}, u32[]{:S(2)}, u32[]{:S(2)}) collective-permute-start(bf16[192,512]{1,0:T(8,128)(2,1)S(1)} %get-tuple-element.40), channel_id=1, source_target_pairs={{0,2},{1,3},{2,0},{3,1},{4,6},{5,7},{6,4},{7,5},{8,10},{9,11},{10,... | collective-permute-start | bytes 589832 | tf_op jit(solution)/shard_map/ppermute | solution.py:38
  185.1 2.7 %collective-permute-done.12 = bf16[192,512]{1,0:T(8,128)(2,1)S(1)} collective-permute-done((bf16[192,512]{1,0:T(8,128)(2,1)S(1)}, bf16[192,512]{1,0:T(8,128)(2,1)S(1)}, u32[]{:S(2)}, u32[]{:S(2)}) %collective-permute-start.12) | collective-permute-done | bytes 196640 | tf_op jit(solution)/shard_map/ppermute | solution.py:38
  187.8 3.4 %collective-permute-done.13 = bf16[192,512]{1,0:T(8,128)(2,1)S(1)} collective-permute-done((bf16[192,512]{1,0:T(8,128)(2,1)S(1)}, bf16[192,512]{1,0:T(8,128)(2,1)S(1)}, u32[]{:S(2)}, u32[]{:S(2)}) %collective-permute-start.13) | collective-permute-done | bytes 196640 | tf_op jit(solution)/shard_map/ppermute | solution.py:38
  (47 shorter events, 19.6 us)
Async XLA Ops:
  0.0 62.5 %copy-start = (bf16[512,512]{1,0:T(8,128)(2,1)S(1)}, bf16[512,512]{1,0:T(8,128)(2,1)}, u32[]{:S(2)}) copy-start(bf16[512,512]{1,0:T(8,128)(2,1)} %param.10) | copy-start | bytes 1572868
  0.0 20.5 %collective-permute-start.5 = (bf16[16,64,512]{2,1,0:T(8,128)(2,1)}, bf16[16,64,512]{2,1,0:T(8,128)(2,1)S(1)}, u32[]{:S(2)}, u32[]{:S(2)}) collective-permute-start(bf16[16,64,512]{2,1,0:T(8,128)(2,1)} %refs_0_.1), channel_id=1, source_target_pairs={{0,32},{16,496},{32,64},{48,16},{64,96},{80,48},{96,128},{112,80},... | collective-permute-start | bytes 3145736 | tf_op jit(solution)/shard_map/ppermute | solution.py:373
  4.0 47.6 %collective-permute-start.3 = (bf16[16,64,512]{2,1,0:T(8,128)(2,1)}, bf16[16,64,512]{2,1,0:T(8,128)(2,1)S(1)}, u32[]{:S(2)}, u32[]{:S(2)}) collective-permute-start(bf16[16,64,512]{2,1,0:T(8,128)(2,1)} %refs_0_.1), channel_id=1, source_target_pairs={{0,16},{16,0},{1,17},{17,1},{2,18},{18,2},{3,19},{19,3},{4,20},{20... | collective-permute-start | bytes 3145736 | tf_op jit(solution)/shard_map/ppermute | solution.py:379
  20.5 31.1 %collective-permute-start.7 = (bf16[16,64,512]{2,1,0:T(8,128)(2,1)S(1)}, bf16[16,64,512]{2,1,0:T(8,128)(2,1)}, u32[]{:S(2)}, u32[]{:S(2)}) collective-permute-start(bf16[16,64,512]{2,1,0:T(8,128)(2,1)S(1)} %collective-permute-done.5.refs_4_), channel_id=1, source_target_pairs={{0,16},{16,0},{1,17},{17,1},{2,18},{18,2},{3,19},{19,3},{4,20},{20... | collective-permute-start | bytes 3145736 | tf_op jit(solution)/shard_map/ppermute | solution.py:382
  22.4 20.0 %collective-permute-start.6 = (bf16[16,16,128]{2,1,0:T(8,128)(2,1)}, bf16[16,16,128]{2,1,0:T(8,128)(2,1)S(1)}, u32[]{:S(2)}, u32[]{:S(2)}) collective-permute-start(bf16[16,16,128]{2,1,0:T(8,128)(2,1)} %bitcast.38), channel_id=1, source_target_pairs={{0,32},{16,496},{32,64},{48,16},{64,96},{80,48},{96,128},{112,80},... | collective-permute-start | bytes 196616 | tf_op jit(solution)/shard_map/ppermute | solution.py:374
  24.3 0.7 copy-start.2
  26.9 24.6 %all-to-all-start.1 = ((s32[16,1,128]{2,1,0:T(1,128)}), s32[16,1,128]{2,1,0:T(1,128)S(1)}, u32[]{:S(2)}, u32[]{:S(2)}) async-start(s32[16,1,128]{2,1,0:T(1,128)} %get-tuple-element.31), calls=%async_computation.1 | async-start | bytes 16384 | tf_op jit(solution)/shard_map/all_to_all | solution.py:377
  40.5 11.1 %collective-permute-start.4 = (bf16[16,16,128]{2,1,0:T(8,128)(2,1)}, bf16[16,16,128]{2,1,0:T(8,128)(2,1)S(1)}, u32[]{:S(2)}, u32[]{:S(2)}) collective-permute-start(bf16[16,16,128]{2,1,0:T(8,128)(2,1)} %bitcast.39), channel_id=1, source_target_pairs={{0,16},{16,0},{1,17},{17,1},{2,18},{18,2},{3,19},{19,3},{4,20},{20... | collective-permute-start | bytes 196616 | tf_op jit(solution)/shard_map/ppermute | solution.py:380
  42.4 9.1 %collective-permute-start.8 = (bf16[16,16,128]{2,1,0:T(8,128)(2,1)S(1)}, bf16[16,16,128]{2,1,0:T(8,128)(2,1)S(1)}, u32[]{:S(2)}, u32[]{:S(2)}) collective-permute-start(bf16[16,16,128]{2,1,0:T(8,128)(2,1)S(1)} %collective-permute-done.6.refs_5_), channel_id=1, source_target_pairs={{0,16},{16,0},{1,17},{17,1},{2,18},{18,2},{3,19},{19,3},{4,20},{20... | collective-permute-start | bytes 196616 | tf_op jit(solution)/shard_map/ppermute | solution.py:381
  51.5 29.2 %copy-start.7 = (s32[16,128]{1,0:T(8,128)}, s32[16,128]{1,0:T(8,128)S(1)}, u32[]{:S(2)}) copy-start(s32[16,128]{1,0:T(8,128)S(1)} %clamp_bitcast_fusion.told_ref) | copy-start | bytes 24580
  56.3 105.5 %all-to-all-start.2 = ((bf16[16,2,272,128]{3,2,1,0:T(8,128)(2,1)}), bf16[16,2,272,128]{3,2,1,0:T(8,128)(2,1)}, u32[]{:S(2)}, u32[]{:S(2)}) async-start(bf16[16,2,272,128]{3,2,1,0:T(8,128)(2,1)} %bitcast.16), calls=%async_computation.2 | async-start | bytes 4456448 | tf_op jit(solution)/shard_map/all_to_all | solution.py:388
  66.1 1.7 copy-start.5
  67.8 12.6 %copy-start.9 = (s32[1,22]{1,0:T(1,128)S(1)}, s32[1,22]{1,0:T(1,128)}, u32[]{:S(2)}) copy-start(s32[1,22]{1,0:T(1,128)} %param.13) | copy-start | bytes 268
  69.4 92.5 %copy-start.4 = (bf16[16,64,512]{2,1,0:T(8,128)(2,1)S(1)}, bf16[16,64,512]{2,1,0:T(8,128)(2,1)}, u32[]{:S(2)}) copy-start(bf16[16,64,512]{2,1,0:T(8,128)(2,1)} %refs_0_.1) | copy-start | bytes 3145732
  69.4 22.8 %collective-permute-start.9 = (bf16[768,512]{1,0:T(8,128)(2,1)}, bf16[768,512]{1,0:T(8,128)(2,1)S(1)}, u32[]{:S(2)}, u32[]{:S(2)}) collective-permute-start(bf16[768,512]{1,0:T(8,128)(2,1)} %get-tuple-element.35), channel_id=1, source_target_pairs={{0,4},{4,8},{8,12},{12,0},{1,5},{5,9},{9,13},{13,1},{2,6},{6,10},{... | collective-permute-start | bytes 2359304 | tf_op jit(solution)/shard_map/ppermute | solution.py:38
  73.0 22.5 %collective-permute-start.11 = (bf16[768,512]{1,0:T(8,128)(2,1)}, bf16[768,512]{1,0:T(8,128)(2,1)S(1)}, u32[]{:S(2)}, u32[]{:S(2)}) collective-permute-start(bf16[768,512]{1,0:T(8,128)(2,1)} %get-tuple-element.36), channel_id=1, source_target_pairs={{0,12},{4,0},{8,4},{12,8},{1,13},{5,1},{9,5},{13,9},{2,14},{6,2},{... | collective-permute-start | bytes 2359304 | tf_op jit(solution)/shard_map/ppermute | solution.py:38
  76.5 33.8 %collective-permute-start.10 = (bf16[768,512]{1,0:T(8,128)(2,1)}, bf16[768,512]{1,0:T(8,128)(2,1)}, u32[]{:S(2)}, u32[]{:S(2)}) collective-permute-start(bf16[768,512]{1,0:T(8,128)(2,1)} %get-tuple-element.37), channel_id=1, source_target_pairs={{0,8},{4,12},{8,0},{12,4},{1,9},{5,13},{9,1},{13,5},{2,10},{6,14},... | collective-permute-start | bytes 2359304 | tf_op jit(solution)/shard_map/ppermute | solution.py:38
  82.0 3.1 %collective-permute-start.2 = (s32[8,128]{1,0:T(8,128)S(1)}, s32[8,128]{1,0:T(8,128)S(1)}, u32[]{:S(2)}, u32[]{:S(2)}) collective-permute-start(s32[8,128]{1,0:T(8,128)S(1)} %broadcast_in_dim.20), channel_id=1, source_target_pairs={{0,16},{16,0},{1,17},{17,1},{2,18},{18,2},{3,19},{19,3},{4,20},{20... | collective-permute-start | bytes 12296 | tf_op jit(solution)/shard_map/ppermute | solution.py:396
  84.2 77.6 %copy-start.8 = (s32[16,128]{1,0:T(8,128)S(1)}, s32[16,128]{1,0:T(8,128)}, u32[]{:S(2)}) copy-start(s32[16,128]{1,0:T(8,128)} %copy-done.7) | copy-start | bytes 24580
  95.5 0.9 copy-start.6
  166.8 24.5 %all-to-all-start.3 = ((bf16[16,128,128]{2,1,0:T(8,128)(2,1)}), bf16[16,128,128]{2,1,0:T(8,128)(2,1)S(1)}, u32[]{:S(2)}, u32[]{:S(2)}) async-start(bf16[16,128,128]{2,1,0:T(8,128)(2,1)} %shard_map.75), calls=%async_computation.3 | async-start | bytes 1048576 | tf_op jit(solution)/shard_map/all_to_all | solution.py:416
  173.9 13.9 %collective-permute-start.12 = (bf16[192,512]{1,0:T(8,128)(2,1)S(1)}, bf16[192,512]{1,0:T(8,128)(2,1)S(1)}, u32[]{:S(2)}, u32[]{:S(2)}) collective-permute-start(bf16[192,512]{1,0:T(8,128)(2,1)S(1)} %get-tuple-element.38), channel_id=1, source_target_pairs={{0,1},{1,2},{2,3},{3,0},{4,5},{5,6},{6,7},{7,4},{8,9},{9,10},{10,1... | collective-permute-start | bytes 589832 | tf_op jit(solution)/shard_map/ppermute | solution.py:38
  177.7 10.1 %collective-permute-start.14 = (bf16[192,512]{1,0:T(8,128)(2,1)S(1)}, bf16[192,512]{1,0:T(8,128)(2,1)S(1)}, u32[]{:S(2)}, u32[]{:S(2)}) collective-permute-start(bf16[192,512]{1,0:T(8,128)(2,1)S(1)} %get-tuple-element.39), channel_id=1, source_target_pairs={{0,3},{1,0},{2,1},{3,2},{4,7},{5,4},{6,5},{7,6},{8,11},{9,8},{10,9... | collective-permute-start | bytes 589832 | tf_op jit(solution)/shard_map/ppermute | solution.py:38
  180.9 10.2 %collective-permute-start.13 = (bf16[192,512]{1,0:T(8,128)(2,1)S(1)}, bf16[192,512]{1,0:T(8,128)(2,1)S(1)}, u32[]{:S(2)}, u32[]{:S(2)}) collective-permute-start(bf16[192,512]{1,0:T(8,128)(2,1)S(1)} %get-tuple-element.40), channel_id=1, source_target_pairs={{0,2},{1,3},{2,0},{3,1},{4,6},{5,7},{6,4},{7,5},{8,10},{9,11},{10,... | collective-permute-start | bytes 589832 | tf_op jit(solution)/shard_map/ppermute | solution.py:38
  (1 other events, 0.7 us)

commit v6 on v4

--- a/solution.py
+++ b/solution.py
@@ -53,11 +53,25 @@
     return up.reshape(held, mine, ucols, LANES).transpose(0, 2, 1, 3).reshape(held, mine * ucols, LANES)
 
 
-def plan_kernel(chips, held, core_ref, owner_ref, slot_ref, ask_ref, place_ref):
-    owner = owner_ref[...]
-    slot = slot_ref[...]
+def plan_kernel(chips, held, core_ref, owner_hbm, slot_hbm, ask_ref, place_ref, owner_ref, slot_ref, sem):
+    reads = [
+        pltpu.make_async_copy(owner_hbm, owner_ref, sem.at[0]),
+        pltpu.make_async_copy(slot_hbm, slot_ref, sem.at[1]),
+    ]
+    for read in reads:
+        read.start()
+    for read in reads:
+        read.wait()
+    count = owner_ref.shape[1]
     core = core_ref[0]
-    count = owner.shape[0]
+    line = lax.broadcasted_iota(I32, (count, count), 0)
+    across = lax.broadcasted_iota(I32, (count, count), 1)
+
+    def column_of(ref):
+        spread = jnp.where(line == across, jnp.broadcast_to(ref[...], (count, count)), 0)
+        return jnp.sum(spread.astype(F32), axis=1, keepdims=True).astype(I32)
+
+    owner, slot = column_of(owner_ref), column_of(slot_ref)
     chip = owner // 2
     lane = owner % 2
     z = lax.broadcasted_iota(I32, (count, LANES), 1)
@@ -110,7 +124,8 @@
     broken = bad.astype(I32) > 0
     place = jnp.where(broken, plain, place)
     source = jnp.where(broken, far * held + slot, source)
-    asked = jnp.sum(jnp.where(place == z, source, 0).astype(F32), axis=0, keepdims=True).astype(I32)
+    empty = 4 * held
+    asked = jnp.sum(jnp.where(place == z, source - empty, 0).astype(F32), axis=0, keepdims=True).astype(I32) + empty
     column = lax.broadcasted_iota(I32, (1, LANES), 1)
     asked = jnp.where(column == 4 * chips, bad.astype(I32), asked)
     ask_ref[...] = jnp.broadcast_to(asked[None], ask_ref.shape)
@@ -118,15 +133,20 @@
 
 
 def plan(core, owners, slots, chips, held):
-    count = owners.shape[0]
+    count = owners.shape[1]
     return pl.pallas_call(
         functools.partial(plan_kernel, chips, held),
         out_shape=(
             jax.ShapeDtypeStruct((chips, 1, LANES), I32),
             jax.ShapeDtypeStruct((count, 1), I32),
         ),
-        in_specs=[SMEM, VMEM, VMEM],
+        in_specs=[SMEM, ANY, ANY],
         out_specs=(VMEM, VMEM),
+        scratch_shapes=[
+            pltpu.VMEM((1, count), I32),
+            pltpu.VMEM((1, count), I32),
+            pltpu.SemaphoreType.DMA((2,)),
+        ],
         compiler_params=params(4),
     )(core, owners, slots)
 
@@ -183,27 +203,67 @@
     )(at, told, *tables)
 
 
-def shrink_kernel(cols, rank, half, at_ref, tok_ref, got_ref, out_ref):
-    blocks = tok_ref.shape[0] // BLOCK
+def merge_kernel(place_ref, first_ref, second_ref, out_ref):
+    held = first_ref.shape[0]
+
+    def one(i, carry):
+        place = place_ref[i]
+
+        @pl.when(place < held)
+        def _():
+            out_ref[i] = first_ref[place]
+
+        @pl.when(place >= held)
+        def _():
+            out_ref[i] = second_ref[place - held]
+
+        return carry
+
+    lax.fori_loop(0, place_ref.shape[0], one, 0)
+
+
+def merge(place, first, second):
+    return pl.pallas_call(
+        merge_kernel,
+        out_shape=jax.ShapeDtypeStruct(first.shape, first.dtype),
+        in_specs=[SMEM, VMEM, VMEM],
+        out_specs=VMEM,
+        compiler_params=params(),
+    )(place, first, second)
+
+
+def shrink_kernel(cols, rank, half, at_ref, tok_ref, got_ref, out_ref, tok, sem):
+    blocks = tok.shape[0] // BLOCK
     ups = got_ref.shape[1] - cols * rank
     per = 3
-    for u in range(blocks // per):
-        parts = []
-        for b in range(u * per, (u + 1) * per):
-            place = at_ref[b]
-            down = jnp.concatenate([got_ref[place, c * rank : (c + 1) * rank, :] for c in range(cols)], axis=1)
-            part = lax.dot_general(
-                tok_ref[b * BLOCK : (b + 1) * BLOCK, :], down, (((1,), (1,)), ((), ())), preferred_element_type=F32
-            )
-            parts.append(part)
-        whole = jnp.concatenate(parts, axis=0)
-        for k in range(2):
-            t = 2 * u + k
-            one = whole[2 * half * k : 2 * half * k + half]
-            two = whole[2 * half * k + half : 2 * half * k + 2 * half]
-            out_ref[t, :half, :] = jnp.concatenate([one, two], axis=1).astype(BF16)
-            out_ref[t, half : half + ups, :] = got_ref[at_ref[u * per + k], cols * rank :, :]
-            out_ref[t, half + ups :, :] = got_ref[at_ref[u * per + k + 1], cols * rank :, :]
+    edges = (0, blocks // 4, blocks // 4 + 9, blocks)
+    stages = list(zip(edges[:-1], edges[1:], strict=True))
+
+    def tokens_of(k):
+        part = pl.ds(stages[k][0] * BLOCK, (stages[k][1] - stages[k][0]) * BLOCK)
+        return pltpu.make_async_copy(tok_ref.at[part], tok.at[part], sem.at[k])
+
+    for k in range(len(stages)):
+        tokens_of(k).start()
+    for k, (low, high) in enumerate(stages):
+        tokens_of(k).wait()
+        for u in range(low // per, high // per):
+            parts = []
+            for b in range(u * per, (u + 1) * per):
+                place = at_ref[b]
+                down = jnp.concatenate([got_ref[place, c * rank : (c + 1) * rank, :] for c in range(cols)], axis=1)
+                part = lax.dot_general(
+                    tok[b * BLOCK : (b + 1) * BLOCK, :], down, (((1,), (1,)), ((), ())), preferred_element_type=F32
+                )
+                parts.append(part)
+            whole = jnp.concatenate(parts, axis=0)
+            for j in range(2):
+                t = 2 * u + j
+                one = whole[2 * half * j : 2 * half * j + half]
+                two = whole[2 * half * j + half : 2 * half * j + 2 * half]
+                out_ref[t, :half, :] = jnp.concatenate([one, two], axis=1).astype(BF16)
+                out_ref[t, half : half + ups, :] = got_ref[at_ref[u * per + j], cols * rank :, :]
+                out_ref[t, half + ups :, :] = got_ref[at_ref[u * per + j + 1], cols * rank :, :]
 
 
 def shrink(at, tokens, got, rank, tensors):
@@ -215,9 +275,10 @@
     return pl.pallas_call(
         functools.partial(shrink_kernel, cols, rank, half),
         out_shape=jax.ShapeDtypeStruct((tensors, half + 2 * ups, lanes), BF16),
-        in_specs=[SMEM, VMEM, VMEM],
+        in_specs=[SMEM, ANY, VMEM],
         out_specs=VMEM,
-        compiler_params=params(),
+        scratch_shapes=[pltpu.VMEM((tok_rows, feats), BF16), pltpu.SemaphoreType.DMA((3,))],
+        compiler_params=params(59),
     )(at, tokens, got)
 
 
@@ -265,7 +326,6 @@
     chips, cores = lax.axis_size("z"), lax.axis_size("core")
     tensors = lax.axis_size(TENSOR)
     held, rank, _ = adapter_down.shape
-    mine = adapter_up.shape[1]
     blocks = tokens.shape[0] // BLOCK
     core = lax.axis_index("core").astype(I32).reshape(1)
     spot = (2 * lax.axis_index("z")).astype(I32).reshape(1)
@@ -275,7 +335,7 @@
     moved_down = lax.ppermute(adapter_down, STORE, apart)
     moved_up = lax.ppermute(up_rows, STORE, apart)
 
-    ask, place = plan(core, segment_owner, segment_slot[:, None], chips, held)
+    ask, place = plan(core, segment_owner.reshape(1, -1), segment_slot.reshape(1, -1), chips, held)
     told = lax.all_to_all(ask, "z", 0, 0, tiled=True)
     told = jnp.clip(told[:, 0, :], 0, 4 * held)
     other_down = lax.ppermute(adapter_down, "core", across)
@@ -300,25 +360,25 @@
     place = place[:, 0]
     count = place.shape[0]
 
-    def twice(g):
+    ends = jnp.cumsum(segment_blocks[0])
+    seg = jnp.sum((ends[None, :] <= jnp.arange(blocks, dtype=I32)[:, None]).astype(I32), axis=1)
+    ids = jnp.arange(count, dtype=I32)
+    at = jnp.sum(jnp.where(seg[:, None] == ids[None, :], place[None, :], 0), axis=1)
+    odd = (lax.axis_index(TENSOR) % 2).astype(I32).reshape(1)
+
+    def low_rank(where, maps):
+        message = shrink(where, tokens, maps, rank, tensors)
+        return lax.all_to_all(message, TENSOR, 0, 0, tiled=True)
+
+    def twice(out):
         mine = (adapter_down, up_rows)
         theirs = tuple(lax.ppermute(x, "core", across) for x in mine)
         second = exchange(select(spot + 2 * chips, told, *mine, *theirs))
-        needed = jnp.take(jnp.concatenate([g, second]), place, axis=0)
-        return jnp.pad(needed, ((0, g.shape[0] - count), (0, 0), (0, 0)))
-
-    got = lax.cond(any_bad, twice, lambda g: g, got)
-    place = jnp.where(any_bad, jnp.arange(count, dtype=I32), place)
-    ends = jnp.cumsum(segment_blocks[0])
-    seg = jnp.sum((ends[None, :] <= jnp.arange(blocks, dtype=I32)[:, None]).astype(I32), axis=1)
-    at = jnp.sum(
-        jnp.where(seg[:, None] == jnp.arange(count, dtype=I32)[None, :], place[None, :], 0), axis=1
-    )
-
-    message = shrink(at, tokens, got, rank, tensors)
-    got_low = lax.all_to_all(message, TENSOR, 0, 0, tiled=True)
-    odd = (lax.axis_index(TENSOR) % 2).astype(I32).reshape(1)
-    return finish(odd, got_low, base, rank, mine)
+        return finish(odd, low_rank(seg, merge(place, got, second)), base, rank, mine_ranks)
+
+    mine_ranks = adapter_up.shape[1]
+    out = finish(odd, low_rank(jnp.minimum(at, got.shape[0] - 1), got), base, rank, mine_ranks)
+    return lax.cond(any_bad, twice, lambda x: x, out)
 
 
 def solution(mesh):

time: 193 us -> 198 us (1.026)
  the two profiles are of different devices: /device:TPU:32 before, /device:TPU:1 now
where the time goes in v6:
time: 198 us; the launch traced here: 197 us
  waiting for transfers between devices  92 us (46%)
  starting transfers between devices  71.4 us (36%)
  Pallas kernels  10.3 us (5%)
  local copies, waits for them, and re-layouts  9.63 us (5%)
  other arithmetic  8.55 us (4%)
  matrix products  3.69 us (2%)
    all_to_all x1, waiting for transfers between devices, exchange(): lax.all_to_all(x.reshape(chips, cores, *x.shape[1:]), 'z', 0, 0, tiled=True)  48.5 us
    ppermute x6, waiting for transfers between devices, summed_rows(): lax.ppermute(piece(d), axis, shift(count, d))  25.7 us
    ppermute x6, starting transfers between devices, summed_rows(): lax.ppermute(piece(d), axis, shift(count, d))  20.7 us
    ppermute x1, starting transfers between devices, device_part(): moved_down = lax.ppermute(adapter_down, STORE, apart)  12.1 us
    ppermute x1, waiting for transfers between devices, device_part(): moved_down = lax.ppermute(adapter_down, STORE, apart)  10.1 us
    all_to_all x1, starting transfers between devices, device_part(): told = lax.all_to_all(ask, 'z', 0, 0, tiled=True)  7.21 us
    all_to_all x1, starting transfers between devices, low_rank(): return lax.all_to_all(message, TENSOR, 0, 0, tiled=True)  6.9 us
    all_to_all x1, waiting for transfers between devices, device_part(): told = lax.all_to_all(ask, 'z', 0, 0, tiled=True)  6.82 us
  transfers between devices with their start and end apart: 16, of which 7 were waited for; matrix products, arithmetic and copies ran while one was open for 10% of the time, Pallas kernels for 1%

profile of v6, /device:TPU:1, one launch (start us, length us, event | category | flops | bytes accessed | tf_op | source)
XLA Modules:
  0.0 197.3 jit_solution(12330359788749084224)
XLA Ops:
  0.0 12.1 %collective-permute-start.5 = (bf16[16,64,512]{2,1,0:T(8,128)(2,1)}, bf16[16,64,512]{2,1,0:T(8,128)(2,1)S(1)}, u32[]{:S(2)}, u32[]{:S(2)}) collective-permute-start(bf16[16,64,512]{2,1,0:T(8,128)(2,1)} %refs_0_.1), channel_id=1, source_target_pairs={{0,32},{16,496},{32,64},{48,16},{64,96},{80,48},{96,128},{112,80},... | collective-permute-start | bytes 3145736 | tf_op jit(solution)/shard_map/ppermute | solution.py:335
  14.0 10.1 %collective-permute-done.5.refs_4_ = bf16[16,64,512]{2,1,0:T(8,128)(2,1)S(1)} collective-permute-done((bf16[16,64,512]{2,1,0:T(8,128)(2,1)}, bf16[16,64,512]{2,1,0:T(8,128)(2,1)S(1)}, u32[]{:S(2)}, u32[]{:S(2)}) %collective-permute-start.5) | collective-permute-done | bytes 1048608 | tf_op jit(solution)/shard_map/ppermute | solution.py:335
  24.1 3.8 %collective-permute-start.7 = (bf16[16,64,512]{2,1,0:T(8,128)(2,1)S(1)}, bf16[16,64,512]{2,1,0:T(8,128)(2,1)}, u32[]{:S(2)}, u32[]{:S(2)}) collective-permute-start(bf16[16,64,512]{2,1,0:T(8,128)(2,1)S(1)} %collective-permute-done.5.refs_4_), channel_id=1, source_target_pairs={{0,16},{16,0},{1,17},{17,1},{2,18},{18,2},{3,19},{19,3},{4,20},{20... | collective-permute-start | bytes 3145736 | tf_op jit(solution)/shard_map/ppermute | solution.py:344
  27.9 3.6 %collective-permute-start.6 = (bf16[16,16,128]{2,1,0:T(8,128)(2,1)}, bf16[16,16,128]{2,1,0:T(8,128)(2,1)S(1)}, u32[]{:S(2)}, u32[]{:S(2)}) collective-permute-start(bf16[16,16,128]{2,1,0:T(8,128)(2,1)} %bitcast.41), channel_id=1, source_target_pairs={{0,32},{16,496},{32,64},{48,16},{64,96},{80,48},{96,128},{112,80},... | collective-permute-start | bytes 196616 | tf_op jit(solution)/shard_map/ppermute | solution.py:336
  34.2 7.2 %all-to-all-start.2 = ((s32[16,1,128]{2,1,0:T(1,128)}), s32[16,1,128]{2,1,0:T(1,128)S(1)}, u32[]{:S(2)}, u32[]{:S(2)}) async-start(s32[16,1,128]{2,1,0:T(1,128)} %get-tuple-element.43), calls=%async_computation.2 | async-start | bytes 16384 | tf_op jit(solution)/shard_map/all_to_all | solution.py:339
  41.4 2.5 %collective-permute-start.4 = (bf16[16,16,128]{2,1,0:T(8,128)(2,1)}, bf16[16,16,128]{2,1,0:T(8,128)(2,1)S(1)}, u32[]{:S(2)}, u32[]{:S(2)}) collective-permute-start(bf16[16,16,128]{2,1,0:T(8,128)(2,1)} %bitcast.42), channel_id=1, source_target_pairs={{0,16},{16,0},{1,17},{17,1},{2,18},{18,2},{3,19},{19,3},{4,20},{20... | collective-permute-start | bytes 196616 | tf_op jit(solution)/shard_map/ppermute | solution.py:342
  45.8 6.8 %all-to-all-done.2 = s32[16,1,128]{2,1,0:T(1,128)S(1)} async-done(((s32[16,1,128]{2,1,0:T(1,128)}), s32[16,1,128]{2,1,0:T(1,128)S(1)}, u32[]{:S(2)}, u32[]{:S(2)}) %all-to-all-start.2) | async-done | bytes 8224 | tf_op jit(solution)/shard_map/all_to_all | solution.py:339
  52.7 4.0 %shard_map.76 = bf16[32,272,128]{2,1,0:T(8,128)(2,1)} custom-call(s32[1]{0:T(128)} %bitcast.10.at_ref, s32[16,128]{1,0:T(8,128)S(1)} %clamp_bitcast_fusion.told_ref, bf16[16,64,512]{2,1,0:T(8,128)(2,1)} %refs_0_.1, bf16[16,16,128]{2,1,0:T(8,128)(2,1)} %bitcast.43, bf16[16,64,512]{2,1,0:T(8,128)(2,1)S(1)} %collective-permute-done.3.refs_2_, ...), custom_call_target="tpu_custom_call" | custom-call | tf_op jit(solution)/shard_map/pallas_call | solution.py:196
  56.7 6.1 %all-to-all-start.3 = ((bf16[16,2,272,128]{3,2,1,0:T(8,128)(2,1)}), bf16[16,2,272,128]{3,2,1,0:T(8,128)(2,1)S(1)}, u32[]{:S(2)}, u32[]{:S(2)}) async-start(bf16[16,2,272,128]{3,2,1,0:T(8,128)(2,1)} %bitcast.16), calls=%async_computation.3 | async-start | bytes 4456448 | tf_op jit(solution)/shard_map/all_to_all | solution.py:350
  62.9 3.7 %convolution_convert_fusion = bf16[512,3072]{0,1:T(8,128)(2,1)S(1)} fusion(bf16[3072,512]{1,0:T(8,128)(2,1)} %tok_ref.1, bf16[512,512]{1,0:T(8,128)(2,1)S(1)} %copy-done), kind=kOutput, calls=%fused_computation | convolution fusion | flops 1612185600 | bytes 6815744 | tf_op jit(solution)/shard_map/dot_general | solution.py:354
  68.9 4.8 %collective-permute-start.10 = (bf16[768,512]{1,0:T(8,128)(2,1)}, bf16[768,512]{1,0:T(8,128)(2,1)S(1)}, u32[]{:S(2)}, u32[]{:S(2)}) collective-permute-start(bf16[768,512]{1,0:T(8,128)(2,1)} %get-tuple-element.50), channel_id=1, source_target_pairs={{0,8},{4,12},{8,0},{12,4},{1,9},{5,13},{9,1},{13,5},{2,10},{6,14},... | collective-permute-start | bytes 2359304 | tf_op jit(solution)/shard_map/ppermute | solution.py:38
  73.8 2.7 %collective-permute-start.11 = (bf16[768,512]{1,0:T(8,128)(2,1)}, bf16[768,512]{1,0:T(8,128)(2,1)}, u32[]{:S(2)}, u32[]{:S(2)}) collective-permute-start(bf16[768,512]{1,0:T(8,128)(2,1)} %get-tuple-element.49), channel_id=1, source_target_pairs={{0,12},{4,0},{8,4},{12,8},{1,13},{5,1},{9,5},{13,9},{2,14},{6,2},{... | collective-permute-start | bytes 2359304 | tf_op jit(solution)/shard_map/ppermute | solution.py:38
  76.5 2.6 %collective-permute-start.9 = (bf16[768,512]{1,0:T(8,128)(2,1)}, bf16[768,512]{1,0:T(8,128)(2,1)}, u32[]{:S(2)}, u32[]{:S(2)}) collective-permute-start(bf16[768,512]{1,0:T(8,128)(2,1)} %get-tuple-element.48), channel_id=1, source_target_pairs={{0,4},{4,8},{8,12},{12,0},{1,5},{5,9},{9,13},{13,1},{2,6},{6,10},{... | collective-permute-start | bytes 2359304 | tf_op jit(solution)/shard_map/ppermute | solution.py:38
  83.3 7.9 %collective-permute-done.10 = bf16[768,512]{1,0:T(8,128)(2,1)S(1)} collective-permute-done((bf16[768,512]{1,0:T(8,128)(2,1)}, bf16[768,512]{1,0:T(8,128)(2,1)S(1)}, u32[]{:S(2)}, u32[]{:S(2)}) %collective-permute-start.10) | collective-permute-done | bytes 786464 | tf_op jit(solution)/shard_map/ppermute | solution.py:38
  91.3 17.3 %collective-permute-done.11 = bf16[768,512]{1,0:T(8,128)(2,1)} collective-permute-done((bf16[768,512]{1,0:T(8,128)(2,1)}, bf16[768,512]{1,0:T(8,128)(2,1)}, u32[]{:S(2)}, u32[]{:S(2)}) %collective-permute-start.11) | collective-permute-done | bytes 786464 | tf_op jit(solution)/shard_map/ppermute | solution.py:38
  109.0 2.9 %fusion.2 = bf16[768,512]{1,0:T(8,128)(2,1)} fusion(bf16[768,512]{1,0:T(8,128)(2,1)} %collective-permute-done.11, bf16[768,512]{1,0:T(8,128)(2,1)S(1)} %collective-permute-done.10, bf16[768,512]{1,0:T(8,128)(2,1)} %collective-permute-done.9, bf16[512,3072]{0,1:T(8,128)(2,1)} %copy-done.6, s32[]{:T(128)S(6)} %select_n.70), kind=kLoop, calls=%fused_computation.4 | loop fusion | flops 3145728 | bytes 3932164 | tf_op jit(solution)/shard_map/convert_element_type | solution.py:42
  111.9 48.5 %all-to-all-done.3 = bf16[16,2,272,128]{3,2,1,0:T(8,128)(2,1)S(1)} async-done(((bf16[16,2,272,128]{3,2,1,0:T(8,128)(2,1)}), bf16[16,2,272,128]{3,2,1,0:T(8,128)(2,1)S(1)}, u32[]{:S(2)}, u32[]{:S(2)}) %all-to-all-start.3) | async-done | bytes 2228256 | tf_op jit(solution)/shard_map/all_to_all | solution.py:350
  160.4 4.3 %shard_map.77 = bf16[16,128,128]{2,1,0:T(8,128)(2,1)} custom-call(s32[24]{0:T(128)} %broadcast_minimum_fusion.at_ref, bf16[3072,512]{1,0:T(8,128)(2,1)} %tok_ref.1, bf16[32,272,128]{2,1,0:T(8,128)(2,1)S(1)} %bitcast.39), custom_call_target="tpu_custom_call" | custom-call | tf_op jit(solution)/shard_map/pallas_call | solution.py:275
  164.8 6.9 %all-to-all-start.4 = ((bf16[16,128,128]{2,1,0:T(8,128)(2,1)}), bf16[16,128,128]{2,1,0:T(8,128)(2,1)S(1)}, u32[]{:S(2)}, u32[]{:S(2)}) async-start(bf16[16,128,128]{2,1,0:T(8,128)(2,1)} %shard_map.77), calls=%async_computation.4 | async-start | bytes 1048576 | tf_op jit(solution)/shard_map/all_to_all | solution.py:371
  171.7 2.1 %constant_dynamic-slice_fusion.2 = (bf16[192,512]{1,0:T(8,128)(2,1)}, bf16[192,512]{1,0:T(8,128)(2,1)S(1)}, bf16[192,512]{1,0:T(8,128)(2,1)}) fusion(bf16[768,512]{1,0:T(8,128)(2,1)} %fusion.2, s32[]{:T(128)S(6)} %select_n.80, s32[]{:T(128)S(6)} %select_n.84, s32[]{:T(128)S(6)} %select_n.82), kind=kLoop, calls=%fused_computation.17 | loop fusion | bytes 1179660 | tf_op jit(solution)/shard_map/dynamic_slice | solution.py:36
  173.8 3.3 %collective-permute-start.12 = (bf16[192,512]{1,0:T(8,128)(2,1)}, bf16[192,512]{1,0:T(8,128)(2,1)}, u32[]{:S(2)}, u32[]{:S(2)}) collective-permute-start(bf16[192,512]{1,0:T(8,128)(2,1)} %get-tuple-element.51), channel_id=1, source_target_pairs={{0,1},{1,2},{2,3},{3,0},{4,5},{5,6},{6,7},{7,4},{8,9},{9,10},{10,1... | collective-permute-start | bytes 589832 | tf_op jit(solution)/shard_map/ppermute | solution.py:38
  177.0 4.3 %collective-permute-start.13 = (bf16[192,512]{1,0:T(8,128)(2,1)}, bf16[192,512]{1,0:T(8,128)(2,1)}, u32[]{:S(2)}, u32[]{:S(2)}) collective-permute-start(bf16[192,512]{1,0:T(8,128)(2,1)} %get-tuple-element.53), channel_id=1, source_target_pairs={{0,2},{1,3},{2,0},{3,1},{4,6},{5,7},{6,4},{7,5},{8,10},{9,11},{10,... | collective-permute-start | bytes 589832 | tf_op jit(solution)/shard_map/ppermute | solution.py:38
  181.3 3.1 %collective-permute-start.14 = (bf16[192,512]{1,0:T(8,128)(2,1)S(1)}, bf16[192,512]{1,0:T(8,128)(2,1)}, u32[]{:S(2)}, u32[]{:S(2)}) collective-permute-start(bf16[192,512]{1,0:T(8,128)(2,1)S(1)} %get-tuple-element.52), channel_id=1, source_target_pairs={{0,3},{1,0},{2,1},{3,2},{4,7},{5,4},{6,5},{7,6},{8,11},{9,8},{10,9... | collective-permute-start | bytes 589832 | tf_op jit(solution)/shard_map/ppermute | solution.py:38
  186.5 4.6 %collective-permute-start.2 = (s32[8,128]{1,0:T(8,128)S(1)}, s32[8,128]{1,0:T(8,128)}, u32[]{:S(2)}, u32[]{:S(2)}) collective-permute-start(s32[8,128]{1,0:T(8,128)S(1)} %broadcast_in_dim.21), channel_id=1, source_target_pairs={{0,16},{16,0},{1,17},{17,1},{2,18},{18,2},{3,19},{19,3},{4,20},{20... | collective-permute-start | bytes 12296 | tf_op jit(solution)/shard_map/ppermute | solution.py:358
  (51 shorter events, 20.4 us)
Async XLA Ops:
  0.0 62.9 %copy-start = (bf16[512,512]{1,0:T(8,128)(2,1)S(1)}, bf16[512,512]{1,0:T(8,128)(2,1)}, u32[]{:S(2)}) copy-start(bf16[512,512]{1,0:T(8,128)(2,1)} %param.10) | copy-start | bytes 1572868
  0.0 24.1 %collective-permute-start.5 = (bf16[16,64,512]{2,1,0:T(8,128)(2,1)}, bf16[16,64,512]{2,1,0:T(8,128)(2,1)S(1)}, u32[]{:S(2)}, u32[]{:S(2)}) collective-permute-start(bf16[16,64,512]{2,1,0:T(8,128)(2,1)} %refs_0_.1), channel_id=1, source_target_pairs={{0,32},{16,496},{32,64},{48,16},{64,96},{80,48},{96,128},{112,80},... | collective-permute-start | bytes 3145736 | tf_op jit(solution)/shard_map/ppermute | solution.py:335
  12.1 40.6 %collective-permute-start.3 = (bf16[16,64,512]{2,1,0:T(8,128)(2,1)}, bf16[16,64,512]{2,1,0:T(8,128)(2,1)S(1)}, u32[]{:S(2)}, u32[]{:S(2)}) collective-permute-start(bf16[16,64,512]{2,1,0:T(8,128)(2,1)} %refs_0_.1), channel_id=1, source_target_pairs={{0,16},{16,0},{1,17},{17,1},{2,18},{18,2},{3,19},{19,3},{4,20},{20... | collective-permute-start | bytes 3145736 | tf_op jit(solution)/shard_map/ppermute | solution.py:341
  24.1 28.6 %collective-permute-start.7 = (bf16[16,64,512]{2,1,0:T(8,128)(2,1)S(1)}, bf16[16,64,512]{2,1,0:T(8,128)(2,1)}, u32[]{:S(2)}, u32[]{:S(2)}) collective-permute-start(bf16[16,64,512]{2,1,0:T(8,128)(2,1)S(1)} %collective-permute-done.5.refs_4_), channel_id=1, source_target_pairs={{0,16},{16,0},{1,17},{17,1},{2,18},{18,2},{3,19},{19,3},{4,20},{20... | collective-permute-start | bytes 3145736 | tf_op jit(solution)/shard_map/ppermute | solution.py:344
  27.9 16.0 %collective-permute-start.6 = (bf16[16,16,128]{2,1,0:T(8,128)(2,1)}, bf16[16,16,128]{2,1,0:T(8,128)(2,1)S(1)}, u32[]{:S(2)}, u32[]{:S(2)}) collective-permute-start(bf16[16,16,128]{2,1,0:T(8,128)(2,1)} %bitcast.41), channel_id=1, source_target_pairs={{0,32},{16,496},{32,64},{48,16},{64,96},{80,48},{96,128},{112,80},... | collective-permute-start | bytes 196616 | tf_op jit(solution)/shard_map/ppermute | solution.py:336
  34.2 18.5 %all-to-all-start.2 = ((s32[16,1,128]{2,1,0:T(1,128)}), s32[16,1,128]{2,1,0:T(1,128)S(1)}, u32[]{:S(2)}, u32[]{:S(2)}) async-start(s32[16,1,128]{2,1,0:T(1,128)} %get-tuple-element.43), calls=%async_computation.2 | async-start | bytes 16384 | tf_op jit(solution)/shard_map/all_to_all | solution.py:339
  41.4 11.3 %collective-permute-start.4 = (bf16[16,16,128]{2,1,0:T(8,128)(2,1)}, bf16[16,16,128]{2,1,0:T(8,128)(2,1)S(1)}, u32[]{:S(2)}, u32[]{:S(2)}) collective-permute-start(bf16[16,16,128]{2,1,0:T(8,128)(2,1)} %bitcast.42), channel_id=1, source_target_pairs={{0,16},{16,0},{1,17},{17,1},{2,18},{18,2},{3,19},{19,3},{4,20},{20... | collective-permute-start | bytes 196616 | tf_op jit(solution)/shard_map/ppermute | solution.py:342
  43.9 8.8 %collective-permute-start.8 = (bf16[16,16,128]{2,1,0:T(8,128)(2,1)S(1)}, bf16[16,16,128]{2,1,0:T(8,128)(2,1)S(1)}, u32[]{:S(2)}, u32[]{:S(2)}) collective-permute-start(bf16[16,16,128]{2,1,0:T(8,128)(2,1)S(1)} %collective-permute-done.6.refs_5_), channel_id=1, source_target_pairs={{0,16},{16,0},{1,17},{17,1},{2,18},{18,2},{3,19},{19,3},{4,20},{20... | collective-permute-start | bytes 196616 | tf_op jit(solution)/shard_map/ppermute | solution.py:343
  52.7 4.0 %copy-start.9 = (s32[16,128]{1,0:T(8,128)}, s32[16,128]{1,0:T(8,128)S(1)}, u32[]{:S(2)}) copy-start(s32[16,128]{1,0:T(8,128)S(1)} %clamp_bitcast_fusion.told_ref) | copy-start | bytes 24580
  56.7 103.7 %all-to-all-start.3 = ((bf16[16,2,272,128]{3,2,1,0:T(8,128)(2,1)}), bf16[16,2,272,128]{3,2,1,0:T(8,128)(2,1)S(1)}, u32[]{:S(2)}, u32[]{:S(2)}) async-start(bf16[16,2,272,128]{3,2,1,0:T(8,128)(2,1)} %bitcast.16), calls=%async_computation.3 | async-start | bytes 4456448 | tf_op jit(solution)/shard_map/all_to_all | solution.py:350
  66.6 2.4 %copy-start.6 = (bf16[512,3072]{0,1:T(8,128)(2,1)}, bf16[512,3072]{0,1:T(8,128)(2,1)S(1)}, u32[]{:S(2)}) copy-start(bf16[512,3072]{0,1:T(8,128)(2,1)S(1)} %convolution_convert_fusion) | copy-start | bytes 9437188
  68.9 22.3 %collective-permute-start.10 = (bf16[768,512]{1,0:T(8,128)(2,1)}, bf16[768,512]{1,0:T(8,128)(2,1)S(1)}, u32[]{:S(2)}, u32[]{:S(2)}) collective-permute-start(bf16[768,512]{1,0:T(8,128)(2,1)} %get-tuple-element.50), channel_id=1, source_target_pairs={{0,8},{4,12},{8,0},{12,4},{1,9},{5,13},{9,1},{13,5},{2,10},{6,14},... | collective-permute-start | bytes 2359304 | tf_op jit(solution)/shard_map/ppermute | solution.py:38
  73.8 34.8 %collective-permute-start.11 = (bf16[768,512]{1,0:T(8,128)(2,1)}, bf16[768,512]{1,0:T(8,128)(2,1)}, u32[]{:S(2)}, u32[]{:S(2)}) collective-permute-start(bf16[768,512]{1,0:T(8,128)(2,1)} %get-tuple-element.49), channel_id=1, source_target_pairs={{0,12},{4,0},{8,4},{12,8},{1,13},{5,1},{9,5},{13,9},{2,14},{6,2},{... | collective-permute-start | bytes 2359304 | tf_op jit(solution)/shard_map/ppermute | solution.py:38
  76.5 32.5 %collective-permute-start.9 = (bf16[768,512]{1,0:T(8,128)(2,1)}, bf16[768,512]{1,0:T(8,128)(2,1)}, u32[]{:S(2)}, u32[]{:S(2)}) collective-permute-start(bf16[768,512]{1,0:T(8,128)(2,1)} %get-tuple-element.48), channel_id=1, source_target_pairs={{0,4},{4,8},{8,12},{12,0},{1,5},{5,9},{9,13},{13,1},{2,6},{6,10},{... | collective-permute-start | bytes 2359304 | tf_op jit(solution)/shard_map/ppermute | solution.py:38
  82.7 82.1 %copy-start.11 = (s32[24]{0:T(128)}, s32[24]{0:T(128)S(1)}, u32[]{:S(2)}) copy-start(s32[24]{0:T(128)S(1)} %convert_reduce_fusion) | copy-start | bytes 292
  160.4 4.3 %copy-start.4 = (bf16[16,2,272,128]{3,2,1,0:T(8,128)(2,1)}, bf16[16,2,272,128]{3,2,1,0:T(8,128)(2,1)S(1)}, u32[]{:S(2)}) copy-start(bf16[16,2,272,128]{3,2,1,0:T(8,128)(2,1)S(1)} %all-to-all-done.3) | copy-start | bytes 6684676
  164.8 31.2 %copy-start.7 = (bf16[16,4,512]{2,1,0:T(4,128)(2,1)S(1)}, bf16[16,4,512]{2,1,0:T(4,128)(2,1)}, u32[]{:S(2)}) copy-start(bf16[16,4,512]{2,1,0:T(4,128)(2,1)} %param.12) | copy-start | bytes 196612
  164.8 31.1 %all-to-all-start.4 = ((bf16[16,128,128]{2,1,0:T(8,128)(2,1)}), bf16[16,128,128]{2,1,0:T(8,128)(2,1)S(1)}, u32[]{:S(2)}, u32[]{:S(2)}) async-start(bf16[16,128,128]{2,1,0:T(8,128)(2,1)} %shard_map.77), calls=%async_computation.4 | async-start | bytes 1048576 | tf_op jit(solution)/shard_map/all_to_all | solution.py:371
  171.7 24.2 %copy-start.5 = (bf16[16,2,272,128]{3,2,1,0:T(8,128)(2,1)S(1)}, bf16[16,2,272,128]{3,2,1,0:T(8,128)(2,1)}, u32[]{:S(2)}) copy-start(bf16[16,2,272,128]{3,2,1,0:T(8,128)(2,1)} %copy-done.4) | copy-start | bytes 6684676
  171.7 24.2 %copy-start.10 = (s32[16,128]{1,0:T(8,128)S(1)}, s32[16,128]{1,0:T(8,128)}, u32[]{:S(2)}) copy-start(s32[16,128]{1,0:T(8,128)} %copy-done.9) | copy-start | bytes 24580
  173.8 20.8 %collective-permute-start.12 = (bf16[192,512]{1,0:T(8,128)(2,1)}, bf16[192,512]{1,0:T(8,128)(2,1)}, u32[]{:S(2)}, u32[]{:S(2)}) collective-permute-start(bf16[192,512]{1,0:T(8,128)(2,1)} %get-tuple-element.51), channel_id=1, source_target_pairs={{0,1},{1,2},{2,3},{3,0},{4,5},{5,6},{6,7},{7,4},{8,9},{9,10},{10,1... | collective-permute-start | bytes 589832 | tf_op jit(solution)/shard_map/ppermute | solution.py:38
  177.0 17.5 %collective-permute-start.13 = (bf16[192,512]{1,0:T(8,128)(2,1)}, bf16[192,512]{1,0:T(8,128)(2,1)}, u32[]{:S(2)}, u32[]{:S(2)}) collective-permute-start(bf16[192,512]{1,0:T(8,128)(2,1)} %get-tuple-element.53), channel_id=1, source_target_pairs={{0,2},{1,3},{2,0},{3,1},{4,6},{5,7},{6,4},{7,5},{8,10},{9,11},{10,... | collective-permute-start | bytes 589832 | tf_op jit(solution)/shard_map/ppermute | solution.py:38
  181.3 13.2 %collective-permute-start.14 = (bf16[192,512]{1,0:T(8,128)(2,1)S(1)}, bf16[192,512]{1,0:T(8,128)(2,1)}, u32[]{:S(2)}, u32[]{:S(2)}) collective-permute-start(bf16[192,512]{1,0:T(8,128)(2,1)S(1)} %get-tuple-element.52), channel_id=1, source_target_pairs={{0,3},{1,0},{2,1},{3,2},{4,7},{5,4},{6,5},{7,6},{8,11},{9,8},{10,9... | collective-permute-start | bytes 589832 | tf_op jit(solution)/shard_map/ppermute | solution.py:38
  186.5 5.6 %collective-permute-start.2 = (s32[8,128]{1,0:T(8,128)S(1)}, s32[8,128]{1,0:T(8,128)}, u32[]{:S(2)}, u32[]{:S(2)}) collective-permute-start(s32[8,128]{1,0:T(8,128)S(1)} %broadcast_in_dim.21), channel_id=1, source_target_pairs={{0,16},{16,0},{1,17},{17,1},{2,18},{18,2},{3,19},{19,3},{4,20},{20... | collective-permute-start | bytes 12296 | tf_op jit(solution)/shard_map/ppermute | solution.py:358
  (3 other events, 2.0 us)
